TPU v7x, 32 devices: a whole 2x2x4 slice. The times are simulated.
32 devices in a mesh: fsdp: 8 (over z, y), tp: 4 (over x, core).
Axes of the slice: x: 2, y: 2, z: 4, core: 2. Of those that a mesh axis runs over, the one named last changes fastest.
Arguments:
- tokens: bfloat16 [2048, 2048], P('fsdp'), may hold values from -6 to 6
- cotangent: bfloat16 [2048, 2048], P('fsdp'), may hold values from -6 to 6
- caption_lengths: int32 [16], P('fsdp'), may hold values from 1 to 64, 768 in all
- w_qkv: bfloat16 [2048, 3, 2048], P('fsdp', None, 'tp'), as said below
- head_biases: bfloat16 [4, 2048], P(None, ('tp', 'fsdp')), may hold values from -3 to 3
- head_gain: bfloat16 [2048], P(('tp', 'fsdp')), may hold values from 0.5 to 1.5
- w_out: bfloat16 [2048, 2048], P('tp', 'fsdp'), may hold values from -0.125 to 0.125
- model_gains: bfloat16 [2, 2048], P(None, 'fsdp'), may hold values from 0.5 to 1.5
- model_biases: bfloat16 [4, 2048], P(None, 'fsdp'), may hold values from -3 to 3
- w_fc1: bfloat16 [2048, 8192], P('fsdp', 'tp'), as said below
- w_fc2: bfloat16 [8192, 2048], P('tp', 'fsdp'), may hold values from -0.0625 to 0.0625
- ffn_gain: bfloat16 [8192], P(('tp', 'fsdp')), may hold values from 0.5 to 1.5
- ffn_biases: bfloat16 [2, 8192], P(None, ('tp', 'fsdp')), may hold values from -3 to 3
Outputs:
- layer_out: bfloat16 [2048, 2048], P('fsdp')
- grad_tokens: float32 [2048, 2048], P('fsdp')
- grad_w_qkv: float32 [2048, 3, 2048], P('fsdp', None, 'tp')
- grad_head_biases: float32 [4, 2048], P(None, ('tp', 'fsdp'))
- grad_head_gain: float32 [2048], P(('tp', 'fsdp'))
- grad_w_out: float32 [2048, 2048], P('tp', 'fsdp')
- grad_model_gains: float32 [2, 2048], P(None, 'fsdp')
- grad_model_biases: float32 [4, 2048], P(None, 'fsdp')
- grad_w_fc1: float32 [2048, 8192], P('fsdp', 'tp')
- grad_w_fc2: float32 [8192, 2048], P('tp', 'fsdp')
- grad_ffn_gain: float32 [8192], P(('tp', 'fsdp'))
- grad_ffn_biases: float32 [2, 8192], P(None, ('tp', 'fsdp'))
Inputs may be any that keep to these rules, and one draw needn't show every extreme that they name: Pair p holds 64 image tokens, then caption_lengths[p] caption tokens; its other slots are padding. `w_qkv`: A projection matrix. `w_fc1`: A projection matrix.
All inputs are finite; a program needn't handle non-finite values. No bound on the sum of `caption_lengths` on one device may be relied on, other than what follows from the above.
Results may differ from a plain program's by a relative error of at most 0.014.
Values may be sent and summed in bfloat16 or wider, within the bound.
No kernel may reach another device: no remote copies, remote signals or barrier semaphores. Data moves between devices by JAX's collectives and lax.ppermute only.
A program may use at most 192 MiB of HBM per device.

v0:
```python
import math

import jax
import jax.numpy as jnp
from jax import lax
from jax.sharding import PartitionSpec as P

HEADS = 32
FF = 8192
IMAGE = 64


norm_eps = 1e-05


def rotation_tables(count, row_width):
    position = jnp.arange(count).astype(jnp.float32)[:, None]
    channel = jnp.arange(row_width // 2).astype(jnp.float32)[None, :]
    frequency = jnp.exp(-(2.0 * channel / row_width) * jnp.log(10000.0))
    angle = position * frequency
    zeta_base = (2.0 * channel + 0.4 * row_width) / (1.4 * row_width)
    growth = jnp.exp((position - count // 2) / 512.0 * jnp.log(zeta_base))
    return (jnp.cos(angle), jnp.sin(angle), growth)


def turn(values, cosine, sine_table, factor):
    paired = values.reshape(values.shape[:-1] + (values.shape[-1] // 2, 2))
    even_part = paired[..., 0]
    odd_part = paired[..., 1]
    cosine = cosine[:, None, :]
    sine_table = sine_table[:, None, :]
    factor = factor[:, None, :]
    new_even = (even_part * cosine - odd_part * sine_table) * factor
    new_odd = (odd_part * cosine + even_part * sine_table) * factor
    return jnp.stack([new_even, new_odd], axis=-1).reshape(values.shape)


def turn_back(values, cosine, sine_table, factor):
    paired = values.reshape(values.shape[:-1] + (values.shape[-1] // 2, 2))
    even_part = paired[..., 0] * factor[:, None, :]
    odd_part = paired[..., 1] * factor[:, None, :]
    cosine = cosine[:, None, :]
    sine_table = sine_table[:, None, :]
    new_even = even_part * cosine + odd_part * sine_table
    new_odd = odd_part * cosine - even_part * sine_table
    return jnp.stack([new_even, new_odd], axis=-1).reshape(values.shape)


def row_sums(values):
    return (
        jnp.sum(values, axis=-1, keepdims=True),
        jnp.sum(values * values, axis=-1, keepdims=True),
    )


def norm_apply(values, first_sum, square_sum, row_width, gain_vector, shift_vector):
    mean_value = first_sum / row_width
    variance = square_sum / row_width - mean_value * mean_value
    inverse = lax.rsqrt(variance + norm_eps)
    normed = (values - mean_value) * inverse
    return (normed * gain_vector + shift_vector, normed, inverse)


def norm_finish(scaled, normed, inverse, first_sum, second_sum, row_width):
    return inverse * (scaled - first_sum / row_width - normed * second_sum / row_width)


def exact_gelu(values):
    return jax.nn.gelu(values, approximate=False)


def stats_total(pieces):
    return lax.psum((pieces[0], pieces[1]), "tp")


def width_total(product):
    return lax.psum(product, "tp")


def per_device(
    tokens,
    cotangent,
    caption_lengths,
    w_qkv,
    head_biases,
    head_gain,
    w_out,
    model_gains,
    model_biases,
    w_fc1,
    w_fc2,
    ffn_gain,
    ffn_biases,
):
    pair_count = caption_lengths.shape[0]
    row_count = tokens.shape[0]
    slot_count = row_count // pair_count
    model_width = tokens.shape[1]
    head_dim = model_width // HEADS
    hidden_width = FF
    cosine, sine_table, growth = rotation_tables(slot_count, head_dim)
    slot_index = jnp.arange(slot_count)[None, :]
    key_valid = slot_index < IMAGE + caption_lengths[:, None]
    keep_rows = key_valid.reshape(row_count).astype(jnp.float32)[:, None]
    causal = jnp.arange(slot_count)[:, None] >= jnp.arange(slot_count)[None, :]
    allowed = causal[None, None] & key_valid[:, None, None, :]
    scale_value = 1.0 / math.sqrt(head_dim)
    qkv_full, out_full, head_vectors, head_scale, model_scale, model_shift = (
        lax.all_gather(w_qkv, "fsdp", axis=0, tiled=True),
        lax.all_gather(w_out, "fsdp", axis=1, tiled=True),
        lax.all_gather(head_biases, "fsdp", axis=1, tiled=True),
        lax.all_gather(head_gain, "fsdp", axis=0, tiled=True),
        lax.all_gather(model_gains, "fsdp", axis=1, tiled=True),
        lax.all_gather(model_biases, "fsdp", axis=1, tiled=True),
    )
    fc1_full, fc2_full, unit_scale, unit_vectors = (
        lax.all_gather(w_fc1, "fsdp", axis=0, tiled=True),
        lax.all_gather(w_fc2, "fsdp", axis=1, tiled=True),
        lax.all_gather(ffn_gain, "fsdp", axis=0, tiled=True),
        lax.all_gather(ffn_biases, "fsdp", axis=1, tiled=True),
    )
    local_heads = qkv_full.shape[2] // head_dim
    head_shift = head_vectors.astype(jnp.float32)
    model_offset = model_shift.astype(jnp.float32)
    unit_shift = unit_vectors.astype(jnp.float32)
    tokens_f = tokens.astype(jnp.float32)
    first_sum, square_sum = row_sums(tokens_f)
    normed_in, hat_in, inverse_in = norm_apply(
        tokens_f,
        first_sum,
        square_sum,
        model_width,
        model_scale[0].astype(jnp.float32),
        model_offset[0],
    )
    normed_in_b = normed_in.astype(jnp.bfloat16)
    linear = (
        jnp.einsum("td,dce->tce", normed_in_b, qkv_full, preferred_element_type=jnp.float32)
        + head_shift[:3][None]
    )
    shaped = linear.reshape(pair_count, slot_count, 3, local_heads, head_dim)
    queries = turn(shaped[:, :, 0], cosine, sine_table, growth).astype(jnp.bfloat16)
    keys_rot = turn(shaped[:, :, 1], cosine, sine_table, 1.0 / growth).astype(jnp.bfloat16)
    values_in = shaped[:, :, 2].astype(jnp.bfloat16)
    raw_scores = jnp.einsum(
        "gqhe,gkhe->ghqk", queries, keys_rot, preferred_element_type=jnp.float32
    )
    scores = jnp.where(allowed, raw_scores * scale_value, -1e30)
    top_score = jnp.max(scores, axis=-1, keepdims=True)
    log_total = top_score + jnp.log(jnp.sum(jnp.exp(scores - top_score), axis=-1, keepdims=True))
    probs_b = jnp.exp(scores - log_total).astype(jnp.bfloat16)
    heads_out = jnp.einsum(
        "ghqk,gkhe->gqhe", probs_b, values_in, preferred_element_type=jnp.float32
    ).reshape(row_count, local_heads * head_dim)
    head_stats = stats_total(row_sums(heads_out))
    post_attn, hat_attn, inverse_attn = norm_apply(
        heads_out,
        head_stats[0],
        head_stats[1],
        model_width,
        head_scale.astype(jnp.float32),
        head_shift[3],
    )
    post_attn_b = post_attn.astype(jnp.bfloat16)
    attn_product = jnp.dot(post_attn_b, out_full, preferred_element_type=jnp.float32)
    middle = tokens_f + width_total(attn_product) + model_offset[2]
    mid_first, mid_square = row_sums(middle)
    normed_mid, hat_mid, inverse_mid = norm_apply(
        middle,
        mid_first,
        mid_square,
        model_width,
        model_scale[1].astype(jnp.float32),
        model_offset[1],
    )
    normed_mid_b = normed_mid.astype(jnp.bfloat16)
    before = jnp.dot(normed_mid_b, fc1_full, preferred_element_type=jnp.float32) + unit_shift[0]
    active, gelu_back = jax.vjp(exact_gelu, before)
    unit_stats = stats_total(row_sums(active))
    post_ffn, hat_ffn, inverse_ffn = norm_apply(
        active,
        unit_stats[0],
        unit_stats[1],
        hidden_width,
        unit_scale.astype(jnp.float32),
        unit_shift[1],
    )
    post_ffn_b = post_ffn.astype(jnp.bfloat16)
    ffn_product = jnp.dot(post_ffn_b, fc2_full, preferred_element_type=jnp.float32)
    layer_out = ((middle + width_total(ffn_product) + model_offset[3]) * keep_rows).astype(
        jnp.bfloat16
    )
    qkv_back, out_back, head_scale_back, model_scale_back, fc1_back, fc2_back, unit_scale_back = (
        lax.all_gather(w_qkv, "fsdp", axis=0, tiled=True),
        lax.all_gather(w_out, "fsdp", axis=1, tiled=True),
        lax.all_gather(head_gain, "fsdp", axis=0, tiled=True),
        lax.all_gather(model_gains, "fsdp", axis=1, tiled=True),
        lax.all_gather(w_fc1, "fsdp", axis=0, tiled=True),
        lax.all_gather(w_fc2, "fsdp", axis=1, tiled=True),
        lax.all_gather(ffn_gain, "fsdp", axis=0, tiled=True),
    )
    grad_out = cotangent.astype(jnp.float32) * keep_rows
    grad_out_b = grad_out.astype(jnp.bfloat16)
    grad_fc2 = jnp.einsum("tf,td->fd", post_ffn_b, grad_out_b, preferred_element_type=jnp.float32)
    grad_post_ffn = jnp.einsum(
        "td,fd->tf", grad_out_b, fc2_back, preferred_element_type=jnp.float32
    )
    scaled_ffn = grad_post_ffn * unit_scale_back.astype(jnp.float32)
    unit_back = stats_total(
        (
            jnp.sum(scaled_ffn, axis=-1, keepdims=True),
            jnp.sum(scaled_ffn * hat_ffn, axis=-1, keepdims=True),
        )
    )
    grad_active = norm_finish(
        scaled_ffn, hat_ffn, inverse_ffn, unit_back[0], unit_back[1], hidden_width
    )
    grad_before_b = gelu_back(grad_active)[0].astype(jnp.bfloat16)
    grad_fc1 = jnp.einsum(
        "td,tf->df", normed_mid_b, grad_before_b, preferred_element_type=jnp.float32
    )
    mid_product = jnp.einsum(
        "tf,df->td", grad_before_b, fc1_back, preferred_element_type=jnp.float32
    )
    ffn_bias_grads = jnp.stack(
        [jnp.sum(grad_before_b.astype(jnp.float32), axis=0), jnp.sum(grad_post_ffn, axis=0)]
    )
    grad_fc1_s, grad_fc2_s, grad_unit_gain, grad_unit_biases = (
        lax.psum_scatter(
            grad_fc1.astype(jnp.bfloat16), "fsdp", scatter_dimension=0, tiled=True
        ).astype(jnp.float32),
        lax.psum_scatter(
            grad_fc2.astype(jnp.bfloat16), "fsdp", scatter_dimension=1, tiled=True
        ).astype(jnp.float32),
        lax.psum_scatter(
            jnp.sum(grad_post_ffn * hat_ffn, axis=0).astype(jnp.bfloat16),
            "fsdp",
            scatter_dimension=0,
            tiled=True,
        ).astype(jnp.float32),
        lax.psum_scatter(
            ffn_bias_grads.astype(jnp.bfloat16), "fsdp", scatter_dimension=1, tiled=True
        ).astype(jnp.float32),
    )
    mid_scale = model_scale_back[1].astype(jnp.float32)
    grad_mid_normed = width_total(mid_product)
    scaled_mid = grad_mid_normed * mid_scale
    grad_middle = grad_out + norm_finish(
        scaled_mid,
        hat_mid,
        inverse_mid,
        jnp.sum(scaled_mid, axis=-1, keepdims=True),
        jnp.sum(scaled_mid * hat_mid, axis=-1, keepdims=True),
        model_width,
    )
    mid_vectors = jnp.stack(
        [jnp.sum(grad_mid_normed * hat_mid, axis=0), jnp.sum(grad_mid_normed, axis=0)]
    )
    grad_middle_b = grad_middle.astype(jnp.bfloat16)
    grad_out_proj = jnp.einsum(
        "te,td->ed", post_attn_b, grad_middle_b, preferred_element_type=jnp.float32
    )
    grad_post_attn = jnp.einsum(
        "td,ed->te", grad_middle_b, out_back, preferred_element_type=jnp.float32
    )
    scaled_attn = grad_post_attn * head_scale_back.astype(jnp.float32)
    head_back = stats_total(
        (
            jnp.sum(scaled_attn, axis=-1, keepdims=True),
            jnp.sum(scaled_attn * hat_attn, axis=-1, keepdims=True),
        )
    )
    grad_heads_b = (
        norm_finish(scaled_attn, hat_attn, inverse_attn, head_back[0], head_back[1], model_width)
        .astype(jnp.bfloat16)
        .reshape(pair_count, slot_count, local_heads, head_dim)
    )
    raw_again = jnp.einsum("gqhe,gkhe->ghqk", queries, keys_rot, preferred_element_type=jnp.float32)
    probs_again = jnp.exp(jnp.where(allowed, raw_again * scale_value, -1e30) - log_total)
    grad_probs = jnp.einsum(
        "gqhe,gkhe->ghqk", grad_heads_b, values_in, preferred_element_type=jnp.float32
    )
    grad_values = jnp.einsum(
        "ghqk,gqhe->gkhe",
        probs_again.astype(jnp.bfloat16),
        grad_heads_b,
        preferred_element_type=jnp.float32,
    )
    grad_scores = probs_again * (
        grad_probs - jnp.sum(probs_again * grad_probs, axis=-1, keepdims=True)
    )
    grad_scores_b = (grad_scores * scale_value).astype(jnp.bfloat16)
    grad_queries = jnp.einsum(
        "ghqk,gkhe->gqhe", grad_scores_b, keys_rot, preferred_element_type=jnp.float32
    )
    grad_keys = jnp.einsum(
        "ghqk,gqhe->gkhe", grad_scores_b, queries, preferred_element_type=jnp.float32
    )
    grad_linear = jnp.stack(
        [
            turn_back(grad_queries, cosine, sine_table, growth),
            turn_back(grad_keys, cosine, sine_table, 1.0 / growth),
            grad_values,
        ],
        axis=2,
    )
    grad_linear_b = grad_linear.reshape(row_count, 3, local_heads * head_dim).astype(jnp.bfloat16)
    grad_qkv = jnp.einsum(
        "td,tce->dce", normed_in_b, grad_linear_b, preferred_element_type=jnp.float32
    )
    grad_in_normed = width_total(
        jnp.einsum("tce,dce->td", grad_linear_b, qkv_back, preferred_element_type=jnp.float32)
    )
    scaled_in = grad_in_normed * model_scale_back[0].astype(jnp.float32)
    grad_tokens = grad_middle + norm_finish(
        scaled_in,
        hat_in,
        inverse_in,
        jnp.sum(scaled_in, axis=-1, keepdims=True),
        jnp.sum(scaled_in * hat_in, axis=-1, keepdims=True),
        model_width,
    )
    head_bias_grads = jnp.concatenate(
        [jnp.sum(grad_linear_b.astype(jnp.float32), axis=0), jnp.sum(grad_post_attn, axis=0)[None]],
        axis=0,
    )
    model_gain_grads = jnp.stack([jnp.sum(grad_in_normed * hat_in, axis=0), mid_vectors[0]])
    model_bias_grads = jnp.stack(
        [
            jnp.sum(grad_in_normed, axis=0),
            mid_vectors[1],
            jnp.sum(grad_middle, axis=0),
            jnp.sum(grad_out, axis=0),
        ]
    )
    (
        grad_qkv_s,
        grad_out_s,
        grad_head_bias_s,
        grad_head_gain_s,
        grad_model_gain_s,
        grad_model_bias_s,
    ) = (
        lax.psum_scatter(grad_qkv, "fsdp", scatter_dimension=0, tiled=True),
        lax.psum_scatter(grad_out_proj, "fsdp", scatter_dimension=1, tiled=True),
        lax.psum_scatter(head_bias_grads, "fsdp", scatter_dimension=1, tiled=True),
        lax.psum_scatter(
            jnp.sum(grad_post_attn * hat_attn, axis=0), "fsdp", scatter_dimension=0, tiled=True
        ),
        lax.psum_scatter(model_gain_grads, "fsdp", scatter_dimension=1, tiled=True),
        lax.psum_scatter(model_bias_grads, "fsdp", scatter_dimension=1, tiled=True),
    )
    return (
        layer_out,
        grad_tokens,
        grad_qkv_s,
        grad_head_bias_s,
        grad_head_gain_s,
        grad_out_s,
        grad_model_gain_s,
        grad_model_bias_s,
        grad_fc1_s,
        grad_fc2_s,
        grad_unit_gain,
        grad_unit_biases,
    )


def solution(mesh):
    placed = (
        P("fsdp", None),
        P("fsdp", None),
        P("fsdp"),
        P("fsdp", None, "tp"),
        P(None, ("tp", "fsdp")),
        P(("tp", "fsdp")),
        P("tp", "fsdp"),
        P(None, "fsdp"),
        P(None, "fsdp"),
        P("fsdp", "tp"),
        P("tp", "fsdp"),
        P(("tp", "fsdp")),
        P(None, ("tp", "fsdp")),
    )
    return jax.shard_map(
        per_device,
        mesh=mesh,
        in_specs=placed,
        out_specs=(
            P("fsdp", None),
            P("fsdp", None),
            P("fsdp", None, "tp"),
            P(None, ("tp", "fsdp")),
            P(("tp", "fsdp")),
            P("tp", "fsdp"),
            P(None, "fsdp"),
            P(None, "fsdp"),
            P("fsdp", "tp"),
            P("tp", "fsdp"),
            P(("tp", "fsdp")),
            P(None, ("tp", "fsdp")),
        ),
        check_vma=False,
    )
```

profile of v0, /device:TPU:0, one launch (start us, length us, event | category | flops | bytes accessed | tf_op | source)
XLA Modules:
  0.0 1563.4 jit_solution(18410686721082106536)
XLA Ops:
  8.8 28.3 %all_gather.38 = bf16[4,2048]{1,0:T(4,128)(2,1)S(1)} all-gather(bf16[4,256]{1,0:T(4,128)(2,1)} %param.21), channel_id=1, replica_groups=mesh['fsdp'=8,'tp'=4] {'fsdp'}, dimensions={1}, use_global_device_ids=true | all-gather | bytes 18432 | tf_op jit(solution)/shard_map/all_gather | solution.py:114
  37.1 19.3 %all-gather = bf16[8,64,4]{1,2,0:T(4,128)(2,1)S(1)} all-gather(bf16[1,64,4]{1,2,0:T(4,128)(2,1)} %bitcast.170), channel_id=1, replica_groups=mesh['fsdp'=8,'tp'=4] {'fsdp'}, dimensions={0}, use_global_device_ids=true | all-gather | bytes 4608 | tf_op jit(solution)/shard_map/all_gather | solution.py:111
  56.5 17.0 %all_gather.37 = bf16[2,2048]{1,0:T(2,128)(2,1)S(1)} all-gather(bf16[2,256]{1,0:T(2,128)(2,1)} %param.20), channel_id=1, replica_groups=mesh['fsdp'=8,'tp'=4] {'fsdp'}, dimensions={1}, use_global_device_ids=true | all-gather | bytes 9216 | tf_op jit(solution)/shard_map/all_gather | solution.py:113
  76.9 19.5 %all-reduce = bf16[512]{0:T(512)(128)(2,1)S(1)} all-reduce(bf16[512]{0:T(512)(128)(2,1)S(1)} %dynamic-update-slice), channel_id=1, replica_groups=mesh['fsdp'=8,'tp'=4] {'fsdp'}, use_global_device_ids=true, to_apply=%add | all-reduce | flops 512 | bytes 2048
  97.5 15.4 all-gather.7.cloned.1.call-done
  112.9 5.8 convolution_add_fusion.1
  130.4 5.8 all-reduce.6
  136.2 28.0 %all-gather.9.cloned.1.call-done = bf16[512,2048]{1,0:T(8,128)(2,1)} async-done(((bf16[512,256]{1,0:T(8,128)(2,1)}), bf16[512,2048]{1,0:T(8,128)(2,1)}) %all-gather.9.cloned.1.call-update) | async-done | bytes 2097168 | tf_op jit(solution)/shard_map/all_gather | solution.py:110
  164.3 3.7 fusion.64
  169.2 17.7 %all-gather.1 = bf16[8,1,256]{2,1,0:T(2,128)(2,1)S(1)} all-gather(bf16[1,1,256]{2,1,0:T(2,128)(2,1)S(1)} %reshape.322), channel_id=1, replica_groups=mesh['fsdp'=8,'tp'=4] {'fsdp'}, dimensions={0}, use_global_device_ids=true | all-gather | bytes 4608 | tf_op jit(solution)/shard_map/all_gather | solution.py:119
  186.9 17.0 %all_gather.44 = bf16[2,2048]{1,0:T(2,128)(2,1)S(1)} all-gather(bf16[2,256]{1,0:T(2,128)(2,1)S(1)} %copy-done.60), channel_id=1, replica_groups=mesh['fsdp'=8,'tp'=4] {'fsdp'}, dimensions={1}, use_global_device_ids=true | all-gather | bytes 9216 | tf_op jit(solution)/shard_map/all_gather | solution.py:120
  204.0 13.7 all-reduce.12.cloned.1.call-done
  219.8 125.1 %all-gather.11.cloned.1.call-done = bf16[2048,2048]{1,0:T(8,128)(2,1)} async-done(((bf16[256,2048]{1,0:T(8,128)(2,1)}), bf16[2048,2048]{1,0:T(8,128)(2,1)}) %all-gather.11.cloned.1.call-update) | async-done | bytes 8388624 | tf_op jit(solution)/shard_map/all_gather | solution.py:117
  344.9 11.0 fusion.66
  356.0 6.5 all-reduce.5
  362.5 108.1 %all-gather.13.cloned.1.call-done = bf16[2048,2048]{1,0:T(8,128)(2,1)} async-done(((bf16[2048,256]{1,0:T(8,128)(2,1)}), bf16[2048,2048]{1,0:T(8,128)(2,1)}) %all-gather.13.cloned.1.call-update) | async-done | bytes 8388624 | tf_op jit(solution)/shard_map/all_gather | solution.py:118
  470.6 9.1 multiply_reduce_fusion
  479.7 6.1 all-reduce.4
  485.8 5.0 fusion.69
  491.9 3.7 fusion.80
  495.9 8.1 fusion.65
  504.0 41.1 %all-reduce.14.cloned.1.call-done = f32[256,2048]{1,0:T(8,128)} async-done(((f32[256,2048]{1,0:T(8,128)}), f32[256,2048]{1,0:T(8,128)}) %all-reduce.14.cloned.1.call-update) | async-done | bytes 2097168 | tf_op jit(solution)/shard_map/psum | solution.py:77
  545.2 3.2 multiply_reduce_fusion.1
  552.5 5.7 all-reduce.3
  562.1 2.4 fusion.29
  564.6 2.3 fusion.57
  566.8 4.2 fusion.32
  571.1 4.3 fusion.31
  593.6 6.1 convolution_bitcast_fusion
  603.7 82.6 %all-reduce.16.cloned.1.call-done = (f32[256,2048]{1,0:T(8,128)}, f32[256,2048]{1,0:T(8,128)}) async-done(((f32[256,2048]{1,0:T(8,128)}, f32[256,2048]{1,0:T(8,128)}), (f32[256,2048]{1,0:T(8,128)}, f32[256,2048]{1,0:T(8,128)})) %all-reduce.16.cloned.1.call-update) | async-done | bytes 4194320 | tf_op jit(solution)/shard_map/psum | solution.py:77
  686.4 2.6 fusion.14
  692.2 7.0 convolution_convert_fusion.1
  699.9 7.8 convolution_convert_fusion
  708.4 4.6 fusion.38
  713.7 7.6 fusion.51
  722.6 21.4 %all-reduce.2 = bf16[2048]{0:T(1024)(128)(2,1)S(1)} all-reduce(bf16[2048]{0:T(1024)(128)(2,1)S(1)} %copy-done.58), channel_id=10, replica_groups=mesh['fsdp'=8,'tp'=4] {'fsdp'}, use_global_device_ids=true, to_apply=%region_49.50.clone | all-reduce | flops 2048 | bytes 8192
  744.7 8.0 reduce-scatter.31.cloned.1.call-done
  754.2 19.4 %all-reduce.1 = f32[512]{0:T(512)S(1)} all-reduce(f32[512]{0:T(512)S(1)} %copy-done.56), channel_id=4, replica_groups=mesh['fsdp'=8,'tp'=4] {'fsdp'}, use_global_device_ids=true, to_apply=%region_36.37.clone | all-reduce | flops 512 | bytes 4096
  774.2 42.1 %reduce-scatter.25.cloned.1.call-done = f32[64,4]{1,0:T(8,128)} async-done(((f32[512,4]{1,0:T(8,128)}), f32[64,4]{1,0:T(8,128)}) %reduce-scatter.25.cloned.1.call-update) | async-done | bytes 1040
  817.7 3.0 multiply_convert_fusion
  822.9 59.6 %reduce-scatter.27.cloned.1.call-done = f32[256,2]{1,0:T(8,128)} async-done(((f32[2048,2]{1,0:T(8,128)}), f32[256,2]{1,0:T(8,128)}) %reduce-scatter.27.cloned.1.call-update) | async-done | bytes 2064
  884.0 64.7 %reduce-scatter.29.cloned.1.call-done = f32[256,4]{1,0:T(8,128)} async-done(((f32[2048,4]{1,0:T(8,128)}), f32[256,4]{1,0:T(8,128)}) %reduce-scatter.29.cloned.1.call-update) | async-done | bytes 4112
  950.3 150.0 %reduce-scatter.21.cloned.1.call-done = bf16[256,2048]{1,0:T(8,128)(2,1)} async-done(((bf16[2048,2048]{1,0:T(8,128)(2,1)}), bf16[256,2048]{1,0:T(8,128)(2,1)}) %reduce-scatter.21.cloned.1.call-update) | async-done | bytes 1048592 | tf_op jit(solution)/shard_map/reduce_scatter | solution.py:229
  1100.3 2.8 convert_element_type.253
  1103.1 149.7 %reduce-scatter.23.cloned.1.call-done = bf16[2048,256]{1,0:T(8,128)(2,1)} async-done(((bf16[2048,2048]{1,0:T(8,128)(2,1)}), bf16[2048,256]{1,0:T(8,128)(2,1)}) %reduce-scatter.23.cloned.1.call-update) | async-done | bytes 1048592 | tf_op jit(solution)/shard_map/reduce_scatter | solution.py:232
  1252.8 2.7 convert_element_type.255
  1255.5 88.9 %reduce-scatter.19.cloned.1.call-done = f32[512,256]{1,0:T(8,128)} async-done(((f32[512,2048]{1,0:T(8,128)}), f32[512,256]{1,0:T(8,128)}) %reduce-scatter.19.cloned.1.call-update) | async-done | bytes 524304 | tf_op jit(solution)/shard_map/reduce_scatter | solution.py:345
  1344.4 212.0 %reduce-scatter.17.cloned.1.call-done = f32[256,3,512]{2,0,1:T(8,128)} async-done(((f32[2048,3,512]{2,0,1:T(8,128)}), f32[256,3,512]{2,0,1:T(8,128)}) %reduce-scatter.17.cloned.1.call-update) | async-done | bytes 1572880 | tf_op jit(solution)/shard_map/reduce_scatter | solution.py:344
  (245 shorter events, 66.4 us)
Async XLA Ops:
  7.2 68.2 %copy-start.59 = (u32[32]{0:T(128)S(1)}, u32[32]{0:T(128)}, u32[]{:S(2)}) copy-start(u32[32]{0:T(128)} %constant.119) | copy-start | bytes 388
  7.2 105.7 %copy-start.2 = (bf16[256,2048]{1,0:T(8,128)(2,1)S(1)}, bf16[256,2048]{1,0:T(8,128)(2,1)}, u32[]{:S(2)}) copy-start(bf16[256,2048]{1,0:T(8,128)(2,1)} %param.13) | copy-start | bytes 3145732
  7.2 68.0 %copy-start.62 = (s32[2]{0:T(128)S(1)}, s32[2]{0:T(128)}, u32[]{:S(2)}) copy-start(s32[2]{0:T(128)} %param.15) | copy-start | bytes 28
  7.2 69.4 %copy-start.63 = (bf16[64]{0:T(256)(128)(2,1)S(1)}, bf16[64]{0:T(256)(128)(2,1)}, u32[]{:S(2)}) copy-start(bf16[64]{0:T(256)(128)(2,1)} %param.18) | copy-start | bytes 388
  7.2 105.6 %all-gather.7.cloned.1.call-start = ((), (), s32[]{:S(2)}) async-start(), calls=%async_computation.8 | async-start | bytes 7077888 | tf_op jit(solution)/shard_map/all_gather | solution.py:109
  8.0 156.3 %all-gather.9.cloned.1.call-start = ((), (), s32[]{:S(2)}) async-start(), calls=%async_computation.9 | async-start | bytes 2359296 | tf_op jit(solution)/shard_map/all_gather | solution.py:110
  8.7 209.0 %all-reduce.12.cloned.1.call-start = ((), (), s32[]{:S(2)}) async-start(), calls=%async_computation.10 | async-start | bytes 4194304 | tf_op jit(solution)/shard_map/psum | solution.py:77
  75.3 473.1 %copy-start.53 = (f32[256]{0:T(256)}, f32[256]{0:T(256)S(1)}, u32[]{:S(2)}) copy-start(f32[256]{0:T(256)S(1)} %get-tuple-element.94) | copy-start | bytes 3076
  75.3 88.9 %copy-start.31 = (f32[1,512]{1,0:T(1,128)}, f32[1,512]{1,0:T(1,128)S(1)}, u32[]{:S(2)}) copy-start(f32[1,512]{1,0:T(1,128)S(1)} %slice.97) | copy-start | bytes 6148
  96.4 461.9 %copy-start.25 = (f32[512]{0:T(512)}, f32[512]{0:T(512)S(1)}, u32[]{:S(2)}) copy-start(f32[512]{0:T(512)S(1)} %convert_element_type.236) | copy-start | bytes 6148
  96.4 22.3 %copy-start.45 = (f32[256]{0:T(256)}, f32[256]{0:T(256)S(1)}, u32[]{:S(2)}) copy-start(f32[256]{0:T(256)S(1)} %get-tuple-element.90) | copy-start | bytes 3076
  96.4 22.2 %copy-start.47 = (f32[256]{0:T(256)}, f32[256]{0:T(256)S(1)}, u32[]{:S(2)}) copy-start(f32[256]{0:T(256)S(1)} %get-tuple-element.91) | copy-start | bytes 3076
  96.5 29.2 %copy-start.15 = (f32[128,32]{0,1:T(8,128)}, f32[128,32]{0,1:T(8,128)S(1)}, u32[]{:S(2)}) copy-start(f32[128,32]{0,1:T(8,128)S(1)} %get-tuple-element.86) | copy-start | bytes 49156
  96.5 29.2 %copy-start.16 = (f32[128,32]{0,1:T(8,128)}, f32[128,32]{0,1:T(8,128)S(1)}, u32[]{:S(2)}) copy-start(f32[128,32]{0,1:T(8,128)S(1)} %get-tuple-element.87) | copy-start | bytes 49156
  96.7 29.1 %copy-start.17 = (f32[128,32]{0,1:T(8,128)}, f32[128,32]{0,1:T(8,128)S(1)}, u32[]{:S(2)}) copy-start(f32[128,32]{0,1:T(8,128)S(1)} %get-tuple-element.88) | copy-start | bytes 49156
  96.7 29.1 %copy-start.18 = (f32[128,32]{0,1:T(8,128)}, f32[128,32]{0,1:T(8,128)S(1)}, u32[]{:S(2)}) copy-start(f32[128,32]{0,1:T(8,128)S(1)} %get-tuple-element.89) | copy-start | bytes 49156
  96.8 21.8 %copy-start.21 = (f32[1,2048]{1,0:T(1,128)}, f32[1,2048]{1,0:T(1,128)S(1)}, u32[]{:S(2)}) copy-start(f32[1,2048]{1,0:T(1,128)S(1)} %get-tuple-element.79) | copy-start | bytes 24580
  97.5 21.2 %copy-start.35 = (f32[1,2048]{1,0:T(1,128)}, f32[1,2048]{1,0:T(1,128)S(1)}, u32[]{:S(2)}) copy-start(f32[1,2048]{1,0:T(1,128)S(1)} %get-tuple-element.75) | copy-start | bytes 24580
  97.5 247.5 %copy-start.19 = (f32[1,2048]{1,0:T(1,128)}, f32[1,2048]{1,0:T(1,128)S(1)}, u32[]{:S(2)}) copy-start(f32[1,2048]{1,0:T(1,128)S(1)} %get-tuple-element.73) | copy-start | bytes 24580
  130.4 37.5 %copy-start.4 = (f32[256,512]{1,0:T(8,128)}, f32[256,512]{1,0:T(8,128)S(1)}, u32[]{:S(2)}) copy-start(f32[256,512]{1,0:T(8,128)S(1)} %reshape.331) | copy-start | bytes 1572868
  136.2 422.1 %copy-start.27 = (f32[256,1]{0,1:T(1,128)}, f32[256,1]{0,1:T(1,128)S(1)}, u32[]{:S(2)}) copy-start(f32[256,1]{0,1:T(1,128)S(1)} %get-tuple-element.84) | copy-start | bytes 3076
  136.2 422.1 %copy-start.29 = (f32[256,1]{0,1:T(1,128)}, f32[256,1]{0,1:T(1,128)S(1)}, u32[]{:S(2)}) copy-start(f32[256,1]{0,1:T(1,128)S(1)} %get-tuple-element.85) | copy-start | bytes 3076
  167.9 19.0 %copy-start.60 = (bf16[2,256]{1,0:T(2,128)(2,1)S(1)}, bf16[2,256]{1,0:T(2,128)(2,1)}, u32[]{:S(2)}) copy-start(bf16[2,256]{1,0:T(2,128)(2,1)} %param.25) | copy-start | bytes 3076
  168.0 177.0 %all-gather.11.cloned.1.call-start = ((), (), s32[]{:S(2)}) async-start(), calls=%async_computation.11 | async-start | bytes 9437184 | tf_op jit(solution)/shard_map/all_gather | solution.py:117
  168.6 302.1 %all-gather.13.cloned.1.call-start = ((), (), s32[]{:S(2)}) async-start(), calls=%async_computation.12 | async-start | bytes 9437184 | tf_op jit(solution)/shard_map/all_gather | solution.py:118
  169.1 376.0 %all-reduce.14.cloned.1.call-start = ((), (), s32[]{:S(2)}) async-start(), calls=%async_computation.13 | async-start | bytes 4194304 | tf_op jit(solution)/shard_map/psum | solution.py:77
  204.0 291.9 %copy-start.23 = (f32[1,2048]{1,0:T(1,128)}, f32[1,2048]{1,0:T(1,128)S(1)}, u32[]{:S(2)}) copy-start(f32[1,2048]{1,0:T(1,128)S(1)} %get-tuple-element.76) | copy-start | bytes 24580
  219.8 328.6 %copy-start.40 = (f32[256]{0:T(256)}, f32[256]{0:T(256)S(1)}, u32[]{:S(2)}) copy-start(f32[256]{0:T(256)S(1)} %get-tuple-element.82) | copy-start | bytes 3076
  219.8 328.6 %copy-start.42 = (f32[256]{0:T(256)}, f32[256]{0:T(256)S(1)}, u32[]{:S(2)}) copy-start(f32[256]{0:T(256)S(1)} %get-tuple-element.83) | copy-start | bytes 3076
  362.5 133.4 %copy-start.49 = (f32[256,1]{0,1:T(1,128)}, f32[256,1]{0,1:T(1,128)S(1)}, u32[]{:S(2)}) copy-start(f32[256,1]{0,1:T(1,128)S(1)} %get-tuple-element.80) | copy-start | bytes 3076
  362.5 133.4 %copy-start.51 = (f32[256,1]{0,1:T(1,128)}, f32[256,1]{0,1:T(1,128)S(1)}, u32[]{:S(2)}) copy-start(f32[256,1]{0,1:T(1,128)S(1)} %get-tuple-element.81) | copy-start | bytes 3076
  485.8 6.1 copy-start.61
  495.6 190.7 %all-reduce.16.cloned.1.call-start = ((), (), s32[]{:S(2)}) async-start(), calls=%async_computation.22 | async-start | bytes 8388608 | tf_op jit(solution)/shard_map/psum | solution.py:77
  566.8 8.5 copy-start.14
  599.8 86.6 %copy-start.22 = (f32[1,2048]{1,0:T(1,128)S(1)}, f32[1,2048]{1,0:T(1,128)}, u32[]{:S(2)}) copy-start(f32[1,2048]{1,0:T(1,128)} %copy-done.21) | copy-start | bytes 24580
  599.8 86.5 %copy-start.46 = (f32[256]{0:T(256)S(1)}, f32[256]{0:T(256)}, u32[]{:S(2)}) copy-start(f32[256]{0:T(256)} %copy-done.45) | copy-start | bytes 3076
  599.8 86.5 %copy-start.48 = (f32[256]{0:T(256)S(1)}, f32[256]{0:T(256)}, u32[]{:S(2)}) copy-start(f32[256]{0:T(256)} %copy-done.47) | copy-start | bytes 3076
  599.8 152.9 %reduce-scatter.31.cloned.1.call-start = ((), (), s32[]{:S(2)}) async-start(), calls=%async_computation.21 | async-start | bytes 589824
  601.6 87.4 %copy-start.33 = (f32[2048]{0:T(1024)S(1)}, f32[2048]{0:T(1024)}, u32[]{:S(2)}) copy-start(f32[2048]{0:T(1024)} %get-tuple-element.14) | copy-start | bytes 24580
  601.6 214.7 %reduce-scatter.25.cloned.1.call-start = ((), (), s32[]{:S(2)}) async-start(), calls=%async_computation.18 | async-start | bytes 294912
  603.7 278.8 %reduce-scatter.27.cloned.1.call-start = ((), (), s32[]{:S(2)}) async-start(), calls=%async_computation.19 | async-start | bytes 1179648
  690.4 258.4 %reduce-scatter.29.cloned.1.call-start = ((), (), s32[]{:S(2)}) async-start(), calls=%async_computation.20 | async-start | bytes 1179648
  691.9 408.4 %reduce-scatter.21.cloned.1.call-start = ((), (), s32[]{:S(2)}) async-start(), calls=%async_computation.16 | async-start | bytes 9437184 | tf_op jit(solution)/shard_map/reduce_scatter | solution.py:229
  699.3 553.6 %reduce-scatter.23.cloned.1.call-start = ((), (), s32[]{:S(2)}) async-start(), calls=%async_computation.17 | async-start | bytes 9437184 | tf_op jit(solution)/shard_map/reduce_scatter | solution.py:232
  707.7 636.7 %reduce-scatter.19.cloned.1.call-start = ((), (), s32[]{:S(2)}) async-start(), calls=%async_computation.15 | async-start | bytes 4718592 | tf_op jit(solution)/shard_map/reduce_scatter | solution.py:345
  713.0 843.4 %reduce-scatter.17.cloned.1.call-start = ((), (), s32[]{:S(2)}) async-start(), calls=%async_computation.14 | async-start | bytes 14155776 | tf_op jit(solution)/shard_map/reduce_scatter | solution.py:344
  721.3 32.9 %copy-start.56 = (f32[512]{0:T(512)S(1)}, f32[512]{0:T(512)}, u32[]{:S(2)}) copy-start(f32[512]{0:T(512)} %get-tuple-element.28) | copy-start | bytes 6148
  721.3 96.4 %copy-start.34 = (f32[1,2048]{1,0:T(1,128)S(1)}, f32[1,2048]{1,0:T(1,128)}, u32[]{:S(2)}) copy-start(f32[1,2048]{1,0:T(1,128)} %get-tuple-element.72) | copy-start | bytes 24580
  (32 other events, 62.4 us)
Sparse Core Ops, SparseCore 0:
  10.2 102.5 all-gather.6
  114.9 49.3 all-gather.8
  168.1 49.5 all-reduce.11
  219.9 125.0 all-gather.10
  347.0 123.5 all-gather.12
  495.8 49.3 all-reduce.13
  599.9 86.3 all-reduce.15
  690.6 62.0 reduce-scatter.30
  756.0 60.2 reduce-scatter.24
  820.1 62.3 reduce-scatter.26
  886.3 62.4 reduce-scatter.28
  952.2 148.0 reduce-scatter.20
  1104.4 148.3 reduce-scatter.22
  1256.9 87.4 reduce-scatter.18
  1348.9 207.5 reduce-scatter.16
where the time goes:
time: 1570 us; the launch traced here: 1560 us
  waiting for transfers between devices  1190 us (76%)
  blocking collectives  184 us (12%)
  matrix products  90.4 us (6%)
  local copies, waits for them, and re-layouts  43.9 us (3%)
  other arithmetic  35.3 us (2%)
  between operations  17.2 us (1%)
    reduce_scatter x1, waiting for transfers between devices, per_device(): lax.psum_scatter(grad_qkv, 'fsdp', scatter_dimension=0, tiled=True)  212 us
    unnamed x19, waiting for transfers between devices  177 us
    reduce_scatter x1, waiting for transfers between devices, per_device(): lax.psum_scatter(grad_fc1.astype(jnp.bfloat16), 'fsdp', scatter_dimension...  150 us
    reduce_scatter x1, waiting for transfers between devices, per_device(): lax.psum_scatter(grad_fc2.astype(jnp.bfloat16), 'fsdp', scatter_dimension...  150 us
    psum x3, waiting for transfers between devices, width_total(): return lax.psum(product, 'tp')  137 us
    all_gather x1, waiting for transfers between devices, per_device(): lax.all_gather(w_fc1, 'fsdp', axis=0, tiled=True)  125 us
    all_gather x1, waiting for transfers between devices, per_device(): lax.all_gather(w_fc2, 'fsdp', axis=1, tiled=True)  108 us
    reduce_scatter x1, waiting for transfers between devices, per_device(): lax.psum_scatter(grad_out_proj, 'fsdp', scatter_dimension=1, tiled=True)  88.9 us
  transfers between devices with their start and end apart: 15, of which 15 were waited for; matrix products, arithmetic and copies ran while one was open for 6% of the time, Pallas kernels for 0%

commit v1 on v0

v1 whole, which is shorter than its diff:
```python
import functools
import math

import jax
import jax.numpy as jnp
from jax import lax
from jax.sharding import PartitionSpec as P

HEADS = 32
FF = 8192
IMAGE = 64
GROUPS = 4

f32 = jnp.float32
bf16 = jnp.bfloat16
norm_eps = 1e-05


def pick(table, index):
    return lax.dynamic_index_in_dim(jnp.asarray(table, jnp.int32), index, keepdims=False)


def put(buffer, block, index):
    return lax.dynamic_update_slice(buffer, block[None], (index,) + (0,) * block.ndim)


def put_all(buffer, blocks, index_of, k):
    for label in range(blocks.shape[0]):
        buffer = put(buffer, blocks[label], index_of(k, label))
    return buffer


def block_at(array, index, axis=0):
    return lax.dynamic_index_in_dim(array, index, axis, keepdims=False)


class Ring:
    def __init__(self, members, here, of_group):
        self.size = len(members[0])
        self.sorted_members = [sorted(ring) for ring in members]
        device_count = sum(len(ring) for ring in members)
        place = [0] * device_count
        for ring in members:
            for step, device in enumerate(ring):
                place[device] = step
        self.position = pick(place, here)
        self.labels = [of_group(device) for device in members[0]]
        self.forward = [
            (ring[i], ring[(i + 1) % self.size]) for ring in members for i in range(self.size)
        ]
        self.backward = [(b, a) for a, b in self.forward]

    def label(self, offset):
        return pick(self.labels, (self.position + offset) % self.size)

    def send(self, block, way):
        return lax.ppermute(block, "fsdp", self.forward if way > 0 else self.backward)

    def gather_native(self, chunk):
        return lax.all_gather(chunk, "fsdp", axis=0, axis_index_groups=self.sorted_members)

    def scatter_native(self, part):
        return lax.psum_scatter(
            part,
            "fsdp",
            scatter_dimension=0,
            axis_index_groups=self.sorted_members,
            tiled=False,
        ).astype(f32)

    def gather(self, chunks, buffers, index_of=lambda k, label: label):
        if self.size > 4 * GROUPS:
            gathered = [self.gather_native(c) for c in chunks]
            return [put_all(b, g, index_of, k) for k, (b, g) in enumerate(zip(buffers, gathered))]
        half = self.size // 2
        buffers = [put(b, c, index_of(k, self.label(0))) for k, (b, c) in enumerate(zip(buffers, chunks))]
        onward = list(chunks)
        backward = list(chunks)
        for step in range(1, half):
            for k in range(len(chunks)):
                onward[k] = self.send(onward[k], 1)
                backward[k] = self.send(backward[k], -1)
                buffers[k] = put(buffers[k], onward[k], index_of(k, self.label(-step)))
                buffers[k] = put(buffers[k], backward[k], index_of(k, self.label(step)))
        for k in range(len(chunks)):
            cut = chunks[k].shape[0] // 2
            last = jnp.concatenate(
                [self.send(onward[k][:cut], 1), self.send(backward[k][cut:], -1)], axis=0
            )
            buffers[k] = put(buffers[k], last, index_of(k, self.label(half)))
        return buffers

    def scatter(self, parts):
        if self.size > 4 * GROUPS:
            return [self.scatter_native(part) for part in parts]
        half = self.size // 2
        onward, backward = [], []
        for part in parts:
            far = block_at(part, self.label(half))
            cut = part.shape[1] // 2
            onward.append(self.send(far[:cut], 1))
            backward.append(self.send(far[cut:], -1))
        for step in range(half - 1, 0, -1):
            for k, part in enumerate(parts):
                ahead = block_at(part, self.label(step)).astype(f32)
                behind = block_at(part, self.label(-step)).astype(f32)
                if step == half - 1:
                    cut = part.shape[1] // 2
                    ahead = jnp.concatenate(
                        [ahead[:cut] + onward[k].astype(f32), ahead[cut:]], axis=0
                    )
                    behind = jnp.concatenate(
                        [behind[:cut], behind[cut:] + backward[k].astype(f32)], axis=0
                    )
                else:
                    ahead = ahead + onward[k].astype(f32)
                    behind = behind + backward[k].astype(f32)
                onward[k] = self.send(ahead.astype(part.dtype), 1)
                backward[k] = self.send(behind.astype(part.dtype), -1)
        sums = []
        for k, part in enumerate(parts):
            own = block_at(part, self.label(0)).astype(f32)
            if half == 1:
                sums.append(own + jnp.concatenate([onward[k], backward[k]], axis=0).astype(f32))
            else:
                sums.append(own + onward[k].astype(f32) + backward[k].astype(f32))
        return sums


def tp_send(block, mask):
    return lax.ppermute(block, "tp", [(i, i ^ mask) for i in range(4)])


def tp_sum(values):
    return values + tp_send(values, 1) + tp_send(values, 2) + tp_send(values, 3)


def tp_rows_gather(piece, buffer, rank):
    across = tp_send(piece, 2)
    buffer = put(buffer, piece, rank)
    buffer = put(buffer, tp_send(piece, 1), rank ^ 1)
    buffer = put(buffer, across, rank ^ 2)
    return put(buffer, tp_send(across, 1), rank ^ 3)


def rotation_tables(count, row_width):
    position = jnp.arange(count).astype(f32)[:, None]
    channel = jnp.arange(row_width // 2).astype(f32)[None, :]
    frequency = jnp.exp(-(2.0 * channel / row_width) * jnp.log(10000.0))
    angle = position * frequency
    zeta_base = (2.0 * channel + 0.4 * row_width) / (1.4 * row_width)
    growth = jnp.exp((position - count // 2) / 512.0 * jnp.log(zeta_base))
    return (jnp.cos(angle), jnp.sin(angle), growth)


def turn(values, cosine, sine_table, factor):
    paired = values.reshape(values.shape[:-1] + (values.shape[-1] // 2, 2))
    even_part = paired[..., 0]
    odd_part = paired[..., 1]
    cosine = cosine[:, None, :]
    sine_table = sine_table[:, None, :]
    factor = factor[:, None, :]
    new_even = (even_part * cosine - odd_part * sine_table) * factor
    new_odd = (odd_part * cosine + even_part * sine_table) * factor
    return jnp.stack([new_even, new_odd], axis=-1).reshape(values.shape)


def turn_back(values, cosine, sine_table, factor):
    paired = values.reshape(values.shape[:-1] + (values.shape[-1] // 2, 2))
    even_part = paired[..., 0] * factor[:, None, :]
    odd_part = paired[..., 1] * factor[:, None, :]
    cosine = cosine[:, None, :]
    sine_table = sine_table[:, None, :]
    new_even = even_part * cosine + odd_part * sine_table
    new_odd = odd_part * cosine - even_part * sine_table
    return jnp.stack([new_even, new_odd], axis=-1).reshape(values.shape)


def norm_stats(first_sum, square_sum, row_width):
    mean_value = first_sum / row_width
    variance = square_sum / row_width - mean_value * mean_value
    return mean_value, lax.rsqrt(variance + norm_eps)


def norm_rows(values, gain_vector, shift_vector):
    width = values.shape[-1]
    mean_value, inverse = norm_stats(
        jnp.sum(values, axis=-1, keepdims=True),
        jnp.sum(values * values, axis=-1, keepdims=True),
        width,
    )
    hat = (values - mean_value) * inverse
    return hat * gain_vector + shift_vector, hat, inverse


def norm_back_rows(scaled, hat, inverse):
    width = scaled.shape[-1]
    return inverse * (
        scaled
        - jnp.sum(scaled, axis=-1, keepdims=True) / width
        - hat * jnp.sum(scaled * hat, axis=-1, keepdims=True) / width
    )


def matmul(a, b, dims):
    return lax.dot_general(a, b, (dims, ((), ())), preferred_element_type=f32)


def per_device(
    tokens,
    cotangent,
    caption_lengths,
    w_qkv,
    head_biases,
    head_gain,
    w_out,
    model_gains,
    model_biases,
    w_fc1,
    w_fc2,
    ffn_gain,
    ffn_biases,
    *,
    fsdp_size,
):
    here = lax.axis_index("fsdp")
    rank = lax.axis_index("tp")
    core, side = rank % 2, rank // 2
    others = fsdp_size // GROUPS
    group, member = here // others, here % others
    ring = Ring(
        [list(range(0, fsdp_size, 2)) + list(range(fsdp_size - 1, 0, -2))], here, lambda f: f
    )
    member_ring = Ring(
        [[g * others + o for o in range(others)] for g in range(GROUPS)],
        here,
        lambda f: f % others,
    )

    def group_send(block, shift):
        return lax.ppermute(
            block,
            "fsdp",
            [
                (g * others + o, (g + shift) % GROUPS * others + o)
                for g in range(GROUPS)
                for o in range(others)
            ],
        )

    pair_count = caption_lengths.shape[0]
    row_count, model_width = tokens.shape
    slot_count = row_count // pair_count
    sub_rows = row_count // 4
    head_dim = model_width // HEADS
    local_width = w_qkv.shape[2]
    local_heads = local_width // head_dim
    block_rows = w_qkv.shape[0]
    hidden_width = FF
    local_hidden = w_fc1.shape[1] // GROUPS

    model_part = jnp.concatenate([model_gains, model_biases], axis=0)
    head_part = jnp.concatenate([head_biases, head_gain[None]], axis=0)
    unit_part = jnp.concatenate([ffn_biases, ffn_gain[None]], axis=0)
    packed = jnp.concatenate([model_part.reshape(-1), head_part.reshape(-1), unit_part.reshape(-1)])
    packed_size = packed.shape[0]
    packed = jnp.pad(packed, (0, -packed_size % 256)).reshape(2, -1)
    qkv_blocks = [w_qkv[:, c] for c in range(3)]

    def room(chunk):
        return jnp.zeros((fsdp_size,) + chunk.shape, chunk.dtype)

    first = [packed] + qkv_blocks
    vectors, *qkv_full = ring.gather(first, [room(c) for c in first])
    qkv_full = [w.reshape(model_width, local_width) for w in qkv_full]
    vectors = vectors.reshape(fsdp_size, -1)[:, :packed_size]
    sizes = [model_part.size, head_part.size, unit_part.size]
    model_vectors = (
        vectors[:, : sizes[0]].reshape((fsdp_size,) + model_part.shape).transpose(1, 0, 2)
    ).reshape(6, model_width).astype(f32)
    head_vectors = (
        vectors[:, sizes[0] : sizes[0] + sizes[1]]
        .reshape((fsdp_size,) + head_part.shape)
        .transpose(1, 0, 2)
    ).reshape(5, local_width).astype(f32)
    unit_all = vectors[:, sizes[0] + sizes[1] :].reshape((GROUPS, others) + unit_part.shape)
    unit_vectors = block_at(unit_all, group).transpose(1, 0, 2).reshape(3, local_hidden).astype(f32)

    (out_full,) = ring.gather([w_out.T], [room(w_out.T)])
    out_full = out_full.reshape(model_width, local_width)

    fc_full = []
    for weights in (w_fc2.T, w_fc1):
        pieces = weights.reshape(block_rows, GROUPS, local_hidden)
        chunks = [block_at(pieces, group, 1)]
        for shift in range(1, GROUPS):
            chunks.append(group_send(block_at(pieces, (group + shift) % GROUPS, 1), shift))
        buffer = jnp.zeros((fsdp_size, block_rows, local_hidden), bf16)
        for shift in range(GROUPS):
            (buffer,) = member_ring.gather(
                [chunks[shift]],
                [buffer],
                lambda k, label, s=shift: (group - s) % GROUPS * others + label,
            )
        fc_full.append(buffer.reshape(model_width, local_hidden))
    fc2_full, fc1_full = fc_full

    def rows_gather(piece):
        buffer = jnp.zeros((GROUPS * 4,) + piece.shape, piece.dtype)
        pieces = [piece] + [group_send(piece, shift) for shift in range(1, GROUPS)]
        for shift, block in enumerate(pieces):
            base = (group - shift) % GROUPS * 4
            across = tp_send(block, 2)
            buffer = put(buffer, block, base + rank)
            buffer = put(buffer, tp_send(block, 1), base + (rank ^ 1))
            buffer = put(buffer, across, base + (rank ^ 2))
            buffer = put(buffer, tp_send(across, 1), base + (rank ^ 3))
        return buffer.reshape(GROUPS * 4 * piece.shape[0], piece.shape[1])

    def rows_product(left, right, dims):
        by_rank = left.reshape(2, 2, sub_rows, left.shape[1])
        away = block_at(by_rank, 1 - core, 1).reshape(2 * sub_rows, -1)
        sent = tp_send(matmul(away, right, dims).astype(bf16), 1)
        kept = block_at(by_rank, core, 1).reshape(2 * sub_rows, -1)
        total = (matmul(kept, right, dims) + sent.astype(f32)).reshape(2, sub_rows, -1)
        crossing = tp_send(block_at(total, 1 - side).astype(bf16), 2)
        return block_at(total, side) + crossing.astype(f32)

    def group_product(left, right, dims):
        by_rank = left.reshape(GROUPS * 2, 2, sub_rows, left.shape[1])
        width = GROUPS * 2 * sub_rows
        away = block_at(by_rank, 1 - core, 1).reshape(width, -1)
        sent = tp_send(matmul(away, right, dims).astype(bf16), 1)
        kept = block_at(by_rank, core, 1).reshape(width, -1)
        total = (matmul(kept, right, dims) + sent.astype(f32)).reshape(GROUPS, 2, sub_rows, -1)
        pieces = []
        for shift in (2, 1, 3, 0):
            chunk = block_at(total, (group + shift) % GROUPS)
            crossing = tp_send(block_at(chunk, 1 - side).astype(bf16), 2)
            chunk = block_at(chunk, side) + crossing.astype(f32)
            if shift:
                chunk = group_send(chunk.astype(bf16), shift).astype(f32)
            pieces.append(chunk)
        return pieces[3] + pieces[0] + pieces[1] + pieces[2]

    def group_sum(values):
        values = tp_sum(values)
        return values + sum(group_send(values, shift) for shift in range(1, GROUPS))

    def my_rows(array):
        return lax.dynamic_slice_in_dim(array, rank * sub_rows, sub_rows, 0)

    slot_index = jnp.arange(slot_count)[None, :]
    key_valid = slot_index < IMAGE + caption_lengths[:, None]
    keep_rows = key_valid.reshape(row_count).astype(f32)[:, None]
    my_keep = my_rows(keep_rows)
    my_grad_out = my_rows(cotangent).astype(f32) * my_keep
    grad_out_all = rows_gather(my_grad_out.astype(bf16))

    cosine, sine_table, growth = rotation_tables(slot_count, head_dim)
    causal = jnp.arange(slot_count)[:, None] >= jnp.arange(slot_count)[None, :]
    allowed = causal[None, None] & key_valid[:, None, None, :]
    scale_value = 1.0 / math.sqrt(head_dim)
    normed_in, _, _ = norm_rows(tokens.astype(f32), model_vectors[0], model_vectors[2])
    normed_in_b = normed_in.astype(bf16)
    linear = [
        (matmul(normed_in_b, qkv_full[c], ((1,), (0,))) + head_vectors[c]).reshape(
            pair_count, slot_count, local_heads, head_dim
        )
        for c in range(3)
    ]
    queries = turn(linear[0], cosine, sine_table, growth).astype(bf16)
    keys_rot = turn(linear[1], cosine, sine_table, 1.0 / growth).astype(bf16)
    values_in = linear[2].astype(bf16)
    raw_scores = jnp.einsum("gqhe,gkhe->ghqk", queries, keys_rot, preferred_element_type=f32)
    scores = jnp.where(allowed, raw_scores * scale_value, -1e30)
    top_score = jnp.max(scores, axis=-1, keepdims=True)
    log_total = top_score + jnp.log(jnp.sum(jnp.exp(scores - top_score), axis=-1, keepdims=True))
    probs = jnp.exp(scores - log_total)
    heads_out = jnp.einsum(
        "ghqk,gkhe->gqhe", probs.astype(bf16), values_in, preferred_element_type=f32
    ).reshape(row_count, local_width)
    head_stats = tp_sum(
        jnp.stack([jnp.sum(heads_out, axis=-1), jnp.sum(heads_out * heads_out, axis=-1)])
    )
    mean_attn, inverse_attn = norm_stats(
        head_stats[0][:, None], head_stats[1][:, None], model_width
    )
    hat_attn = (heads_out - mean_attn) * inverse_attn
    post_attn_b = (hat_attn * head_vectors[4] + head_vectors[3]).astype(bf16)
    branch = rows_product(post_attn_b, out_full, ((1,), (1,)))
    middle = my_rows(tokens).astype(f32) + branch + model_vectors[4]
    normed_mid, hat_mid, inverse_mid = norm_rows(middle, model_vectors[1], model_vectors[3])

    normed_mid_all = rows_gather(normed_mid.astype(bf16))
    grad_post_ffn = matmul(grad_out_all, fc2_full, ((1,), (0,)))
    before = matmul(normed_mid_all, fc1_full, ((1,), (0,))) + unit_vectors[0]
    below = 0.5 * lax.erfc(-before * math.sqrt(0.5))
    active = before * below
    slope = below + before * (math.sqrt(0.5 / math.pi) * jnp.exp(-0.5 * before * before))
    scaled_ffn = grad_post_ffn * unit_vectors[2]
    sums = group_sum(
        jnp.stack(
            [
                jnp.sum(active, axis=-1),
                jnp.sum(active * active, axis=-1),
                jnp.sum(scaled_ffn, axis=-1),
                jnp.sum(scaled_ffn * active, axis=-1),
            ]
        )
    )[:, :, None]
    mean_ffn, inverse_ffn = norm_stats(sums[0], sums[1], hidden_width)
    hat_ffn = (active - mean_ffn) * inverse_ffn
    hat_sum = inverse_ffn * (sums[3] - mean_ffn * sums[2])
    grad_active = inverse_ffn * (
        scaled_ffn - sums[2] / hidden_width - hat_ffn * hat_sum / hidden_width
    )
    grad_before_b = (grad_active * slope).astype(bf16)
    grad_mid_normed = group_product(grad_before_b, fc1_full, ((1,), (1,)))
    grad_middle = my_grad_out + norm_back_rows(
        grad_mid_normed * model_vectors[1], hat_mid, inverse_mid
    )
    grad_middle_b = tp_rows_gather(
        grad_middle.astype(bf16), jnp.zeros((4, sub_rows, model_width), bf16), rank
    ).reshape(row_count, model_width)

    post_ffn_b = (hat_ffn * unit_vectors[2] + unit_vectors[1]).astype(bf16)
    second = group_product(post_ffn_b, fc2_full, ((1,), (1,)))
    out_rows = ((middle + second + model_vectors[5]) * my_keep).astype(bf16)
    layer_out = tp_rows_gather(
        out_rows, jnp.zeros((4, sub_rows, model_width), bf16), rank
    ).reshape(row_count, model_width)

    def fc_scatter(left, right):
        grad = matmul(left, right, ((0,), (0,))).astype(bf16)
        grad = grad.reshape(GROUPS, others, block_rows, local_hidden)
        buffer = jnp.zeros((GROUPS, block_rows, local_hidden), f32)
        for shift in (2, 1, 3, 0):
            (chunk,) = member_ring.scatter([block_at(grad, (group + shift) % GROUPS)])
            if shift:
                chunk = group_send(chunk.astype(bf16), shift).astype(f32)
            buffer = put(buffer, chunk, (group - shift) % GROUPS)
        return buffer.transpose(1, 0, 2).reshape(block_rows, GROUPS * local_hidden)

    grad_fc2_s = fc_scatter(grad_out_all, post_ffn_b).T
    grad_fc1_s = fc_scatter(normed_mid_all, grad_before_b)
    unit_grads = jnp.stack(
        [
            jnp.sum(grad_before_b.astype(f32), axis=0),
            jnp.sum(grad_post_ffn, axis=0),
            jnp.sum(grad_post_ffn * hat_ffn, axis=0),
        ]
    )

    grad_post_attn = matmul(grad_middle_b, out_full, ((1,), (0,)))
    grad_out_proj = matmul(grad_middle_b, post_attn_b, ((0,), (0,))).astype(bf16)
    (grad_out_s,) = ring.scatter([grad_out_proj.reshape(fsdp_size, block_rows, local_width)])
    scaled_attn = grad_post_attn * head_vectors[4]
    head_back = tp_sum(
        jnp.stack([jnp.sum(scaled_attn, axis=-1), jnp.sum(scaled_attn * hat_attn, axis=-1)])
    )[:, :, None]
    grad_heads_b = (
        (
            inverse_attn
            * (scaled_attn - head_back[0] / model_width - hat_attn * head_back[1] / model_width)
        )
        .astype(bf16)
        .reshape(pair_count, slot_count, local_heads, head_dim)
    )
    grad_probs = jnp.einsum("gqhe,gkhe->ghqk", grad_heads_b, values_in, preferred_element_type=f32)
    grad_values = jnp.einsum(
        "ghqk,gqhe->gkhe", probs.astype(bf16), grad_heads_b, preferred_element_type=f32
    )
    grad_scores = probs * (grad_probs - jnp.sum(probs * grad_probs, axis=-1, keepdims=True))
    grad_scores_b = (grad_scores * scale_value).astype(bf16)
    grad_queries = jnp.einsum(
        "ghqk,gkhe->gqhe", grad_scores_b, keys_rot, preferred_element_type=f32
    )
    grad_keys = jnp.einsum("ghqk,gqhe->gkhe", grad_scores_b, queries, preferred_element_type=f32)
    grad_linear = [
        part.reshape(row_count, local_width).astype(bf16)
        for part in (
            turn_back(grad_queries, cosine, sine_table, growth),
            turn_back(grad_keys, cosine, sine_table, 1.0 / growth),
            grad_values,
        )
    ]
    grad_qkv = [
        matmul(normed_in_b, part, ((0,), (0,)))
        .astype(bf16)
        .reshape(fsdp_size, block_rows, local_width)
        for part in grad_linear
    ]
    grad_qkv_s = jnp.stack(ring.scatter(grad_qkv), axis=1)
    grad_in_normed = rows_product(
        jnp.concatenate(grad_linear, axis=1),
        jnp.concatenate(qkv_full, axis=1),
        ((1,), (1,)),
    )
    _, hat_in, inverse_in = norm_rows(
        my_rows(tokens).astype(f32), model_vectors[0], model_vectors[2]
    )
    grad_token_rows = grad_middle + norm_back_rows(
        grad_in_normed * model_vectors[0], hat_in, inverse_in
    )
    grad_tokens = tp_rows_gather(
        grad_token_rows, jnp.zeros((4, sub_rows, model_width), f32), rank
    ).reshape(row_count, model_width)

    model_grads = jnp.stack(
        [
            jnp.sum(grad_in_normed * hat_in, axis=0),
            jnp.sum(grad_mid_normed * hat_mid, axis=0),
            jnp.sum(grad_in_normed, axis=0),
            jnp.sum(grad_mid_normed, axis=0),
            jnp.sum(grad_middle, axis=0),
            jnp.sum(my_grad_out, axis=0),
        ]
    )
    head_grads = jnp.stack(
        [jnp.sum(part.astype(f32), axis=0) for part in grad_linear]
        + [jnp.sum(grad_post_attn, axis=0), jnp.sum(grad_post_attn * hat_attn, axis=0)]
    )

    def by_block(vectors_in, blocks):
        return vectors_in.reshape(vectors_in.shape[0], blocks, -1).transpose(1, 0, 2)

    model_blocks = by_block(tp_sum(model_grads), fsdp_size).reshape(fsdp_size, -1)
    head_blocks = by_block(head_grads, fsdp_size).reshape(fsdp_size, -1)
    joined = jnp.concatenate([model_blocks, head_blocks], axis=1)
    joined_size = joined.shape[1]
    joined = jnp.pad(joined, ((0, 0), (0, -joined_size % 256))).reshape(fsdp_size, 2, -1)
    (joined_s,) = ring.scatter([joined])
    joined_s = joined_s.reshape(-1)
    model_s = joined_s[: model_blocks.shape[1]].reshape(6, -1)
    head_s = joined_s[model_blocks.shape[1] : joined_size].reshape(5, -1)
    unit_blocks = by_block(unit_grads, others).reshape(others, -1)
    unit_size = unit_blocks.shape[1]
    unit_blocks = jnp.pad(unit_blocks, ((0, 0), (0, -unit_size % 256))).reshape(others, 2, -1)
    (unit_s,) = member_ring.scatter([unit_blocks])
    unit_s = unit_s.reshape(-1)[:unit_size].reshape(3, -1)
    return (
        layer_out,
        grad_tokens,
        grad_qkv_s,
        head_s[:4],
        head_s[4],
        grad_out_s.T,
        model_s[:2],
        model_s[2:],
        grad_fc1_s,
        grad_fc2_s,
        unit_s[2],
        unit_s[:2],
    )


def solution(mesh):
    placed = (
        P("fsdp", None),
        P("fsdp", None),
        P("fsdp"),
        P("fsdp", None, "tp"),
        P(None, ("tp", "fsdp")),
        P(("tp", "fsdp")),
        P("tp", "fsdp"),
        P(None, "fsdp"),
        P(None, "fsdp"),
        P("fsdp", "tp"),
        P("tp", "fsdp"),
        P(("tp", "fsdp")),
        P(None, ("tp", "fsdp")),
    )
    return jax.shard_map(
        functools.partial(per_device, fsdp_size=mesh.shape["fsdp"]),
        mesh=mesh,
        in_specs=placed,
        out_specs=(
            P("fsdp", None),
            P("fsdp", None),
            P("fsdp", None, "tp"),
            P(None, ("tp", "fsdp")),
            P(("tp", "fsdp")),
            P("tp", "fsdp"),
            P(None, "fsdp"),
            P(None, "fsdp"),
            P("fsdp", "tp"),
            P("tp", "fsdp"),
            P(("tp", "fsdp")),
            P(None, ("tp", "fsdp")),
        ),
        check_vma=False,
    )
```

time: 1570 us -> 836 us (0.53)
  waiting for transfers between devices: 1190 us -> 206 us
  starting transfers between devices: 1.07 us -> 246 us
  blocking collectives: 184 us -> 0 us
  local copies, waits for them, and re-layouts: 43.9 us -> 199 us
  other arithmetic: 35.3 us -> 79.4 us
  matrix products: 90.4 us -> 65.4 us
    reduce_scatter x4 -> x0, waiting for transfers between devices: 601 us -> none  [the longest x1 212 us: per_device(): lax.psum_scatter(grad_qkv, 'fsdp', scatter_dimension=0, tiled=True)]
    all_gather x4 -> x0, waiting for transfers between devices: 277 us -> none  [the longest x1 125 us: per_device(): lax.all_gather(w_fc1, 'fsdp', axis=0, tiled=True)]
    ppermute x0 -> x200, starting transfers between devices: none -> 246 us  [the longest x114 139 us: send(): lax.ppermute(block, 'fsdp', self.forward if way > 0 else self.backward)]
    ppermute x0 -> x200, waiting for transfers between devices: none -> 206 us  [the longest x114 91.7 us: send(): lax.ppermute(block, 'fsdp', self.forward if way > 0 else self.backward)]
    unnamed x19 -> x0, waiting for transfers between devices: 177 us -> none
    psum x3 -> x0, waiting for transfers between devices: 137 us -> none  [width_total(): return lax.psum(product, 'tp')]
    all_gather x5 -> x0, blocking collectives: 99.3 us -> none  [the longest x1 28.3 us: per_device(): lax.all_gather(model_biases, 'fsdp', axis=1, tiled=True)]
    unnamed x3 -> x0, blocking collectives: 60.3 us -> none
  transfers between devices with their start and end apart: 15 -> 200, of which waited for: 15 -> 74; matrix products, arithmetic and copies ran while one was open for 6% -> 38% of each run, Pallas kernels for 0% -> 0%
where the time goes in v1:
time: 836 us; the launch traced here: 824 us
  starting transfers between devices  246 us (29%)
  waiting for transfers between devices  206 us (25%)
  local copies, waits for them, and re-layouts  199 us (24%)
  other arithmetic  79.4 us (9%)
  matrix products  65.4 us (8%)
  between operations  28.5 us (3%)
    ppermute x114, starting transfers between devices, send(): lax.ppermute(block, 'fsdp', self.forward if way > 0 else self.backward)  139 us
    ppermute x114, waiting for transfers between devices, send(): lax.ppermute(block, 'fsdp', self.forward if way > 0 else self.backward)  91.7 us
    ppermute x27, starting transfers between devices, group_send(): lax.ppermute(block, 'fsdp', [(g * others + o, (g + shift) % GROUPS * othe...  72.6 us
    ppermute x27, waiting for transfers between devices, group_send(): lax.ppermute(block, 'fsdp', [(g * others + o, (g + shift) % GROUPS * othe...  60.4 us
    dot_general x20, matrix products, matmul(): return lax.dot_general(a, b, (dims, ((), ())), preferred_element_type=f32)  56.6 us
    ppermute x59, waiting for transfers between devices, tp_send(): return lax.ppermute(block, 'tp', [(i, i ^ mask) for i in range(4)])  53.7 us
    dynamic_update_slice x91, local copies, waits for them, and re-layouts, put(): lax.dynamic_update_slice(buffer, block[None], (index,) + (0,) * block.ndim)  50.1 us
    unnamed x316, local copies, waits for them, and re-layouts  35.4 us
  transfers between devices with their start and end apart: 200, of which 74 were waited for; matrix products, arithmetic and copies ran while one was open for 38% of the time, Pallas kernels for 0%

profile of v1, /device:TPU:0, one launch (start us, length us, event | category | flops | bytes accessed | tf_op | source)
XLA Modules:
  0.0 823.8 jit_solution(2017292327691302053)
XLA Ops:
  3.7 3.1 collective-permute-start
  108.0 6.7 collective-permute-done.88
  117.0 3.0 collective-permute-done.62
  126.7 4.7 collective-permute-start.9
  133.7 3.2 collective-permute-start.36
  137.6 4.0 collective-permute-start.91
  143.7 14.0 %collective-permute-start.65 = (bf16[256,512]{1,0:T(8,128)(2,1)S(1)}, bf16[256,512]{1,0:T(8,128)(2,1)S(1)}, u32[]{:S(2)}, u32[]{:S(2)}) collective-permute-start(bf16[256,512]{1,0:T(8,128)(2,1)S(1)} %bitcast.882), channel_id=1, source_target_pairs={{0,16},{4,20},{8,24},{12,28},{16,0},{20,4},{24,8},{28,12},{1,17},{... | collective-permute-start | bytes 786440 | tf_op jit(solution)/shard_map/ppermute | solution.py:241
  158.5 10.8 %collective-permute-start.68 = (bf16[256,512]{1,0:T(8,128)(2,1)S(1)}, bf16[256,512]{1,0:T(8,128)(2,1)S(1)}, u32[]{:S(2)}, u32[]{:S(2)}) collective-permute-start(bf16[256,512]{1,0:T(8,128)(2,1)S(1)} %bitcast.881), channel_id=1, source_target_pairs={{0,24},{4,28},{8,0},{12,4},{16,8},{20,12},{24,16},{28,20},{1,25},{... | collective-permute-start | bytes 786440 | tf_op jit(solution)/shard_map/ppermute | solution.py:241
  169.3 5.4 collective-permute-start.89
  184.7 4.9 collective-permute-done.63
  214.1 3.9 collective-permute-done.76
  222.6 3.0 collective-permute-done.19
  291.8 3.2 convolution_add_fusion.1
  343.9 6.4 collective-permute-done.48
  350.9 9.9 %collective-permute-done.52 = bf16[64,2048]{1,0:T(8,128)(2,1)S(1)} collective-permute-done((bf16[64,2048]{1,0:T(8,128)(2,1)S(1)}, bf16[64,2048]{1,0:T(8,128)(2,1)S(1)}, u32[]{:S(2)}, u32[]{:S(2)}) %collective-permute-start.52) | collective-permute-done | bytes 262176 | tf_op jit(solution)/shard_map/ppermute | solution.py:241
  363.6 6.4 collective-permute-done.54
  370.0 5.2 collective-permute-done.58
  379.3 9.3 %multiply_reduce_fusion.3 = (f32[1024]{0:T(1024)S(1)}, f32[1024]{0:T(1024)S(1)}, f32[1024]{0:T(1024)S(1)}, f32[1024]{0:T(1024)S(1)}, f32[1024,512]{1,0:T(8,128)S...) fusion(f32[512]{0:T(512)S(1)} %bitcast.959, f32[1024,512]{1,0:T(8,128)S(1)} %fusion.202, f32[512]{0:T(512)S(1)} %bitcast.961, ...), kind=kOutput, calls=%fused_computation.56 | convolution fusion | flops 2185228288 | bytes 14700544 | tf_op jit(solution)/shard_map/dot_general | solution.py:206
  393.0 4.8 collective-permute-start.100
  408.1 5.0 convolution_convert_fusion
  424.7 4.3 convolution_convert_fusion.7
  466.6 3.5 collective-permute-start.195
  477.5 8.3 %collective-permute-start.181 = (bf16[256,512]{1,0:T(8,128)(2,1)}, bf16[256,512]{1,0:T(8,128)(2,1)}, u32[]{:S(2)}, u32[]{:S(2)}) collective-permute-start(bf16[256,512]{1,0:T(8,128)(2,1)} %get-tuple-element.105), channel_id=1, source_target_pairs={{0,8},{4,12},{8,16},{12,20},{16,24},{20,28},{24,0},{28,4},{1,9},{5... | collective-permute-start | bytes 786440 | tf_op jit(solution)/shard_map/ppermute | solution.py:241
  487.7 11.8 %collective-permute-done.178 = bf16[256,512]{1,0:T(8,128)(2,1)S(1)} collective-permute-done((bf16[256,512]{1,0:T(8,128)(2,1)}, bf16[256,512]{1,0:T(8,128)(2,1)S(1)}, u32[]{:S(2)}, u32[]{:S(2)}) %collective-permute-start.178) | collective-permute-done | bytes 262176 | tf_op jit(solution)/shard_map/ppermute | solution.py:241
  534.0 3.5 convert_add_fusion.1
  540.4 4.3 collective-permute-done.118
  546.0 4.3 collective-permute-done.120
  551.8 9.7 %collective-permute-done.105 = bf16[64,2048]{1,0:T(8,128)(2,1)S(1)} collective-permute-done((bf16[64,2048]{1,0:T(8,128)(2,1)S(1)}, bf16[64,2048]{1,0:T(8,128)(2,1)S(1)}, u32[]{:S(2)}, u32[]{:S(2)}) %collective-permute-start.105) | collective-permute-done | bytes 262176 | tf_op jit(solution)/shard_map/ppermute | solution.py:131
  561.6 5.6 collective-permute-done.107
  569.2 3.6 collective-permute-done.109
  576.6 6.3 collective-permute-done.117
  582.9 4.1 collective-permute-start.110
  592.8 10.9 %collective-permute-done.106 = bf16[64,2048]{1,0:T(8,128)(2,1)S(1)} collective-permute-done((bf16[64,2048]{1,0:T(8,128)(2,1)S(1)}, bf16[64,2048]{1,0:T(8,128)(2,1)S(1)}, u32[]{:S(2)}, u32[]{:S(2)}) %collective-permute-start.106) | collective-permute-done | bytes 262176 | tf_op jit(solution)/shard_map/ppermute | solution.py:241
  630.2 4.2 collective-permute-start.168
  671.0 4.5 constant_dynamic-slice_fusion.15
  675.5 3.4 copy.365
  678.9 5.9 fusion.4
  707.4 3.0 collective-permute-done.169
  712.8 3.2 collective-permute-done.134
  718.3 3.3 collective-permute-done.142
  728.5 3.9 fusion.3
  735.6 3.4 collective-permute-done.129
  748.2 4.9 collective-permute-done.143
  756.8 7.2 collective-permute-done.160
  766.2 3.1 collective-permute-done.161
  774.9 3.0 collective-permute-done.165
  798.0 3.2 collective-permute-done.155
  803.7 3.1 collective-permute-done.140
  (1055 shorter events, 538.7 us)
Async XLA Ops:
  3.7 41.7 %collective-permute-start = (bf16[2,1408]{1,0:T(2,128)(2,1)S(1)}, bf16[2,1408]{1,0:T(2,128)(2,1)S(1)}, u32[]{:S(2)}, u32[]{:S(2)}) collective-permute-start(bf16[2,1408]{1,0:T(2,128)(2,1)S(1)} %reshape.1016), channel_id=1, source_target_pairs={{0,8},{8,16},{16,24},{24,28},{28,20},{20,12},{12,4},{4,0},{1,9},{9... | collective-permute-start | bytes 16904 | tf_op jit(solution)/shard_map/ppermute | solution.py:57
  6.8 36.6 %collective-permute-start.1 = (bf16[2,1408]{1,0:T(2,128)(2,1)S(1)}, bf16[2,1408]{1,0:T(2,128)(2,1)S(1)}, u32[]{:S(2)}, u32[]{:S(2)}) collective-permute-start(bf16[2,1408]{1,0:T(2,128)(2,1)S(1)} %reshape.1016), channel_id=1, source_target_pairs={{8,0},{16,8},{24,16},{28,24},{20,28},{12,20},{4,12},{0,4},{9,1},{1... | collective-permute-start | bytes 16904 | tf_op jit(solution)/shard_map/ppermute | solution.py:57
  10.5 85.6 %collective-permute-start.86 = (bf16[128,512]{1,0:T(8,128)(2,1)}, bf16[128,512]{1,0:T(8,128)(2,1)}, u32[]{:S(2)}, u32[]{:S(2)}) collective-permute-start(bf16[128,512]{1,0:T(8,128)(2,1)} %get-tuple-element.189), channel_id=1, source_target_pairs={{0,4},{4,0},{8,12},{12,8},{16,20},{20,16},{24,28},{28,24},{1,5},{5... | collective-permute-start | bytes 393224 | tf_op jit(solution)/shard_map/ppermute | solution.py:57
  12.4 85.6 %collective-permute-start.87 = (bf16[128,512]{1,0:T(8,128)(2,1)}, bf16[128,512]{1,0:T(8,128)(2,1)}, u32[]{:S(2)}, u32[]{:S(2)}) collective-permute-start(bf16[128,512]{1,0:T(8,128)(2,1)} %get-tuple-element.190), channel_id=1, source_target_pairs={{4,0},{0,4},{12,8},{8,12},{20,16},{16,20},{28,24},{24,28},{5,1},{1... | collective-permute-start | bytes 393224 | tf_op jit(solution)/shard_map/ppermute | solution.py:57
  17.1 89.1 %collective-permute-start.71 = (bf16[64,2048]{1,0:T(8,128)(2,1)}, bf16[64,2048]{1,0:T(8,128)(2,1)}, u32[]{:S(2)}, u32[]{:S(2)}) collective-permute-start(bf16[64,2048]{1,0:T(8,128)(2,1)} %get-tuple-element.64), channel_id=1, source_target_pairs={{0,1},{1,0},{2,3},{3,2},{4,5},{5,4},{6,7},{7,6},{8,9},{9,8},{10,11... | collective-permute-start | bytes 786440 | tf_op jit(solution)/shard_map/ppermute | solution.py:131
  47.1 21.8 %collective-permute-start.5 = (bf16[2,1408]{1,0:T(2,128)(2,1)S(1)}, bf16[2,1408]{1,0:T(2,128)(2,1)S(1)}, u32[]{:S(2)}, u32[]{:S(2)}) collective-permute-start(bf16[2,1408]{1,0:T(2,128)(2,1)S(1)} %collective-permute-done.3), channel_id=1, source_target_pairs={{8,0},{16,8},{24,16},{28,24},{20,28},{12,20},{4,12},{0,4},{9,1},{1... | collective-permute-start | bytes 16904 | tf_op jit(solution)/shard_map/ppermute | solution.py:57
  49.1 22.4 %collective-permute-start.4 = (bf16[2,1408]{1,0:T(2,128)(2,1)S(1)}, bf16[2,1408]{1,0:T(2,128)(2,1)}, u32[]{:S(2)}, u32[]{:S(2)}) collective-permute-start(bf16[2,1408]{1,0:T(2,128)(2,1)S(1)} %collective-permute-done.2), channel_id=1, source_target_pairs={{0,8},{8,16},{16,24},{24,28},{28,20},{20,12},{12,4},{4,0},{1,9},{9... | collective-permute-start | bytes 16904 | tf_op jit(solution)/shard_map/ppermute | solution.py:57
  96.1 47.6 %collective-permute-start.72 = (bf16[64,2048]{1,0:T(8,128)(2,1)}, bf16[64,2048]{1,0:T(8,128)(2,1)S(1)}, u32[]{:S(2)}, u32[]{:S(2)}) collective-permute-start(bf16[64,2048]{1,0:T(8,128)(2,1)} %get-tuple-element.64), channel_id=1, source_target_pairs={{0,2},{1,3},{2,0},{3,1},{4,6},{5,7},{6,4},{7,5},{8,10},{9,11},{10,... | collective-permute-start | bytes 786440 | tf_op jit(solution)/shard_map/ppermute | solution.py:131
  98.0 107.8 %collective-permute-start.74 = (bf16[64,2048]{1,0:T(8,128)(2,1)}, bf16[64,2048]{1,0:T(8,128)(2,1)S(1)}, u32[]{:S(2)}, u32[]{:S(2)}) collective-permute-start(bf16[64,2048]{1,0:T(8,128)(2,1)} %get-tuple-element.64), channel_id=1, source_target_pairs={{0,8},{4,12},{8,16},{12,20},{16,24},{20,28},{24,0},{28,4},{1,9},{5... | collective-permute-start | bytes 786440 | tf_op jit(solution)/shard_map/ppermute | solution.py:241
  133.7 41.2 %collective-permute-start.36 = (bf16[256,512]{1,0:T(8,128)(2,1)S(1)}, bf16[256,512]{1,0:T(8,128)(2,1)S(1)}, u32[]{:S(2)}, u32[]{:S(2)}) collective-permute-start(bf16[256,512]{1,0:T(8,128)(2,1)S(1)} %bitcast.863), channel_id=1, source_target_pairs={{8,0},{16,8},{24,16},{28,24},{20,28},{12,20},{4,12},{0,4},{9,1},{1... | collective-permute-start | bytes 786440 | tf_op jit(solution)/shard_map/ppermute | solution.py:57
  142.3 27.0 %collective-permute-start.94 = (bf16[256,512]{1,0:T(8,128)(2,1)S(1)}, bf16[256,512]{1,0:T(8,128)(2,1)S(1)}, u32[]{:S(2)}, u32[]{:S(2)}) collective-permute-start(bf16[256,512]{1,0:T(8,128)(2,1)S(1)} %bitcast.883), channel_id=1, source_target_pairs={{0,24},{4,28},{8,0},{12,4},{16,8},{20,12},{24,16},{28,20},{1,25},{... | collective-permute-start | bytes 786440 | tf_op jit(solution)/shard_map/ppermute | solution.py:241
  143.7 31.1 %collective-permute-start.65 = (bf16[256,512]{1,0:T(8,128)(2,1)S(1)}, bf16[256,512]{1,0:T(8,128)(2,1)S(1)}, u32[]{:S(2)}, u32[]{:S(2)}) collective-permute-start(bf16[256,512]{1,0:T(8,128)(2,1)S(1)} %bitcast.882), channel_id=1, source_target_pairs={{0,16},{4,20},{8,24},{12,28},{16,0},{20,4},{24,8},{28,12},{1,17},{... | collective-permute-start | bytes 786440 | tf_op jit(solution)/shard_map/ppermute | solution.py:241
  205.8 32.7 %collective-permute-start.82 = (bf16[64,2048]{1,0:T(8,128)(2,1)}, bf16[64,2048]{1,0:T(8,128)(2,1)}, u32[]{:S(2)}, u32[]{:S(2)}) collective-permute-start(bf16[64,2048]{1,0:T(8,128)(2,1)} %get-tuple-element.64), channel_id=1, source_target_pairs={{0,24},{4,28},{8,0},{12,4},{16,8},{20,12},{24,16},{28,20},{1,25},{... | collective-permute-start | bytes 786440 | tf_op jit(solution)/shard_map/ppermute | solution.py:241
  209.5 39.6 %collective-permute-start.79 = (bf16[64,2048]{1,0:T(8,128)(2,1)S(1)}, bf16[64,2048]{1,0:T(8,128)(2,1)S(1)}, u32[]{:S(2)}, u32[]{:S(2)}) collective-permute-start(bf16[64,2048]{1,0:T(8,128)(2,1)S(1)} %collective-permute-done.78), channel_id=1, source_target_pairs={{0,1},{1,0},{2,3},{3,2},{4,5},{5,4},{6,7},{7,6},{8,9},{9,8},{10,11... | collective-permute-start | bytes 786440 | tf_op jit(solution)/shard_map/ppermute | solution.py:131
  210.5 39.5 %collective-permute-start.80 = (bf16[64,2048]{1,0:T(8,128)(2,1)S(1)}, bf16[64,2048]{1,0:T(8,128)(2,1)S(1)}, u32[]{:S(2)}, u32[]{:S(2)}) collective-permute-start(bf16[64,2048]{1,0:T(8,128)(2,1)S(1)} %collective-permute-done.78), channel_id=1, source_target_pairs={{0,2},{1,3},{2,0},{3,1},{4,6},{5,7},{6,4},{7,5},{8,10},{9,11},{10,... | collective-permute-start | bytes 786440 | tf_op jit(solution)/shard_map/ppermute | solution.py:131
  238.6 81.4 %collective-permute-start.83 = (bf16[64,2048]{1,0:T(8,128)(2,1)}, bf16[64,2048]{1,0:T(8,128)(2,1)}, u32[]{:S(2)}, u32[]{:S(2)}) collective-permute-start(bf16[64,2048]{1,0:T(8,128)(2,1)} %collective-permute-done.82), channel_id=1, source_target_pairs={{0,1},{1,0},{2,3},{3,2},{4,5},{5,4},{6,7},{7,6},{8,9},{9,8},{10,11... | collective-permute-start | bytes 786440 | tf_op jit(solution)/shard_map/ppermute | solution.py:131
  245.0 22.6 %collective-permute-start.84 = (bf16[64,2048]{1,0:T(8,128)(2,1)}, bf16[64,2048]{1,0:T(8,128)(2,1)}, u32[]{:S(2)}, u32[]{:S(2)}) collective-permute-start(bf16[64,2048]{1,0:T(8,128)(2,1)} %collective-permute-done.82), channel_id=1, source_target_pairs={{0,2},{1,3},{2,0},{3,1},{4,6},{5,7},{6,4},{7,5},{8,10},{9,11},{10,... | collective-permute-start | bytes 786440 | tf_op jit(solution)/shard_map/ppermute | solution.py:131
  268.6 59.3 %collective-permute-start.85 = (bf16[64,2048]{1,0:T(8,128)(2,1)}, bf16[64,2048]{1,0:T(8,128)(2,1)}, u32[]{:S(2)}, u32[]{:S(2)}) collective-permute-start(bf16[64,2048]{1,0:T(8,128)(2,1)} %collective-permute-done.84), channel_id=1, source_target_pairs={{0,1},{1,0},{2,3},{3,2},{4,5},{5,4},{6,7},{7,6},{8,9},{9,8},{10,11... | collective-permute-start | bytes 786440 | tf_op jit(solution)/shard_map/ppermute | solution.py:131
  280.0 21.4 %collective-permute-start.14 = (bf16[128,512]{1,0:T(8,128)(2,1)}, bf16[128,512]{1,0:T(8,128)(2,1)S(1)}, u32[]{:S(2)}, u32[]{:S(2)}) collective-permute-start(bf16[128,512]{1,0:T(8,128)(2,1)} %slice.776), channel_id=1, source_target_pairs={{0,8},{8,16},{16,24},{24,28},{28,20},{20,12},{12,4},{4,0},{1,9},{9... | collective-permute-start | bytes 393224 | tf_op jit(solution)/shard_map/ppermute | solution.py:57
  406.0 23.0 %collective-permute-start.198 = (f32[1,384]{1,0:T(1,128)S(1)}, f32[1,384]{1,0:T(1,128)S(1)}, u32[]{:S(2)}, u32[]{:S(2)}) collective-permute-start(f32[1,384]{1,0:T(1,128)S(1)} %get-tuple-element.222), channel_id=1, source_target_pairs={{0,4},{4,0},{8,12},{12,8},{16,20},{20,16},{24,28},{28,24},{1,5},{5... | collective-permute-start | bytes 4616 | tf_op jit(solution)/shard_map/ppermute | solution.py:57
  406.1 25.8 %collective-permute-start.199 = (f32[1,384]{1,0:T(1,128)S(1)}, f32[1,384]{1,0:T(1,128)S(1)}, u32[]{:S(2)}, u32[]{:S(2)}) collective-permute-start(f32[1,384]{1,0:T(1,128)S(1)} %get-tuple-element.223), channel_id=1, source_target_pairs={{4,0},{0,4},{12,8},{8,12},{20,16},{16,20},{28,24},{24,28},{5,1},{1... | collective-permute-start | bytes 4616 | tf_op jit(solution)/shard_map/ppermute | solution.py:57
  461.5 65.2 %collective-permute-start.114 = (bf16[512,2048]{1,0:T(8,128)(2,1)}, bf16[512,2048]{1,0:T(8,128)(2,1)}, u32[]{:S(2)}, u32[]{:S(2)}) collective-permute-start(bf16[512,2048]{1,0:T(8,128)(2,1)} %convolution_convert_fusion.6), channel_id=1, source_target_pairs={{0,1},{1,0},{2,3},{3,2},{4,5},{5,4},{6,7},{7,6},{8,9},{9,8},{10,11... | collective-permute-start | bytes 6291464 | tf_op jit(solution)/shard_map/ppermute | solution.py:131
  463.9 70.1 %collective-permute-start.103 = (bf16[512,2048]{1,0:T(8,128)(2,1)}, bf16[512,2048]{1,0:T(8,128)(2,1)}, u32[]{:S(2)}, u32[]{:S(2)}) collective-permute-start(bf16[512,2048]{1,0:T(8,128)(2,1)} %convolution_convert_fusion.7), channel_id=1, source_target_pairs={{0,1},{1,0},{2,3},{3,2},{4,5},{5,4},{6,7},{7,6},{8,9},{9,8},{10,11... | collective-permute-start | bytes 6291464 | tf_op jit(solution)/shard_map/ppermute | solution.py:131
  466.6 58.3 %collective-permute-start.195 = (bf16[256,512]{1,0:T(8,128)(2,1)}, bf16[256,512]{1,0:T(8,128)(2,1)}, u32[]{:S(2)}, u32[]{:S(2)}) collective-permute-start(bf16[256,512]{1,0:T(8,128)(2,1)} %get-tuple-element.93), channel_id=1, source_target_pairs={{0,24},{4,28},{8,0},{12,4},{16,8},{20,12},{24,16},{28,20},{1,25},{... | collective-permute-start | bytes 786440 | tf_op jit(solution)/shard_map/ppermute | solution.py:241
  474.0 25.5 %collective-permute-start.178 = (bf16[256,512]{1,0:T(8,128)(2,1)}, bf16[256,512]{1,0:T(8,128)(2,1)S(1)}, u32[]{:S(2)}, u32[]{:S(2)}) collective-permute-start(bf16[256,512]{1,0:T(8,128)(2,1)} %get-tuple-element.106), channel_id=1, source_target_pairs={{0,16},{4,20},{8,24},{12,28},{16,0},{20,4},{24,8},{28,12},{1,17},{... | collective-permute-start | bytes 786440 | tf_op jit(solution)/shard_map/ppermute | solution.py:241
  477.5 33.8 %collective-permute-start.181 = (bf16[256,512]{1,0:T(8,128)(2,1)}, bf16[256,512]{1,0:T(8,128)(2,1)}, u32[]{:S(2)}, u32[]{:S(2)}) collective-permute-start(bf16[256,512]{1,0:T(8,128)(2,1)} %get-tuple-element.105), channel_id=1, source_target_pairs={{0,8},{4,12},{8,16},{12,20},{16,24},{20,28},{24,0},{28,4},{1,9},{5... | collective-permute-start | bytes 786440 | tf_op jit(solution)/shard_map/ppermute | solution.py:241
  533.2 40.9 %collective-permute-start.115 = (bf16[64,2048]{1,0:T(8,128)(2,1)S(1)}, bf16[64,2048]{1,0:T(8,128)(2,1)S(1)}, u32[]{:S(2)}, u32[]{:S(2)}) collective-permute-start(bf16[64,2048]{1,0:T(8,128)(2,1)S(1)} %get-tuple-element.70), channel_id=1, source_target_pairs={{0,2},{1,3},{2,0},{3,1},{4,6},{5,7},{6,4},{7,5},{8,10},{9,11},{10,... | collective-permute-start | bytes 786440 | tf_op jit(solution)/shard_map/ppermute | solution.py:131
  537.7 23.9 %collective-permute-start.105 = (bf16[64,2048]{1,0:T(8,128)(2,1)S(1)}, bf16[64,2048]{1,0:T(8,128)(2,1)S(1)}, u32[]{:S(2)}, u32[]{:S(2)}) collective-permute-start(bf16[64,2048]{1,0:T(8,128)(2,1)S(1)} %get-tuple-element.80), channel_id=1, source_target_pairs={{0,2},{1,3},{2,0},{3,1},{4,6},{5,7},{6,4},{7,5},{8,10},{9,11},{10,... | collective-permute-start | bytes 786440 | tf_op jit(solution)/shard_map/ppermute | solution.py:131
  539.1 28.1 %collective-permute-start.107 = (bf16[64,2048]{1,0:T(8,128)(2,1)S(1)}, bf16[64,2048]{1,0:T(8,128)(2,1)S(1)}, u32[]{:S(2)}, u32[]{:S(2)}) collective-permute-start(bf16[64,2048]{1,0:T(8,128)(2,1)S(1)} %get-tuple-element.79), channel_id=1, source_target_pairs={{0,2},{1,3},{2,0},{3,1},{4,6},{5,7},{6,4},{7,5},{8,10},{9,11},{10,... | collective-permute-start | bytes 786440 | tf_op jit(solution)/shard_map/ppermute | solution.py:131
  544.7 28.1 %collective-permute-start.109 = (bf16[64,2048]{1,0:T(8,128)(2,1)S(1)}, bf16[64,2048]{1,0:T(8,128)(2,1)S(1)}, u32[]{:S(2)}, u32[]{:S(2)}) collective-permute-start(bf16[64,2048]{1,0:T(8,128)(2,1)S(1)} %get-tuple-element.78), channel_id=1, source_target_pairs={{0,2},{1,3},{2,0},{3,1},{4,6},{5,7},{6,4},{7,5},{8,10},{9,11},{10,... | collective-permute-start | bytes 786440 | tf_op jit(solution)/shard_map/ppermute | solution.py:131
  550.3 42.1 %collective-permute-start.104 = (bf16[64,2048]{1,0:T(8,128)(2,1)S(1)}, bf16[64,2048]{1,0:T(8,128)(2,1)S(1)}, u32[]{:S(2)}, u32[]{:S(2)}) collective-permute-start(bf16[64,2048]{1,0:T(8,128)(2,1)S(1)} %get-tuple-element.77), channel_id=1, source_target_pairs={{0,2},{1,3},{2,0},{3,1},{4,6},{5,7},{6,4},{7,5},{8,10},{9,11},{10,... | collective-permute-start | bytes 786440 | tf_op jit(solution)/shard_map/ppermute | solution.py:131
  561.6 21.4 %collective-permute-start.117 = (bf16[64,2048]{1,0:T(8,128)(2,1)S(1)}, bf16[64,2048]{1,0:T(8,128)(2,1)S(1)}, u32[]{:S(2)}, u32[]{:S(2)}) collective-permute-start(bf16[64,2048]{1,0:T(8,128)(2,1)S(1)} %get-tuple-element.74), channel_id=1, source_target_pairs={{0,16},{4,20},{8,24},{12,28},{16,0},{20,4},{24,8},{28,12},{1,17},{... | collective-permute-start | bytes 786440 | tf_op jit(solution)/shard_map/ppermute | solution.py:241
  574.2 29.5 %collective-permute-start.106 = (bf16[64,2048]{1,0:T(8,128)(2,1)S(1)}, bf16[64,2048]{1,0:T(8,128)(2,1)S(1)}, u32[]{:S(2)}, u32[]{:S(2)}) collective-permute-start(bf16[64,2048]{1,0:T(8,128)(2,1)S(1)} %get-tuple-element.81), channel_id=1, source_target_pairs={{0,16},{4,20},{8,24},{12,28},{16,0},{20,4},{24,8},{28,12},{1,17},{... | collective-permute-start | bytes 786440 | tf_op jit(solution)/shard_map/ppermute | solution.py:241
  592.5 25.4 %collective-permute-start.122 = (bf16[64,2048]{1,0:T(8,128)(2,1)}, bf16[64,2048]{1,0:T(8,128)(2,1)}, u32[]{:S(2)}, u32[]{:S(2)}) collective-permute-start(bf16[64,2048]{1,0:T(8,128)(2,1)} %get-tuple-element.57), channel_id=1, source_target_pairs={{0,1},{1,0},{2,3},{3,2},{4,5},{5,4},{6,7},{7,6},{8,9},{9,8},{10,11... | collective-permute-start | bytes 786440 | tf_op jit(solution)/shard_map/ppermute | solution.py:131
  592.5 24.8 %collective-permute-start.123 = (bf16[64,2048]{1,0:T(8,128)(2,1)}, bf16[64,2048]{1,0:T(8,128)(2,1)}, u32[]{:S(2)}, u32[]{:S(2)}) collective-permute-start(bf16[64,2048]{1,0:T(8,128)(2,1)} %get-tuple-element.57), channel_id=1, source_target_pairs={{0,2},{1,3},{2,0},{3,1},{4,6},{5,7},{6,4},{7,5},{8,10},{9,11},{10,... | collective-permute-start | bytes 786440 | tf_op jit(solution)/shard_map/ppermute | solution.py:131
  625.0 26.8 %collective-permute-start.125 = (f32[2,256]{1,0:T(2,128)}, f32[2,256]{1,0:T(2,128)}, u32[]{:S(2)}, u32[]{:S(2)}) collective-permute-start(f32[2,256]{1,0:T(2,128)} %pad_maximum_fusion.26), channel_id=1, source_target_pairs={{0,1},{1,0},{2,3},{3,2},{4,5},{5,4},{6,7},{7,6},{8,9},{9,8},{10,11... | collective-permute-start | bytes 6152 | tf_op jit(solution)/shard_map/ppermute | solution.py:131
  625.5 26.4 %collective-permute-start.126 = (f32[2,256]{1,0:T(2,128)}, f32[2,256]{1,0:T(2,128)}, u32[]{:S(2)}, u32[]{:S(2)}) collective-permute-start(f32[2,256]{1,0:T(2,128)} %pad_maximum_fusion.26), channel_id=1, source_target_pairs={{0,2},{1,3},{2,0},{3,1},{4,6},{5,7},{6,4},{7,5},{8,10},{9,11},{10,... | collective-permute-start | bytes 6152 | tf_op jit(solution)/shard_map/ppermute | solution.py:131
  626.2 25.7 %collective-permute-start.127 = (f32[2,256]{1,0:T(2,128)}, f32[2,256]{1,0:T(2,128)}, u32[]{:S(2)}, u32[]{:S(2)}) collective-permute-start(f32[2,256]{1,0:T(2,128)} %pad_maximum_fusion.26), channel_id=1, source_target_pairs={{0,3},{1,2},{2,1},{3,0},{4,7},{5,6},{6,5},{7,4},{8,11},{9,10},{10,... | collective-permute-start | bytes 6152 | tf_op jit(solution)/shard_map/ppermute | solution.py:131
  630.2 63.6 %collective-permute-start.168 = (bf16[128,512]{0,1:T(8,128)(2,1)}, bf16[128,512]{0,1:T(8,128)(2,1)}, u32[]{:S(2)}, u32[]{:S(2)}) collective-permute-start(bf16[128,512]{0,1:T(8,128)(2,1)} %bitcast.899), channel_id=1, source_target_pairs={{0,8},{8,16},{16,24},{24,28},{28,20},{20,12},{12,4},{4,0},{1,9},{9... | collective-permute-start | bytes 393224 | tf_op jit(solution)/shard_map/ppermute | solution.py:57
  646.9 49.7 %collective-permute-start.172 = (bf16[128,512]{0,1:T(8,128)(2,1)}, bf16[128,512]{0,1:T(8,128)(2,1)}, u32[]{:S(2)}, u32[]{:S(2)}) collective-permute-start(bf16[128,512]{0,1:T(8,128)(2,1)} %bitcast.288), channel_id=1, source_target_pairs={{8,0},{16,8},{24,16},{28,24},{20,28},{12,20},{4,12},{0,4},{9,1},{1... | collective-permute-start | bytes 393224 | tf_op jit(solution)/shard_map/ppermute | solution.py:57
  684.9 43.1 %collective-permute-start.128 = (bf16[128,2048]{1,0:T(8,128)(2,1)}, bf16[128,2048]{1,0:T(8,128)(2,1)}, u32[]{:S(2)}, u32[]{:S(2)}) collective-permute-start(bf16[128,2048]{1,0:T(8,128)(2,1)} %fusion.4), channel_id=1, source_target_pairs={{0,1},{1,0},{2,3},{3,2},{4,5},{5,4},{6,7},{7,6},{8,9},{9,8},{10,11... | collective-permute-start | bytes 1572872 | tf_op jit(solution)/shard_map/ppermute | solution.py:131
  703.8 36.2 %collective-permute-start.138 = (bf16[256,512]{1,0:T(8,128)(2,1)}, bf16[256,512]{1,0:T(8,128)(2,1)}, u32[]{:S(2)}, u32[]{:S(2)}) collective-permute-start(bf16[256,512]{1,0:T(8,128)(2,1)} %pad_maximum_fusion.11), channel_id=1, source_target_pairs={{8,0},{16,8},{24,16},{28,24},{20,28},{12,20},{4,12},{0,4},{9,1},{1... | collective-permute-start | bytes 786440 | tf_op jit(solution)/shard_map/ppermute | solution.py:57
  710.4 36.9 %collective-permute-start.146 = (bf16[256,512]{1,0:T(8,128)(2,1)S(1)}, bf16[256,512]{1,0:T(8,128)(2,1)}, u32[]{:S(2)}, u32[]{:S(2)}) collective-permute-start(bf16[256,512]{1,0:T(8,128)(2,1)S(1)} %pad_maximum_fusion.13), channel_id=1, source_target_pairs={{8,0},{16,8},{24,16},{28,24},{20,28},{12,20},{4,12},{0,4},{9,1},{1... | collective-permute-start | bytes 786440 | tf_op jit(solution)/shard_map/ppermute | solution.py:57
  721.6 48.9 %collective-permute-start.154 = (bf16[256,512]{1,0:T(8,128)(2,1)}, bf16[256,512]{1,0:T(8,128)(2,1)}, u32[]{:S(2)}, u32[]{:S(2)}) collective-permute-start(bf16[256,512]{1,0:T(8,128)(2,1)} %pad_maximum_fusion.15), channel_id=1, source_target_pairs={{8,0},{16,8},{24,16},{28,24},{20,28},{12,20},{4,12},{0,4},{9,1},{1... | collective-permute-start | bytes 786440 | tf_op jit(solution)/shard_map/ppermute | solution.py:57
  745.4 25.4 %collective-permute-start.151 = (bf16[256,512]{1,0:T(8,128)(2,1)}, bf16[256,512]{1,0:T(8,128)(2,1)}, u32[]{:S(2)}, u32[]{:S(2)}) collective-permute-start(bf16[256,512]{1,0:T(8,128)(2,1)} %fusion.63), channel_id=1, source_target_pairs={{0,8},{8,16},{16,24},{24,28},{28,20},{20,12},{12,4},{4,0},{1,9},{9... | collective-permute-start | bytes 786440 | tf_op jit(solution)/shard_map/ppermute | solution.py:57
  746.3 43.7 %collective-permute-start.171 = (bf16[256,512]{0,1:T(8,128)(2,1)S(1)}, bf16[256,512]{0,1:T(8,128)(2,1)S(1)}, u32[]{:S(2)}, u32[]{:S(2)}) collective-permute-start(bf16[256,512]{0,1:T(8,128)(2,1)S(1)} %fusion.58), channel_id=1, source_target_pairs={{0,8},{8,16},{16,24},{24,28},{28,20},{20,12},{12,4},{4,0},{1,9},{9... | collective-permute-start | bytes 786440 | tf_op jit(solution)/shard_map/ppermute | solution.py:57
  764.1 26.7 %collective-permute-start.175 = (bf16[256,512]{0,1:T(8,128)(2,1)S(1)}, bf16[256,512]{0,1:T(8,128)(2,1)S(1)}, u32[]{:S(2)}, u32[]{:S(2)}) collective-permute-start(bf16[256,512]{0,1:T(8,128)(2,1)S(1)} %fusion.56), channel_id=1, source_target_pairs={{8,0},{16,8},{24,16},{28,24},{20,28},{12,20},{4,12},{0,4},{9,1},{1... | collective-permute-start | bytes 786440 | tf_op jit(solution)/shard_map/ppermute | solution.py:57
  769.3 23.6 %collective-permute-start.139 = (bf16[256,512]{1,0:T(8,128)(2,1)}, bf16[256,512]{1,0:T(8,128)(2,1)}, u32[]{:S(2)}, u32[]{:S(2)}) collective-permute-start(bf16[256,512]{1,0:T(8,128)(2,1)} %get-tuple-element.119), channel_id=1, source_target_pairs={{8,0},{16,8},{24,16},{28,24},{20,28},{12,20},{4,12},{0,4},{9,1},{1... | collective-permute-start | bytes 786440 | tf_op jit(solution)/shard_map/ppermute | solution.py:57
  (295 other events, 4861.0 us)

commit v2 on v1

v2 whole, which is shorter than its diff:
```python
import functools
import math

import jax
import jax.numpy as jnp
import numpy as np
from jax import lax
from jax.experimental import pallas as pl
from jax.experimental.pallas import tpu as pltpu
from jax.sharding import PartitionSpec as P

HEADS = 32
FF = 8192
IMAGE = 64
GROUPS = 4

f32 = jnp.float32
bf16 = jnp.bfloat16
norm_eps = 1e-05


def pick(table, index):
    return lax.dynamic_index_in_dim(jnp.asarray(table, jnp.int32), index, keepdims=False)


def row_at(table, index):
    return lax.dynamic_index_in_dim(jnp.asarray(table, jnp.int32), index, keepdims=False)


def put(buffer, block, index):
    return lax.dynamic_update_slice(buffer, block[None], (index,) + (0,) * block.ndim)


def block_at(array, index, axis=0):
    return lax.dynamic_index_in_dim(array, index, axis, keepdims=False)


def after(value, *tokens):
    return lax.optimization_barrier((value,) + tokens)[0]


class Ring:
    def __init__(self, size, here):
        self.size = size
        self.here = here
        self.native = size > 8
        self.order = list(range(0, size, 2)) + list(range(size - 1, 0, -2))
        self.position = pick([self.order.index(i) for i in range(size)], here)
        self.forward = [(self.order[i], self.order[(i + 1) % size]) for i in range(size)]
        self.backward = [(b, a) for a, b in self.forward]

    def label(self, offset):
        return pick(self.order, (self.position + offset) % self.size)

    def labels(self, offsets):
        place = [self.order.index(i) for i in range(self.size)]
        return row_at(
            [[self.order[(place[i] + k) % self.size] for k in offsets] for i in range(self.size)],
            self.here,
        )

    def send(self, block, way):
        return lax.ppermute(block, "fsdp", self.forward if way > 0 else self.backward)

    def gather_parts(self, block):
        half = self.size // 2
        parts = [(0, block)]
        onward = backward = block
        for step in range(1, half):
            onward = self.send(onward, 1)
            backward = self.send(backward, -1)
            onward, backward = lax.optimization_barrier((onward, backward))
            parts += [(-step, onward), (step, backward)]
        cut = block.shape[0] // 2
        return parts, [self.send(onward[:cut], 1), self.send(backward[cut:], -1)]

    def gather(self, block):
        if self.native:
            full = lax.all_gather(block, "fsdp", axis=0)
            wide = full.reshape((8, self.size // 8, 4, -1, block.shape[1]))
            wide = wide.transpose(0, 2, 1, 3, 4).reshape(8, -1, block.shape[1])
            cut = wide.shape[1] // 2
            blocks = [wide[k] for k in range(8)]
            return blocks[:4] + [blocks[4][:cut], blocks[4][cut:]] + blocks[5:]
        parts, halves = self.gather_parts(block)
        parts = dict((offset % 8, part) for offset, part in parts)
        return [parts[k] for k in range(4)] + halves + [parts[k] for k in range(5, 8)]

    def scatter(self, part, stages):
        if self.native:
            for stage in stages:
                stage(part)
            return lax.psum_scatter(part, "fsdp", scatter_dimension=0, tiled=False).astype(f32)
        half = self.size // 2
        cut = part[half][0].shape[0]
        onward = self.send(part[half][0], 1)
        backward = self.send(part[half][1], -1)
        tokens = stages[0](part[half][0])
        for step in range(half - 1, 0, -1):
            onward, backward = after((onward, backward), *tokens)
            ahead = part[step].astype(f32)
            behind = part[self.size - step].astype(f32)
            if step == half - 1:
                ahead = jnp.concatenate([ahead[:cut] + onward.astype(f32), ahead[cut:]], axis=0)
                behind = jnp.concatenate(
                    [behind[:cut], behind[cut:] + backward.astype(f32)], axis=0
                )
            else:
                ahead = ahead + onward.astype(f32)
                behind = behind + backward.astype(f32)
            ahead, behind = ahead.astype(bf16), behind.astype(bf16)
            onward = self.send(ahead, 1)
            backward = self.send(behind, -1)
            tokens = stages[half - step](ahead)
        return part[0].astype(f32) + onward.astype(f32) + backward.astype(f32)


def tp_send(block, mask):
    return lax.ppermute(block, "tp", [(i, i ^ mask) for i in range(4)])


def tp_sum(values):
    return values + tp_send(values, 1) + tp_send(values, 2) + tp_send(values, 3)


def tp_rows_gather(piece, core, side):
    across = tp_send(piece, 2)
    blocks = [piece, tp_send(piece, 1), across, tp_send(across, 1)]
    blocks = [jnp.where(core == 1, blocks[i ^ 1], blocks[i]) for i in range(4)]
    blocks = [jnp.where(side == 1, blocks[i ^ 2], blocks[i]) for i in range(4)]
    return jnp.concatenate(blocks, axis=0)


def rotation_tables(count, row_width):
    position = np.arange(count, dtype=np.float32)[:, None]
    lane = np.arange(2 * row_width)[None, :]
    channel = (lane % row_width // 2).astype(np.float32)
    frequency = np.exp(-(2.0 * channel / row_width) * np.log(np.float32(10000.0)))
    angle = (position * frequency).astype(np.float32)
    zeta_base = (2.0 * channel + 0.4 * row_width) / (1.4 * row_width)
    growth = np.exp((position - count // 2) / 512.0 * np.log(zeta_base))
    cosine = np.cos(angle)
    sine = np.sin(angle) * np.where(lane % 2 == 0, -1.0, 1.0)
    tables = [cosine * growth, sine * growth, cosine / growth, sine / growth]
    return jnp.asarray(np.stack(tables).astype(np.float32))


def swapped(values):
    width = values.shape[1]
    lane = lax.broadcasted_iota(jnp.int32, values.shape, 1)
    return jnp.where(lane % 2 == 0, pltpu.roll(values, width - 1, 1), pltpu.roll(values, 1, 1))


def scores_of(query, key, limit, scale_value):
    raw = matmul(query, key, ((1,), (1,))) * scale_value
    row = lax.broadcasted_iota(jnp.int32, raw.shape, 0)
    column = lax.broadcasted_iota(jnp.int32, raw.shape, 1)
    scores = jnp.where((column <= row) & (column < limit), raw, -1e30)
    top = jnp.max(scores, axis=-1, keepdims=True)
    grown = jnp.exp(scores - top)
    return grown * (1.0 / jnp.sum(grown, axis=-1, keepdims=True))


def in_head(values, head, head_dim):
    lane = lax.broadcasted_iota(jnp.int32, values.shape, 1)
    return jnp.where(lane // head_dim == head, values, jnp.zeros_like(values))


def block_columns(labels, k, depth):
    return pl.ds(pl.multiple_of(labels[k] * depth, depth), depth)


def row_parts(rank, rows):
    core = lax.rem(rank, 2)
    return [
        [pl.ds(pl.multiple_of((2 * side + place) * rows, rows), rows) for side in range(2)]
        for place in (1 - core, core)
    ]


def attention_forward(labels, limits, x, *refs, slots, head_dim, scale):
    blocks, (bias, tables, q_out, k_out, v_out, o_out, sums) = refs[:9], refs[9:]
    depth = x.shape[1] // 8
    pairs = x.shape[0] // slots
    width = 2 * head_dim
    turned = []
    for c in range(3):
        total = bias[c : c + 1, :]
        for k in range(8):
            if k == 4:
                part = blocks[4 + c // 2][c % 2 * depth : (c % 2 + 1) * depth, :]
            else:
                part = blocks[k + k // 5][c * depth : (c + 1) * depth, :]
            total = total + matmul(x[:, block_columns(labels, k, depth)], part, ((1,), (0,)))
        turned.append(total)
    first = jnp.zeros((x.shape[0], 1), f32)
    square = jnp.zeros((x.shape[0], 1), f32)
    for j in range(q_out.shape[1] // width):
        lanes = slice(j * width, (j + 1) * width)
        for p in range(pairs):
            rows = slice(p * slots, (p + 1) * slots)
            q = turned[0][rows, lanes]
            q = q * tables[0] + swapped(q) * tables[1]
            k = turned[1][rows, lanes]
            k = (k * tables[2] + swapped(k) * tables[3]).astype(bf16)
            v = turned[2][rows, lanes].astype(bf16)
            q_out[rows, lanes] = q.astype(bf16)
            k_out[rows, lanes] = k
            v_out[rows, lanes] = v
            mixed = []
            for head in range(2):
                probs = scores_of(in_head(q, head, head_dim).astype(bf16), k, limits[p], scale)
                mixed.append(matmul(probs.astype(bf16), v, ((1,), (0,))))
            lane = lax.broadcasted_iota(jnp.int32, mixed[0].shape, 1)
            o_out[rows, lanes] = jnp.where(lane < head_dim, mixed[0], mixed[1])
    mixed = o_out[...]
    lane = lax.broadcasted_iota(jnp.int32, sums.shape, 1)
    partial = jnp.where(lane == 0, jnp.sum(mixed, axis=-1, keepdims=True), 0.0) + jnp.where(
        lane == 1, jnp.sum(mixed * mixed, axis=-1, keepdims=True), 0.0
    )

    @pl.when(pl.program_id(0) == 0)
    def _():
        sums[...] = partial

    @pl.when(pl.program_id(0) > 0)
    def _():
        sums[...] += partial


def attention_backward(
    limits, grad, mixed, coefficients, gain, tables, q_in, k_in, v_in, gq_out, gk_out, gv_out, sums, *, slots, head_dim, scale
):
    pairs = grad.shape[0] // slots
    width = 2 * head_dim
    mean, inverse = coefficients[:, 0:1], coefficients[:, 1:2]
    first, second = coefficients[:, 2:3], coefficients[:, 3:4]
    row = lax.broadcasted_iota(jnp.int32, (8, width), 0)
    for j in range(grad.shape[1] // width):
        lanes = slice(j * width, (j + 1) * width)
        total = jnp.zeros((8, width), f32)
        for p in range(pairs):
            rows = slice(p * slots, (p + 1) * slots)
            g = grad[rows, lanes]
            hat = (mixed[rows, lanes] - mean[rows]) * inverse[rows]
            total += jnp.where(row == 3, jnp.sum(g, axis=0, keepdims=True), 0.0)
            total += jnp.where(row == 4, jnp.sum(g * hat, axis=0, keepdims=True), 0.0)
            g = inverse[rows] * (g * gain[4:5, lanes] - first[rows] - hat * second[rows])
            q, k, v = q_in[rows, lanes].astype(f32), k_in[rows, lanes].astype(f32), v_in[rows, lanes]
            gq = jnp.zeros((slots, width), f32)
            gk = jnp.zeros((slots, width), f32)
            gv = jnp.zeros((slots, width), f32)
            for head in range(2):
                q_head = in_head(q, head, head_dim).astype(bf16)
                k_head = in_head(k, head, head_dim).astype(bf16)
                g_head = in_head(g, head, head_dim).astype(bf16)
                probs = scores_of(q_head, k_head, limits[p], scale)
                grad_probs = matmul(g_head, v, ((1,), (1,)))
                gv += matmul(probs.astype(bf16), g_head, ((0,), (0,)))
                spread = jnp.sum(probs * grad_probs, axis=-1, keepdims=True)
                grad_scores = (probs * (grad_probs - spread) * scale).astype(bf16)
                gq += matmul(grad_scores, k_head, ((1,), (0,)))
                gk += matmul(grad_scores, q_head, ((0,), (0,)))
            gq = (gq * tables[0] - swapped(gq) * tables[1]).astype(bf16)
            gk = (gk * tables[2] - swapped(gk) * tables[3]).astype(bf16)
            gv = gv.astype(bf16)
            gq_out[rows, lanes] = gq
            gk_out[rows, lanes] = gk
            gv_out[rows, lanes] = gv
            for index, part in enumerate((gq, gk, gv)):
                total += jnp.where(
                    row == index, jnp.sum(part.astype(f32), axis=0, keepdims=True), 0.0
                )
        sums[:, lanes] = total


def output_product(labels, rank, mixed, coefficients, gains, *refs):
    blocks, (away_out, kept_out, post_out) = refs[:8], refs[8:]
    depth = away_out.shape[1] // 8
    rows = away_out.shape[0] // 2
    hat = (mixed[...] - coefficients[:, 0:1]) * coefficients[:, 1:2]
    post_out[...] = (hat * gains[4:5, :] + gains[3:4, :]).astype(bf16)
    for out, slices in zip((away_out, kept_out), row_parts(rank[0], rows)):
        left = jnp.concatenate([post_out[part, :] for part in slices], axis=0)
        for k in range(8):
            product = matmul(left, blocks[k][...], ((1,), (1,)))
            out[:, block_columns(labels, k, depth)] = product.astype(out.dtype)


def output_back(labels, grad, mixed, coefficients, gains, *refs):
    blocks, (out, sums) = refs[:8], refs[8:]
    depth = grad.shape[1] // 8
    total = jnp.zeros(out.shape, f32)
    for k in range(8):
        total = total + matmul(
            grad[:, block_columns(labels, k, depth)], blocks[k][...], ((1,), (0,))
        )
    out[...] = total
    scaled = total * gains[4:5, :]
    hat = (mixed[...] - coefficients[:, 0:1]) * coefficients[:, 1:2]
    lane = lax.broadcasted_iota(jnp.int32, sums.shape, 1)
    sums[...] = jnp.where(lane == 0, jnp.sum(scaled, axis=-1, keepdims=True), 0.0) + jnp.where(
        lane == 1, jnp.sum(scaled * hat, axis=-1, keepdims=True), 0.0
    )


def projection_gradient(labels, x, grad, gq, gk, gv, post, out):
    depth = x.shape[1]
    for c, part in enumerate((gq, gk, gv)):
        out[0, c * depth : (c + 1) * depth, :] = matmul(x[...], part[...], ((0,), (0,))).astype(bf16)
    out[0, 3 * depth :, :] = matmul(grad[...], post[...], ((0,), (0,))).astype(bf16)


def projection_gradient_far(labels, x, grad, gq, gk, gv, post, first_out, second_out):
    depth = x.shape[1]
    first_out[:depth, :] = matmul(x[...], gq[...], ((0,), (0,))).astype(bf16)
    first_out[depth:, :] = matmul(x[...], gk[...], ((0,), (0,))).astype(bf16)
    second_out[:depth, :] = matmul(x[...], gv[...], ((0,), (0,))).astype(bf16)
    second_out[depth:, :] = matmul(grad[...], post[...], ((0,), (0,))).astype(bf16)


def projection_back(labels, rank, gq, gk, gv, *refs):
    blocks, (away_out, kept_out) = refs[:9], refs[9:]
    depth = away_out.shape[1] // 8
    rows = away_out.shape[0] // 2
    for out, slices in zip((away_out, kept_out), row_parts(rank[0], rows)):
        left = [
            jnp.concatenate([grad[part, :] for part in slices], axis=0) for grad in (gq, gk, gv)
        ]
        for k in range(8):
            total = jnp.zeros((2 * rows, depth), f32)
            for c in range(3):
                if k == 4:
                    part = blocks[4 + c // 2][c % 2 * depth : (c % 2 + 1) * depth, :]
                else:
                    part = blocks[k + k // 5][c * depth : (c + 1) * depth, :]
                total = total + matmul(left[c], part, ((1,), (1,)))
            out[:, block_columns(labels, k, depth)] = total.astype(out.dtype)


def columns_of(rows):
    return jnp.transpose(jnp.concatenate([rows] * 16, axis=0))


def ffn_forward(labels, x, g, vectors, *refs):
    blocks, (active_out, slope_out, grad_out, sums) = refs[:8], refs[8:]
    depth = x.shape[1] // 8
    before = vectors[0:1, :]
    grad = jnp.zeros(grad_out.shape, f32)
    for k in range(8):
        lanes = block_columns(labels, k, depth)
        before = before + matmul(x[:, lanes], blocks[k][:depth, :], ((1,), (0,)))
        grad = grad + matmul(g[:, lanes], blocks[k][depth:, :], ((1,), (0,)))
    below = 0.5 + 0.5 * lax.erf(before * math.sqrt(0.5))
    active = before * below
    active_out[...] = active
    slope_out[...] = below + before * (math.sqrt(0.5 / math.pi) * jnp.exp(-0.5 * before * before))
    grad_out[...] = grad
    scaled = grad * vectors[2:3, :]
    lane = lax.broadcasted_iota(jnp.int32, (grad.shape[0], 128), 1)
    columns = jnp.zeros((grad.shape[0], 128), f32)
    for index, values in enumerate((active, active * active, scaled, scaled * active)):
        columns += jnp.where(lane == index, jnp.sum(values, axis=-1, keepdims=True), 0.0)
    sums[...] = jnp.transpose(columns)[:8, :]


def ffn_backward(labels, sums, active, slope, grad, vectors, *refs, width):
    blocks, (before_out, post_out, out, totals) = refs[:8], refs[8:]
    columns = columns_of(sums[...])
    mean = columns[:, 0:1] / width
    inverse = lax.rsqrt(columns[:, 1:2] / width - mean * mean + norm_eps)
    hat_sum = inverse * (columns[:, 3:4] - mean * columns[:, 2:3])
    hat = (active[...] - mean) * inverse
    gain = vectors[2:3, :]
    post_out[...] = (hat * gain + vectors[1:2, :]).astype(bf16)
    moved = grad[...] * gain - columns[:, 2:3] / width - hat * (hat_sum / width)
    grad_before = (inverse * moved * slope[...]).astype(bf16)
    before_out[...] = grad_before
    product_into(labels, grad_before, blocks, out)
    row = lax.broadcasted_iota(jnp.int32, totals.shape, 0)
    partial = jnp.zeros(totals.shape, f32)
    for index, values in enumerate((grad_before.astype(f32), grad[...], grad[...] * hat)):
        partial += jnp.where(row == index, jnp.sum(values, axis=0, keepdims=True), 0.0)

    @pl.when(pl.program_id(0) == 0)
    def _():
        totals[...] = partial

    @pl.when(pl.program_id(0) > 0)
    def _():
        totals[...] += partial


def product_into(labels, left, blocks, out):
    depth = out.shape[1] // 8
    for k in range(8):
        product = matmul(left, blocks[k][...], ((1,), (1,)))
        out[:, block_columns(labels, k, depth)] = product.astype(bf16)


def ffn_product(labels, left, *refs):
    product_into(labels, left[...], refs[:8], refs[8])


def ffn_gradient(labels, near_x, far_x, near_g, far_g, near_before, far_before, near_post, far_post, *outs):
    depth = near_x.shape[1]
    totals = []
    for c, (near, far, near_right, far_right) in enumerate(
        ((near_x, far_x, near_before, far_before), (near_g, far_g, near_post, far_post))
    ):
        total = matmul(near[...], near_right[...], ((0,), (0,)))
        total = total + matmul(far[...], far_right[...], ((0,), (0,)))
        totals.append(total.astype(bf16))
    for k, out in enumerate(outs):

        @pl.when(pl.program_id(0) == k)
        def _(out=out):
            for c, total in enumerate(totals):
                out[c * depth : (c + 1) * depth, :] = total


def ffn_placed(groups, *refs):
    blocks, (first_out, second_out) = refs[:4], refs[4:]
    depth, width = blocks[0].shape[0] // 2, blocks[0].shape[1]
    for k in range(4):
        place = pl.ds(pl.multiple_of(groups[k] * width, width), width)
        first_out[:, place] = blocks[k][:depth, :].astype(f32)
        second_out[place, :] = jnp.transpose(blocks[k][depth:, :].astype(f32))


def cost(flops, moved, exponentials=0):
    return pl.CostEstimate(flops=flops, bytes_accessed=moved, transcendentals=exponentials)


def norm_stats(first_sum, square_sum, row_width):
    mean_value = first_sum / row_width
    variance = square_sum / row_width - mean_value * mean_value
    return mean_value, lax.rsqrt(variance + norm_eps)


def norm_rows(values, gain_vector, shift_vector):
    width = values.shape[-1]
    mean_value, inverse = norm_stats(
        jnp.sum(values, axis=-1, keepdims=True),
        jnp.sum(values * values, axis=-1, keepdims=True),
        width,
    )
    hat = (values - mean_value) * inverse
    return hat * gain_vector + shift_vector, hat, inverse


def norm_back_rows(scaled, hat, inverse):
    width = scaled.shape[-1]
    return inverse * (
        scaled
        - jnp.sum(scaled, axis=-1, keepdims=True) / width
        - hat * jnp.sum(scaled * hat, axis=-1, keepdims=True) / width
    )


def matmul(a, b, dims):
    return lax.dot_general(a, b, (dims, ((), ())), preferred_element_type=f32)


def per_device(
    tokens,
    cotangent,
    caption_lengths,
    w_qkv,
    head_biases,
    head_gain,
    w_out,
    model_gains,
    model_biases,
    w_fc1,
    w_fc2,
    ffn_gain,
    ffn_biases,
    *,
    fsdp_size,
):
    here = lax.axis_index("fsdp")
    rank = lax.axis_index("tp")
    core, side = rank % 2, rank // 2
    others = fsdp_size // GROUPS
    group, member = here // others, here % others
    ring = Ring(fsdp_size, here)
    group_lists = [[g * others + o for g in range(GROUPS)] for o in range(others)]
    member_lists = [[g * others + o for o in range(others)] for g in range(GROUPS)]

    def group_send(block, shift):
        return lax.ppermute(
            block,
            "fsdp",
            [
                (g * others + o, (g + shift) % GROUPS * others + o)
                for g in range(GROUPS)
                for o in range(others)
            ],
        )

    def group_swap(blocks):
        return lax.all_to_all(blocks, "fsdp", 0, 0, axis_index_groups=group_lists)

    def pair_send(block):
        return lax.ppermute(block, "fsdp", [(f, f ^ 1) for f in range(fsdp_size)])

    def member_gather(blocks):
        if others == 2:
            theirs = pair_send(blocks)
            return jnp.stack(
                [jnp.where(member == 0, blocks, theirs), jnp.where(member == 0, theirs, blocks)],
                axis=1,
            )
        full = lax.all_gather(blocks, "fsdp", axis=0, axis_index_groups=member_lists)
        return jnp.moveaxis(full, 0, 1)

    def member_scatter(blocks):
        if others == 2:
            sent = pair_send(block_at(blocks, 1 - member, 1))
            return block_at(blocks, member, 1).astype(f32) + sent.astype(f32)
        return lax.psum_scatter(
            blocks, "fsdp", scatter_dimension=1, axis_index_groups=member_lists, tiled=False
        ).astype(f32)

    pair_count = caption_lengths.shape[0]
    row_count, model_width = tokens.shape
    slot_count = row_count // pair_count
    sub_rows = row_count // 4
    head_dim = model_width // HEADS
    local_width = w_qkv.shape[2]
    block_rows = w_qkv.shape[0]
    hidden_width = FF
    local_hidden = w_fc1.shape[1] // GROUPS

    model_part = jnp.concatenate([model_gains, model_biases], axis=0)
    head_part = jnp.concatenate([head_biases, head_gain[None]], axis=0)
    unit_part = jnp.concatenate([ffn_biases, ffn_gain[None]], axis=0)
    packed = jnp.concatenate([model_part.reshape(-1), head_part.reshape(-1), unit_part.reshape(-1)])
    vectors = lax.all_to_all(
        jnp.broadcast_to(packed[None], (fsdp_size, packed.shape[0])), "fsdp", 0, 0
    )
    sizes = [model_part.size, head_part.size, unit_part.size]
    model_vectors = (
        vectors[:, : sizes[0]].reshape((fsdp_size,) + model_part.shape).transpose(1, 0, 2)
    ).reshape(6, model_width).astype(f32)
    head_vectors = (
        vectors[:, sizes[0] : sizes[0] + sizes[1]]
        .reshape((fsdp_size,) + head_part.shape)
        .transpose(1, 0, 2)
    ).reshape(5, local_width).astype(f32)
    unit_all = vectors[:, sizes[0] + sizes[1] :].reshape((GROUPS, others) + unit_part.shape)
    unit_vectors = block_at(unit_all, group).transpose(1, 0, 2).reshape(3, local_hidden).astype(f32)

    def rows_gather(piece, *tokens):
        pieces = [piece] + [group_send(piece, shift) for shift in range(1, GROUPS)]
        across = [tp_send(piece, 2)]
        pieces[1] = after(pieces[1], across[0])
        across += [tp_send(part, 2) for part in pieces[1:]]
        near = after(jnp.concatenate(pieces + across, axis=0), *tokens)
        return near, tp_send(near, 1)

    def core_sum(away, kept):
        return (kept + tp_send(away, 1).astype(f32)).reshape(2, sub_rows, -1)

    def side_sum(total):
        crossing = tp_send(block_at(total, 1 - side).astype(bf16), 2)
        return block_at(total, side) + crossing.astype(f32)

    def group_core(far, near):
        total = near.astype(f32) + tp_send(far, 1).astype(f32)
        return total.reshape(2, GROUPS, sub_rows, -1)

    def group_shares(total):
        return total[0] + tp_send(total[1].astype(bf16), 2).astype(f32)

    def group_shares_piped(total):
        return {k: total[0, k] + tp_send(total[1, k].astype(bf16), 2).astype(f32) for k in (2, 1, 3, 0)}

    def group_total(shares):
        sent = [group_send(shares[k].astype(bf16), -k).astype(f32) for k in (2, 1, 3)]
        return shares[0], sent

    def group_sum(values):
        def swap(array, width):
            pieces = [array[:, i : i + width] for i in range(0, array.shape[1], width)]
            pieces = [pieces[i ^ 1] for i in range(len(pieces))]
            return jnp.concatenate(pieces, axis=1)

        half_rows = 2 * GROUPS * sub_rows
        flip_core = tp_send(values, 1)
        flip_side = tp_send(values, 2)
        flip_both = tp_send(values, 3)
        values = values + swap(flip_core + swap(flip_both, half_rows // 2), half_rows)
        values = values + swap(flip_side, half_rows // 2)
        total = values
        for shift in range(1, GROUPS):
            part = group_send(values, shift).reshape(8, 4, GROUPS * sub_rows)
            cut = (GROUPS - shift) * sub_rows
            part = jnp.concatenate([part[:, :, cut:], part[:, :, :cut]], axis=2)
            total = total + part.reshape(8, -1)
        return total

    def my_rows(array):
        return lax.dynamic_slice_in_dim(array, rank * sub_rows, sub_rows, 0)

    slot_index = jnp.arange(slot_count)[None, :]
    key_valid = slot_index < IMAGE + caption_lengths[:, None]
    keep_rows = key_valid.reshape(row_count).astype(f32)[:, None]
    my_keep = my_rows(keep_rows)
    my_grad_out = my_rows(cotangent).astype(f32) * my_keep
    depth = model_width // 8
    own_block = jnp.concatenate([w_qkv[:, c] for c in range(3)] + [w_out.T], axis=0)
    blocks = ring.gather(own_block)
    labels = jnp.arange(8, dtype=jnp.int32) if ring.native else ring.labels(range(8))

    fc_pieces = jnp.concatenate(
        [w.reshape(block_rows, GROUPS, local_hidden) for w in (w_fc1, w_fc2.T)], axis=0
    )
    fc_pieces = after(fc_pieces.transpose(1, 0, 2), blocks[3])
    fc_mine = [block_at(fc_pieces, group)]
    for shift in (1, 3, 2):
        fc_mine.append(group_send(block_at(fc_pieces, (group + shift) % GROUPS), shift))
    fc_received = list(fc_mine)
    if others == 2:
        fc_theirs = [pair_send(part) for part in fc_mine]
        fc_labels = row_at(
            [
                [(f // 2 - k) % GROUPS * 2 + f % 2 for k in (0, 1, 3, 2)]
                + [(f // 2 - k) % GROUPS * 2 + 1 - f % 2 for k in (0, 1, 3, 2)]
                for f in range(fsdp_size)
            ],
            here,
        )
    else:
        full = jnp.zeros(fc_pieces.shape, bf16)
        for shift, part in zip((0, 1, 3, 2), fc_mine):
            full = put(full, part, (group - shift) % GROUPS)
        full = lax.all_gather(full, "fsdp", axis=0, axis_index_groups=member_lists)
        full = full.reshape(others, GROUPS, 2, block_rows, local_hidden).transpose(2, 1, 0, 3, 4)
        full = full.reshape(2, 8, depth, local_hidden).transpose(1, 0, 2, 3)
        full = full.reshape(8, 2 * depth, local_hidden)
        fc_mine, fc_theirs = [full[k] for k in range(4)], [full[k] for k in range(4, 8)]
        fc_labels = jnp.arange(8)
    fc_labels = fc_labels.astype(jnp.int32)
    fc_blocks = fc_mine + fc_theirs
    cotangent_rows = after(my_grad_out.astype(bf16), fc_received[3])
    cotangent_rows = [cotangent_rows] + [
        group_send(cotangent_rows, shift) for shift in range(1, GROUPS)
    ]

    tables = rotation_tables(slot_count, head_dim)
    limits = IMAGE + caption_lengths
    scale_value = 1.0 / math.sqrt(head_dim)
    normed_in, _, _ = norm_rows(tokens.astype(f32), model_vectors[0], model_vectors[2])
    normed_in_b = normed_in.astype(bf16)
    part_width = 4 * head_dim
    parts = local_width // part_width
    scalars = pl.BlockSpec(memory_space=pltpu.SMEM)

    def whole(shape, first=0):
        return pl.BlockSpec(shape, lambda j: (first,) + (0,) * (len(shape) - 1))

    def columns(rows):
        return pl.BlockSpec((rows, part_width), lambda j: (0, j))

    def projection_specs(width, index_map):
        full = pl.BlockSpec((3 * depth, width), index_map)
        return [full] * 4 + [pl.BlockSpec((2 * depth, width), index_map)] * 2 + [full] * 3

    out_row = whole((depth, local_width), 3)
    out_specs = [out_row] * 4 + [whole((depth, local_width), 1)] + [out_row] * 3
    out_blocks = blocks[:4] + blocks[5:]
    rank_array = rank.astype(jnp.int32)[None]
    big = pltpu.CompilerParams(vmem_limit_bytes=58 << 20)
    queries, keys_rot, values_in, heads_out, head_sums = pl.pallas_call(
        functools.partial(
            attention_forward, slots=slot_count, head_dim=head_dim, scale=scale_value
        ),
        grid=(parts,),
        in_specs=[scalars, scalars, whole((row_count, model_width))]
        + projection_specs(part_width, lambda j: (0, j))
        + [columns(5), whole((4, slot_count, 2 * head_dim))],
        out_specs=[columns(row_count)] * 4 + [whole((row_count, 128))],
        out_shape=[jax.ShapeDtypeStruct((row_count, local_width), bf16)] * 3
        + [
            jax.ShapeDtypeStruct((row_count, local_width), f32),
            jax.ShapeDtypeStruct((row_count, 128), f32),
        ],
        compiler_params=big,
        cost_estimate=cost(2 * row_count * model_width * 3 * local_width, 12 << 20, 1 << 20),
        name="attention_forward",
    )(labels, limits, normed_in_b, *blocks, head_vectors, tables)
    head_stats = tp_sum(head_sums[:, :2].T)
    mean_attn, inverse_attn = norm_stats(
        head_stats[0][:, None], head_stats[1][:, None], model_width
    )
    coefficients = jnp.concatenate([mean_attn, inverse_attn], axis=1)
    halves = [
        jax.ShapeDtypeStruct((2 * sub_rows, model_width), bf16),
        jax.ShapeDtypeStruct((2 * sub_rows, model_width), f32),
    ]
    half_specs = [whole((2 * sub_rows, model_width))] * 2
    away, kept, post_attn_b = pl.pallas_call(
        output_product,
        grid=(1,),
        in_specs=[
            scalars,
            scalars,
            whole((row_count, local_width)),
            whole((row_count, 2)),
            whole((5, local_width)),
        ]
        + out_specs,
        out_specs=half_specs + [whole((row_count, local_width))],
        out_shape=halves + [jax.ShapeDtypeStruct((row_count, local_width), bf16)],
        compiler_params=big,
        cost_estimate=cost(2 * row_count * model_width * local_width, 5 << 20),
        name="output_product",
    )(labels, rank_array, after(heads_out, *fc_received[1:], fc_theirs[0]), coefficients, head_vectors, *out_blocks)
    branch = side_sum(core_sum(away, kept))
    middle = my_rows(tokens).astype(f32) + branch + model_vectors[4]
    normed_mid, hat_mid, inverse_mid = norm_rows(middle, model_vectors[1], model_vectors[3])

    cotangent_near = after(jnp.concatenate(cotangent_rows, axis=0), branch)
    cotangent_near = jnp.concatenate([cotangent_near, tp_send(cotangent_near, 2)], axis=0)
    grad_out_all = (cotangent_near, tp_send(cotangent_near, 1))
    normed_mid_all = rows_gather(
        after(normed_mid.astype(bf16), *cotangent_rows), *fc_theirs[1:]
    )
    half_rows = 2 * GROUPS * sub_rows
    step_rows = half_rows // 2

    def rows(width):
        return pl.BlockSpec((step_rows, width), lambda j: (j, 0))

    fc_half = [[whole((depth, local_hidden), start)] * 8 for start in range(2)]
    half_shape = jax.ShapeDtypeStruct((half_rows, local_hidden), f32)
    half_shape_b = jax.ShapeDtypeStruct((half_rows, local_hidden), bf16)
    product_shape = jax.ShapeDtypeStruct((half_rows, model_width), bf16)

    def forward_half(x, g):
        return pl.pallas_call(
            ffn_forward,
            grid=(2,),
            in_specs=[scalars, rows(model_width), rows(model_width), whole((3, local_hidden))]
            + [whole((2 * depth, local_hidden))] * 8,
            out_specs=[rows(local_hidden)] * 3 + [pl.BlockSpec((8, step_rows), lambda j: (0, j))],
            out_shape=[half_shape] * 3 + [jax.ShapeDtypeStruct((8, half_rows), f32)],
            compiler_params=big,
            cost_estimate=cost(4 * half_rows * model_width * local_hidden, 10 << 20, 1 << 20),
            name="ffn_forward",
        )(fc_labels, x, g, unit_vectors, *fc_blocks)

    *hidden_near, sums_near = forward_half(normed_mid_all[0], grad_out_all[0])
    *hidden_far, sums_far = forward_half(normed_mid_all[1], grad_out_all[1])
    sums = group_sum(jnp.concatenate([sums_near, sums_far], axis=1))

    def backward_half(index, hidden):
        return pl.pallas_call(
            functools.partial(ffn_backward, width=hidden_width),
            grid=(2,),
            in_specs=[scalars, pl.BlockSpec((8, step_rows), lambda j: (0, j + 2 * index))]
            + [rows(local_hidden)] * 3
            + [whole((3, local_hidden))]
            + fc_half[0],
            out_specs=[rows(local_hidden)] * 2 + [rows(model_width), whole((8, local_hidden))],
            out_shape=[half_shape_b] * 2
            + [product_shape, jax.ShapeDtypeStruct((8, local_hidden), f32)],
            compiler_params=big,
            cost_estimate=cost(2 * half_rows * model_width * local_hidden, 8 << 20),
            name="ffn_backward",
        )(fc_labels, sums, *hidden, unit_vectors, *fc_blocks)

    before_far, post_far, mid_far, totals_far = backward_half(1, hidden_far)
    before_near, post_near, mid_near, totals_near = backward_half(0, hidden_near)

    def second_half(post):
        return pl.pallas_call(
            ffn_product,
            grid=(2,),
            in_specs=[scalars, rows(local_hidden)] + fc_half[1],
            out_specs=rows(model_width),
            out_shape=product_shape,
            compiler_params=big,
            cost_estimate=cost(2 * half_rows * model_width * local_hidden, 5 << 20),
            name="ffn_product",
        )(fc_labels, post, *fc_blocks)

    mid_total = group_core(mid_far, mid_near)
    shares = group_shares_piped(mid_total)
    unit_s = member_scatter((totals_near + totals_far)[:3].reshape(3, others, -1))

    fc_order = (2, 1, 3, 0)

    def fc_gradient(order, token):
        return pl.pallas_call(
            ffn_gradient,
            grid_spec=pltpu.PrefetchScalarGridSpec(
                num_scalar_prefetch=1,
                grid=(4,),
                in_specs=[pl.BlockSpec((half_rows, depth), lambda j, label: (0, label[j]))] * 4
                + [pl.BlockSpec((half_rows, local_hidden), lambda j, label: (0, 0))] * 4,
                out_specs=[pl.BlockSpec((2 * depth, local_hidden), lambda j, label: (0, 0))] * 4,
            ),
            out_shape=[jax.ShapeDtypeStruct((2 * depth, local_hidden), bf16)] * 4,
            compiler_params=big,
            cost_estimate=cost(4 * half_rows * model_width * local_hidden, 9 << 20),
            name="ffn_gradient",
        )(
            order.astype(jnp.int32),
            *normed_mid_all,
            *grad_out_all,
            before_near,
            before_far,
            *after((post_near, post_far), token),
        )

    if others == 2:
        ahead = [[(f // 2 + k) % GROUPS * 2 for k in fc_order] for f in range(fsdp_size)]
        away_labels = row_at([[a + 1 - f % 2 for a in row] for f, row in enumerate(ahead)], here)
        kept_labels = row_at([[a + f % 2 for a in row] for f, row in enumerate(ahead)], here)
        fc_away = fc_gradient(away_labels, mid_total)
        fc_kept = fc_gradient(kept_labels, shares[2])
        fc_sent = [pair_send(part) for part in fc_away]
        fc_summed = [
            (kept.astype(f32) + sent.astype(f32)).astype(bf16)
            for kept, sent in zip(fc_kept, fc_sent)
        ]
    else:
        fc_away = fc_gradient(jnp.arange(4), mid_total)
        fc_kept = fc_gradient(jnp.arange(4, 8), shares[2])
        fc_grads = jnp.stack(fc_away + fc_kept)
        fc_grads = fc_grads.reshape(8, 2, depth, local_hidden).transpose(1, 0, 2, 3)
        fc_grads = fc_grads.reshape(2, GROUPS, others, block_rows, local_hidden)
        fc_grads = fc_grads.transpose(1, 2, 0, 3, 4).reshape(GROUPS, others, -1, local_hidden)
        fc_grads = member_scatter(fc_grads).astype(bf16)
        fc_summed = [block_at(fc_grads, (group + shift) % GROUPS) for shift in fc_order]
        fc_sent = fc_summed

    shares[1], shares[3] = after((shares[1], shares[3]), *fc_away)
    own, sent = group_total(shares)
    own = after(own, fc_kept[0], *fc_sent[:3], unit_s)
    grad_mid_normed = own + sent[0] + sent[1] + sent[2]
    grad_middle = my_grad_out + norm_back_rows(
        grad_mid_normed * model_vectors[1], hat_mid, inverse_mid
    )
    grad_middle_b = tp_rows_gather(grad_middle.astype(bf16), core, side)
    fc_spread = [group_send(part, k) if k else part for k, part in zip(fc_order, fc_summed)]

    grad_post_attn, back_sums = pl.pallas_call(
        output_back,
        grid=(1,),
        in_specs=[
            scalars,
            whole((row_count, model_width)),
            whole((row_count, local_width)),
            whole((row_count, 2)),
            whole((5, local_width)),
        ]
        + out_specs,
        out_specs=[whole((row_count, local_width)), whole((row_count, 128))],
        out_shape=[
            jax.ShapeDtypeStruct((row_count, local_width), f32),
            jax.ShapeDtypeStruct((row_count, 128), f32),
        ],
        compiler_params=big,
        cost_estimate=cost(2 * row_count * model_width * local_width, 5 << 20),
        name="output_back",
    )(labels, after(grad_middle_b, fc_sent[3]), heads_out, coefficients, head_vectors, *out_blocks)
    head_back = tp_sum(back_sums[:, :2].T)[:, :, None]
    coefficients = jnp.concatenate(
        [coefficients, head_back[0] / model_width, head_back[1] / model_width], axis=1
    )
    *grad_linear, head_sums_back = pl.pallas_call(
        functools.partial(
            attention_backward, slots=slot_count, head_dim=head_dim, scale=scale_value
        ),
        grid=(parts,),
        in_specs=[
            scalars,
            columns(row_count),
            columns(row_count),
            whole((row_count, 4)),
            columns(5),
            whole((4, slot_count, 2 * head_dim)),
            columns(row_count),
            columns(row_count),
            columns(row_count),
        ],
        out_specs=[columns(row_count)] * 3 + [columns(8)],
        out_shape=[jax.ShapeDtypeStruct((row_count, local_width), bf16)] * 3
        + [jax.ShapeDtypeStruct((8, local_width), f32)],
        compiler_params=pltpu.CompilerParams(vmem_limit_bytes=40 << 20),
        cost_estimate=cost(10 * row_count * slot_count * 2 * local_width, 4 << 20, 1 << 20),
        name="attention_backward",
    )(
        limits,
        after(grad_post_attn, fc_spread[0]),
        heads_out,
        coefficients,
        head_vectors,
        tables,
        queries,
        keys_rot,
        values_in,
    )
    def weight_gradients(kernel, count, order, out_specs, out_shape):
        return pl.pallas_call(
            kernel,
            grid_spec=pltpu.PrefetchScalarGridSpec(
                num_scalar_prefetch=1,
                grid=(count,),
                in_specs=[pl.BlockSpec((row_count, depth), lambda j, label: (0, label[j]))] * 2
                + [pl.BlockSpec((row_count, local_width), lambda j, label: (0, 0))] * 4,
                out_specs=out_specs,
            ),
            out_shape=out_shape,
            compiler_params=big,
            cost_estimate=cost(count * row_count * depth * 8 * local_width, count << 20),
            name=kernel.__name__,
        )(order, normed_in_b, grad_middle_b, *grad_linear, post_attn_b)

    far_grads = weight_gradients(
        projection_gradient_far,
        1,
        labels[4:5],
        [pl.BlockSpec((2 * depth, local_width), lambda j, label: (0, 0))] * 2,
        [jax.ShapeDtypeStruct((2 * depth, local_width), bf16)] * 2,
    )
    order = [0, 3, 5, 2, 6, 1, 7]
    weight_grads = weight_gradients(
        projection_gradient,
        7,
        jnp.asarray(order, jnp.int32) if ring.native else ring.labels(order),
        pl.BlockSpec((1, 4 * depth, local_width), lambda j, label: (j, 0, 0)),
        jax.ShapeDtypeStruct((7, 4 * depth, local_width), bf16),
    )
    weight_grads = dict((k, weight_grads[j]) for j, k in enumerate(order))
    weight_grads[4] = far_grads
    if ring.native:
        weight_grads[4] = jnp.concatenate(far_grads, axis=0)
        weight_grads = jnp.stack([weight_grads[k] for k in range(8)])
        weight_grads = weight_grads.reshape(8, 4, fsdp_size // 8, block_rows, local_width)
        weight_grads = weight_grads.transpose(0, 2, 1, 3, 4).reshape(fsdp_size, -1, local_width)
    placed_rows = (block_rows, GROUPS * local_hidden)
    def place_ffn(token):
        return pl.pallas_call(
            ffn_placed,
            grid=(1,),
            in_specs=[scalars] + [whole((2 * block_rows, local_hidden))] * 4,
            out_specs=[whole(placed_rows), whole(placed_rows[::-1])],
            out_shape=[
                jax.ShapeDtypeStruct(placed_rows, f32),
                jax.ShapeDtypeStruct(placed_rows[::-1], f32),
            ],
            compiler_params=big,
            cost_estimate=cost(0, 6 << 20),
            name="ffn_placed",
        )(
            row_at([[(f // others - k) % GROUPS for k in fc_order] for f in range(fsdp_size)], here),
            *after(tuple(fc_spread), token),
        )

    results = {}

    def while_half(token):
        results["parts"] = [second_half(after(post, token)) for post in (post_far, post_near)]
        return fc_spread + results["parts"]

    def while_first(token):
        back_away, back_kept = pl.pallas_call(
            projection_back,
            grid=(1,),
            in_specs=[scalars, scalars]
            + [whole((row_count, local_width))] * 3
            + projection_specs(local_width, lambda j: (0, 0)),
            out_specs=half_specs,
            out_shape=halves,
            compiler_params=big,
            cost_estimate=cost(2 * row_count * model_width * 3 * local_width, 10 << 20),
            name="projection_back",
        )(labels, rank_array, *after(tuple(grad_linear), token), *blocks)
        results["back"] = back_away, back_kept
        results["core"] = group_core(*after(tuple(results["parts"]), token))
        return back_away, back_kept, results["core"]

    def while_second(token):
        grad_in_normed = side_sum(core_sum(*after(results["back"], token)))
        _, hat_in, inverse_in = norm_rows(
            my_rows(tokens).astype(f32), model_vectors[0], model_vectors[2]
        )
        grad_token_rows = grad_middle + norm_back_rows(
            grad_in_normed * model_vectors[0], hat_in, inverse_in
        )
        results["model"] = tp_sum(
            jnp.stack(
                [
                    jnp.sum(grad_in_normed * hat_in, axis=0),
                    jnp.sum(grad_mid_normed * hat_mid, axis=0),
                    jnp.sum(grad_in_normed, axis=0),
                    jnp.sum(grad_mid_normed, axis=0),
                    jnp.sum(grad_middle, axis=0),
                    jnp.sum(my_grad_out, axis=0),
                ]
            )
        )
        results["shares"] = group_shares(after(results["core"], token))
        results["tokens"] = grad_token_rows
        results["placed"] = place_ffn(token)
        return [results["model"], results["tokens"], results["shares"]] + list(results["placed"])

    def by_block(vectors_in, blocks_in):
        return vectors_in.reshape(vectors_in.shape[0], blocks_in, -1).transpose(1, 0, 2)

    def while_third(token):
        model_grads, token_rows, shares = after(
            (results["model"], results["tokens"], results["shares"]), token
        )
        model_blocks = by_block(model_grads, fsdp_size).reshape(fsdp_size, -1)
        head_blocks = by_block(head_sums_back[:5], fsdp_size).reshape(fsdp_size, -1)
        joined = jnp.concatenate([model_blocks, head_blocks], axis=1)
        joined_s = jnp.sum(lax.all_to_all(joined, "fsdp", 0, 0), axis=0)
        results["model_s"] = joined_s[: model_blocks.shape[1]].reshape(6, -1)
        results["head_s"] = joined_s[model_blocks.shape[1] :].reshape(5, -1)
        results["grad_tokens"] = tp_rows_gather(token_rows, core, side)
        own, sent = group_total(shares)
        own = after(own, joined_s, results["grad_tokens"])
        second = own + sent[0] + sent[1] + sent[2]
        out_rows = ((middle + second + model_vectors[5]) * my_keep).astype(bf16)
        results["layer_out"] = tp_rows_gather(out_rows, core, side)
        return ()

    weights_s = ring.scatter(weight_grads, [while_half, while_first, while_second, while_third])
    weights_s = weights_s.reshape(4, block_rows, local_width)
    grad_qkv_s = weights_s[:3].transpose(1, 0, 2)
    grad_out_s = weights_s[3]
    return (
        results["layer_out"],
        results["grad_tokens"],
        grad_qkv_s,
        results["head_s"][:4],
        results["head_s"][4],
        grad_out_s.T,
        results["model_s"][:2],
        results["model_s"][2:],
        *results["placed"],
        unit_s[2],
        unit_s[:2],
    )


def solution(mesh):
    placed = (
        P("fsdp", None),
        P("fsdp", None),
        P("fsdp"),
        P("fsdp", None, "tp"),
        P(None, ("tp", "fsdp")),
        P(("tp", "fsdp")),
        P("tp", "fsdp"),
        P(None, "fsdp"),
        P(None, "fsdp"),
        P("fsdp", "tp"),
        P("tp", "fsdp"),
        P(("tp", "fsdp")),
        P(None, ("tp", "fsdp")),
    )
    return jax.shard_map(
        functools.partial(per_device, fsdp_size=mesh.shape["fsdp"]),
        mesh=mesh,
        in_specs=placed,
        out_specs=(
            P("fsdp", None),
            P("fsdp", None),
            P("fsdp", None, "tp"),
            P(None, ("tp", "fsdp")),
            P(("tp", "fsdp")),
            P("tp", "fsdp"),
            P(None, "fsdp"),
            P(None, "fsdp"),
            P("fsdp", "tp"),
            P("tp", "fsdp"),
            P(("tp", "fsdp")),
            P(None, ("tp", "fsdp")),
        ),
        check_vma=False,
    )
```

time: 836 us -> 554 us (0.66)
  local copies, waits for them, and re-layouts: 199 us -> 44 us
  starting transfers between devices: 246 us -> 112 us
  Pallas kernels: 0 us -> 98.9 us
  matrix products: 65.4 us -> 0 us
  between operations: 28.5 us -> 2.2 us
  waiting for transfers between devices: 206 us -> 230 us
  other arithmetic: 79.4 us -> 56.6 us
    ppermute x114 -> x16, starting transfers between devices: 139 us -> 18.1 us  [send(): lax.ppermute(block, 'fsdp', self.forward if way > 0 else self.backward)]
    pallas_call x0 -> x16, Pallas kernels: none -> 98.9 us  [the longest x2 15.6 us: fc_gradient(): pl.pallas_call(ffn_gradient, grid_spec=pltpu.PrefetchScalarGridSpec(num_s...]
    dot_general x26 -> x0, matrix products: 65.4 us -> none  [the longest x20 56.6 us: matmul(): return lax.dot_general(a, b, (dims, ((), ())), preferred_element_type=f32)]
    dynamic_update_slice x91 -> x0, local copies, waits for them, and re-layouts: 50.1 us -> none  [put(): lax.dynamic_update_slice(buffer, block[None], (index,) + (0,) * block.ndim)]
    dynamic_slice x15 -> x1, local copies, waits for them, and re-layouts: 25.2 us -> 0.01 us  [block_at(): return lax.dynamic_index_in_dim(array, index, axis, keepdims=False)]
    ppermute x27 -> x21, starting transfers between devices: 72.6 us -> 50 us  [group_send(): lax.ppermute(block, 'fsdp', [(g * others + o, (g + shift) % GROUPS * othe...]
    unnamed x316 -> x119, local copies, waits for them, and re-layouts: 35.4 us -> 13.7 us
    ppermute x114 -> x16, waiting for transfers between devices: 91.7 us -> 74 us  [send(): lax.ppermute(block, 'fsdp', self.forward if way > 0 else self.backward)]
  transfers between devices with their start and end apart: 200 -> 87, of which waited for: 74 -> 38; matrix products, arithmetic and copies ran while one was open for 38% -> 14% of each run, Pallas kernels for 0% -> 15%
where the time goes in v2:
time: 554 us; the launch traced here: 544 us
  waiting for transfers between devices  230 us (42%)
  starting transfers between devices  112 us (20%)
  Pallas kernels  98.9 us (18%)
  other arithmetic  56.6 us (10%)
  local copies, waits for them, and re-layouts  44 us (8%)
    ppermute x16, waiting for transfers between devices, send(): lax.ppermute(block, 'fsdp', self.forward if way > 0 else self.backward)  74 us
    ppermute x39, waiting for transfers between devices, tp_send(): return lax.ppermute(block, 'tp', [(i, i ^ mask) for i in range(4)])  70.3 us
    ppermute x21, waiting for transfers between devices, group_send(): lax.ppermute(block, 'fsdp', [(g * others + o, (g + shift) % GROUPS * othe...  65 us
    ppermute x21, starting transfers between devices, group_send(): lax.ppermute(block, 'fsdp', [(g * others + o, (g + shift) % GROUPS * othe...  50 us
    ppermute x39, starting transfers between devices, tp_send(): return lax.ppermute(block, 'tp', [(i, i ^ mask) for i in range(4)])  25.9 us
    ppermute x16, starting transfers between devices, send(): lax.ppermute(block, 'fsdp', self.forward if way > 0 else self.backward)  18.1 us
    pallas_call x2, Pallas kernels, fc_gradient(): pl.pallas_call(ffn_gradient, grid_spec=pltpu.PrefetchScalarGridSpec(num_s...  15.6 us
    pallas_call x2, Pallas kernels, forward_half(): pl.pallas_call(ffn_forward, grid=(2,), in_specs=[scalars, rows(model_widt...  14.1 us
  transfers between devices with their start and end apart: 87, of which 38 were waited for; matrix products, arithmetic and copies ran while one was open for 14% of the time, Pallas kernels for 15%

profile of v2, /device:TPU:0, one launch (start us, length us, event | category | flops | bytes accessed | tf_op | source)
XLA Modules:
  0.0 543.8 jit_solution(13053475125427707395)
XLA Ops:
  3.1 3.1 collective-permute-start
  6.2 23.1 %collective-permute-done.refs_8_.refs_7_ = bf16[1024,512]{1,0:T(8,128)(2,1)S(1)} collective-permute-done((bf16[1024,512]{1,0:T(8,128)(2,1)S(1)}, bf16[1024,512]{1,0:T(8,128)(2,1)S(1)}, u32[]{:S(2)}, u32[]{:S(2)}) %collective-permute-start) | collective-permute-done | bytes 1048608 | tf_op jit(solution)/shard_map/ppermute | solution.py:63
  35.3 4.8 all-to-all-start
  46.4 8.4 %collective-permute-done.2.refs_7_.refs_6_ = bf16[1024,512]{1,0:T(8,128)(2,1)} collective-permute-done((bf16[1024,512]{1,0:T(8,128)(2,1)S(1)}, bf16[1024,512]{1,0:T(8,128)(2,1)}, u32[]{:S(2)}, u32[]{:S(2)}) %collective-permute-start.2) | collective-permute-done | bytes 1048608 | tf_op jit(solution)/shard_map/ppermute | solution.py:63
  63.2 15.4 %collective-permute-done.4.refs_6_.refs_5_ = bf16[1024,512]{1,0:T(8,128)(2,1)S(1)} collective-permute-done((bf16[1024,512]{1,0:T(8,128)(2,1)}, bf16[1024,512]{1,0:T(8,128)(2,1)S(1)}, u32[]{:S(2)}, u32[]{:S(2)}) %collective-permute-start.4) | collective-permute-done | bytes 1048608 | tf_op jit(solution)/shard_map/ppermute | solution.py:63
  90.2 6.3 %collective-permute-done.7.refs_5_.refs_4_ = bf16[512,512]{1,0:T(8,128)(2,1)S(1)} collective-permute-done((bf16[512,512]{1,0:T(8,128)(2,1)S(1)}, bf16[512,512]{1,0:T(8,128)(2,1)S(1)}, u32[]{:S(2)}, u32[]{:S(2)}) %collective-permute-start.7) | collective-permute-done | bytes 524320 | tf_op jit(solution)/shard_map/ppermute | solution.py:63
  98.2 11.0 %attention_forward.1 = (bf16[256,512]{1,0:T(8,128)(2,1)}, bf16[256,512]{1,0:T(8,128)(2,1)}, bf16[256,512]{1,0:T(8,128)(2,1)}, f32[256,512]{1,0:T(8,128)}, f32[256,128]{1,0:T(8,128)}) custom-call(s32[8]{0:T(128)} %get-tuple-element.327.labels, s32[2]{0:T(128)} %broadcast_add_fusion.limits, bf16[256,2048]{1,0:T(8,128)(2,1)} %fusion.3.x, ...), custom_call_target="tpu_custom_call" | custom-call | flops 1610612736 | bytes 12582912 | tf_op jit(solution)/shard_map/attention_forward/pallas_call | solution.py:676
  110.2 20.7 %collective-permute-done.10.refs_3_ = bf16[512,512]{1,0:T(8,128)(2,1)S(1)} collective-permute-done((bf16[512,512]{1,0:T(8,128)(2,1)}, bf16[512,512]{1,0:T(8,128)(2,1)S(1)}, u32[]{:S(2)}, u32[]{:S(2)}) %collective-permute-start.10) | collective-permute-done | bytes 524320 | tf_op jit(solution)/shard_map/ppermute | solution.py:492
  132.4 3.9 collective-permute-done.13
  140.2 4.4 output_product.1
  146.1 3.2 collective-permute-start.17
  158.7 9.0 %collective-permute-done.18 = bf16[64,2048]{1,0:T(8,128)(2,1)S(1)} collective-permute-done((bf16[64,2048]{1,0:T(8,128)(2,1)S(1)}, bf16[64,2048]{1,0:T(8,128)(2,1)S(1)}, u32[]{:S(2)}, u32[]{:S(2)}) %collective-permute-start.18) | collective-permute-done | bytes 262176 | tf_op jit(solution)/shard_map/ppermute | solution.py:492
  170.2 6.4 %collective-permute-start.20 = (bf16[64,2048]{1,0:T(8,128)(2,1)S(1)}, bf16[64,2048]{1,0:T(8,128)(2,1)S(1)}, u32[]{:S(2)}, u32[]{:S(2)}) collective-permute-start(bf16[64,2048]{1,0:T(8,128)(2,1)S(1)} %add_convert_fusion.4), channel_id=1, source_target_pairs={{0,8},{4,12},{8,16},{12,20},{16,24},{20,28},{24,0},{28,4},{1,9},{5... | collective-permute-start | bytes 786440 | tf_op jit(solution)/shard_map/ppermute | solution.py:492
  178.1 3.4 collective-permute-start.22
  182.2 4.4 collective-permute-done.20
  190.6 6.0 %collective-permute-done.22 = bf16[64,2048]{1,0:T(8,128)(2,1)S(1)} collective-permute-done((bf16[64,2048]{1,0:T(8,128)(2,1)S(1)}, bf16[64,2048]{1,0:T(8,128)(2,1)S(1)}, u32[]{:S(2)}, u32[]{:S(2)}) %collective-permute-start.22) | collective-permute-done | bytes 262176 | tf_op jit(solution)/shard_map/ppermute | solution.py:492
  201.6 16.0 %collective-permute-done.24 = bf16[64,2048]{1,0:T(8,128)(2,1)S(1)} collective-permute-done((bf16[64,2048]{1,0:T(8,128)(2,1)S(1)}, bf16[64,2048]{1,0:T(8,128)(2,1)S(1)}, u32[]{:S(2)}, u32[]{:S(2)}) %collective-permute-start.24) | collective-permute-done | bytes 262176 | tf_op jit(solution)/shard_map/ppermute | solution.py:119
  217.5 3.7 collective-permute-done.25
  224.2 3.4 collective-permute-done.26
  231.4 7.0 %ffn_forward.2 = (f32[512,512]{1,0:T(8,128)}, f32[512,512]{1,0:T(8,128)}, f32[512,512]{1,0:T(8,128)}, f32[8,512]{1,0:T(8,128)}) custom-call(s32[8]{0:T(128)} %fusion.41.labels, bf16[512,2048]{1,0:T(8,128)(2,1)} %constant_dynamic-update-slice_fusion.x.near_x, bf16[512,2048]{1,0:T(8,128)(2,1)} %copy-done.13, f32[3,512]{1,0:T(4,128)} %bitcast.227, ...), custom_call_target="tpu_custom_call" | custom-call | flops 2147483648 | bytes 10485760 | tf_op jit(solution)/shard_map/ffn_forward/pallas_call | solution.py:743
  239.2 7.1 %ffn_forward.3 = (f32[512,512]{1,0:T(8,128)}, f32[512,512]{1,0:T(8,128)}, f32[512,512]{1,0:T(8,128)}, f32[8,512]{1,0:T(8,128)}) custom-call(s32[8]{0:T(128)} %fusion.41.labels, bf16[512,2048]{1,0:T(8,128)(2,1)} %collective-permute-done.31.x.far_x, bf16[512,2048]{1,0:T(8,128)(2,1)} %collective-permute-done.32.g.far_g, f32[3,512]{1,0:T(4,128)} %bitcast.228, ...), custom_call_target="tpu_custom_call" | custom-call | flops 2147483648 | bytes 10485760 | tf_op jit(solution)/shard_map/ffn_forward/pallas_call | solution.py:743
  256.6 3.3 collective-permute-done.36
  260.7 6.1 %ffn_backward.3 = (bf16[512,512]{1,0:T(8,128)(2,1)}, bf16[512,512]{1,0:T(8,128)(2,1)}, bf16[512,2048]{1,0:T(8,128)(2,1)}, f32[8,512]{1,0:T(8,128)}) custom-call(s32[8]{0:T(128)} %fusion.41.labels, f32[8,1024]{1,0:T(8,128)} %add_add_fusion.3.sums, f32[512,512]{1,0:T(8,128)} %get-tuple-element.125.active, f32[512,512]{1,0:T(8,128)} %get-tuple-element.126.slope, ...), custom_call_target="tpu_custom_call" | custom-call | flops 1073741824 | bytes 8388608 | tf_op jit(solution)/shard_map/ffn_backward/pallas_call | solution.py:760
  270.0 6.0 %ffn_backward.2 = (bf16[512,512]{1,0:T(8,128)(2,1)}, bf16[512,512]{1,0:T(8,128)(2,1)}, bf16[512,2048]{1,0:T(8,128)(2,1)}, f32[8,512]{1,0:T(8,128)}) custom-call(s32[8]{0:T(128)} %fusion.41.labels, f32[8,1024]{1,0:T(8,128)} %add_add_fusion.3.sums, f32[512,512]{1,0:T(8,128)} %get-tuple-element.121.active, f32[512,512]{1,0:T(8,128)} %get-tuple-element.122.slope, ...), custom_call_target="tpu_custom_call" | custom-call | flops 1073741824 | bytes 8388608 | tf_op jit(solution)/shard_map/ffn_backward/pallas_call | solution.py:760
  284.2 7.7 %ffn_gradient.3 = (bf16[512,512]{1,0:T(8,128)(2,1)}, bf16[512,512]{1,0:T(8,128)(2,1)}, bf16[512,512]{1,0:T(8,128)(2,1)}, bf16[512,512]{1,0:T(8,128)(2,1)}) custom-call(s32[4]{0:T(128)} %get-tuple-element.335.labels, bf16[512,2048]{1,0:T(8,128)(2,1)} %constant_dynamic-update-slice_fusion.x.near_x, bf16[512,2048]{1,0:T(8,128)(2,1)} %collective-permute-done.31.x.far_x, ...), custom_call_target="tpu_custom_call" | custom-call | flops 2147483648 | bytes 9437184 | tf_op jit(solution)/shard_map/ffn_gradient/pallas_call | solution.py:797
  298.3 3.6 collective-permute-done.48
  311.6 7.8 %ffn_gradient.2 = (bf16[512,512]{1,0:T(8,128)(2,1)}, bf16[512,512]{1,0:T(8,128)(2,1)}, bf16[512,512]{1,0:T(8,128)(2,1)}, bf16[512,512]{1,0:T(8,128)(2,1)}) custom-call(s32[4]{0:T(128)} %get-tuple-element.334.labels, bf16[512,2048]{1,0:T(8,128)(2,1)} %constant_dynamic-update-slice_fusion.x.near_x, bf16[512,2048]{1,0:T(8,128)(2,1)} %collective-permute-done.31.x.far_x, ...), custom_call_target="tpu_custom_call" | custom-call | flops 2147483648 | bytes 9437184 | tf_op jit(solution)/shard_map/ffn_gradient/pallas_call | solution.py:797
  321.2 8.2 %collective-permute-done.44 = bf16[512,512]{1,0:T(8,128)(2,1)S(1)} collective-permute-done((bf16[512,512]{1,0:T(8,128)(2,1)}, bf16[512,512]{1,0:T(8,128)(2,1)S(1)}, u32[]{:S(2)}, u32[]{:S(2)}) %collective-permute-start.44) | collective-permute-done | bytes 524320 | tf_op jit(solution)/shard_map/ppermute | solution.py:506
  334.6 3.4 collective-permute-start.62
  341.4 3.6 output_back.1
  349.0 11.6 %collective-permute-done.55.refs_0_ = bf16[512,512]{1,0:T(8,128)(2,1)S(1)} collective-permute-done((bf16[512,512]{1,0:T(8,128)(2,1)}, bf16[512,512]{1,0:T(8,128)(2,1)S(1)}, u32[]{:S(2)}, u32[]{:S(2)}) %collective-permute-start.55) | collective-permute-done | bytes 524320 | tf_op jit(solution)/shard_map/ppermute | solution.py:492
  360.7 9.4 %collective-permute-start.61 = (bf16[512,512]{1,0:T(8,128)(2,1)}, bf16[512,512]{1,0:T(8,128)(2,1)}, u32[]{:S(2)}, u32[]{:S(2)}) collective-permute-start(bf16[512,512]{1,0:T(8,128)(2,1)} %add_convert_fusion.2), channel_id=1, source_target_pairs={{0,8},{4,12},{8,16},{12,20},{16,24},{20,28},{24,0},{28,4},{1,9},{5... | collective-permute-start | bytes 1572872 | tf_op jit(solution)/shard_map/ppermute | solution.py:492
  371.4 5.4 attention_backward.1
  379.0 3.3 projection_gradient_far.1
  384.3 4.2 ffn_product.3
  388.5 4.2 ffn_product.2
  392.7 8.9 %projection_gradient.1 = bf16[7,1024,512]{2,1,0:T(8,128)(2,1)} custom-call(s32[7]{0:T(128)} %fusion.44.labels, bf16[256,2048]{1,0:T(8,128)(2,1)} %fusion.3.x, bf16[256,2048]{1,0:T(8,128)(2,1)} %pad_maximum_fusion.3.grad, bf16[256,512]{1,0:T(8,128)(2,1)} %copy-done.1, bf16[256,512]{1,0:T(8,128)(2,1)} %copy-done.2, bf16[256,512]{1,0:T(8,128)(2,1)} %copy-done.3, ...), custom_call_target="tpu_custom_call" | custom-call | flops 1879048192 | bytes 7340032 | tf_op jit(solution)/shard_map/projection_gradient/pallas_call | solution.py:909
  408.7 8.2 %projection_back.1 = (bf16[128,2048]{1,0:T(8,128)(2,1)}, f32[128,2048]{1,0:T(8,128)}) custom-call(s32[8]{0:T(128)} %get-tuple-element.327.labels, s32[1]{0:T(128)} %bitcast.1.rank, bf16[256,512]{1,0:T(8,128)(2,1)} %copy-done.1, bf16[256,512]{1,0:T(8,128)(2,1)} %copy-done.2, bf16[256,512]{1,0:T(8,128)(2,1)} %copy-done.3, bf16[1024,512]{1,0:T(8,128)(2,1)} %copy-done.11, ...), custom_call_target="tpu_custom_call" | custom-call | flops 1610612736 | bytes 10485760 | tf_op jit(solution)/shard_map/projection_back/pallas_call | solution.py:972
  419.3 13.3 %collective-permute-done.64 = bf16[1024,512]{1,0:T(8,128)(2,1)} collective-permute-done((bf16[1024,512]{1,0:T(8,128)(2,1)}, bf16[1024,512]{1,0:T(8,128)(2,1)}, u32[]{:S(2)}, u32[]{:S(2)}) %collective-permute-start.64) | collective-permute-done | bytes 1048608 | tf_op jit(solution)/shard_map/ppermute | solution.py:63
  434.4 4.2 fusion.7
  446.1 3.9 ffn_placed.1
  453.6 20.1 %collective-permute-done.69 = f32[6,2048]{1,0:T(8,128)S(1)} collective-permute-done((f32[6,2048]{1,0:T(8,128)S(1)}, f32[6,2048]{1,0:T(8,128)S(1)}, u32[]{:S(2)}, u32[]{:S(2)}) %collective-permute-start.69) | collective-permute-done | bytes 49184 | tf_op jit(solution)/shard_map/ppermute | solution.py:119
  475.9 4.1 fusion.5
  484.4 10.3 %collective-permute-done.74 = f32[64,2048]{1,0:T(8,128)} collective-permute-done((f32[64,2048]{1,0:T(8,128)}, f32[64,2048]{1,0:T(8,128)}, u32[]{:S(2)}, u32[]{:S(2)}) %collective-permute-start.74) | collective-permute-done | bytes 524320 | tf_op jit(solution)/shard_map/ppermute | solution.py:119
  495.4 5.3 all-to-all-start.1
  504.9 11.7 %all-to-all-done.1 = f32[8,1,1856]{2,1,0:T(1,128)S(1)} async-done(((f32[8,1,1856]{2,1,0:T(1,128)}), f32[8,1,1856]{2,1,0:T(1,128)S(1)}, u32[]{:S(2)}, u32[]{:S(2)}) %all-to-all-start.1) | async-done | bytes 59424 | tf_op jit(solution)/shard_map/all_to_all | solution.py:1023
  516.6 3.8 collective-permute-start.78
  526.5 4.5 collective-permute-done.79
  (397 shorter events, 184.8 us)
Async XLA Ops:
  3.1 26.2 %collective-permute-start = (bf16[1024,512]{1,0:T(8,128)(2,1)S(1)}, bf16[1024,512]{1,0:T(8,128)(2,1)S(1)}, u32[]{:S(2)}, u32[]{:S(2)}) collective-permute-start(bf16[1024,512]{1,0:T(8,128)(2,1)S(1)} %pad_maximum_fusion.1.refs_0_), channel_id=1, source_target_pairs={{0,8},{8,16},{16,24},{24,28},{28,20},{20,12},{12,4},{4,0},{1,9},{9... | collective-permute-start | bytes 3145736 | tf_op jit(solution)/shard_map/ppermute | solution.py:63
  6.2 24.6 %collective-permute-start.1 = (bf16[1024,512]{1,0:T(8,128)(2,1)S(1)}, bf16[1024,512]{1,0:T(8,128)(2,1)S(1)}, u32[]{:S(2)}, u32[]{:S(2)}) collective-permute-start(bf16[1024,512]{1,0:T(8,128)(2,1)S(1)} %pad_maximum_fusion.1.refs_0_), channel_id=1, source_target_pairs={{8,0},{16,8},{24,16},{28,24},{20,28},{12,20},{4,12},{0,4},{9,1},{1... | collective-permute-start | bytes 3145736 | tf_op jit(solution)/shard_map/ppermute | solution.py:63
  30.8 24.0 %collective-permute-start.2 = (bf16[1024,512]{1,0:T(8,128)(2,1)S(1)}, bf16[1024,512]{1,0:T(8,128)(2,1)}, u32[]{:S(2)}, u32[]{:S(2)}) collective-permute-start(bf16[1024,512]{1,0:T(8,128)(2,1)S(1)} %collective-permute-done.refs_8_.refs_7_), channel_id=1, source_target_pairs={{0,8},{8,16},{16,24},{24,28},{28,20},{20,12},{12,4},{4,0},{1,9},{9... | collective-permute-start | bytes 3145736 | tf_op jit(solution)/shard_map/ppermute | solution.py:63
  32.4 23.9 %collective-permute-start.3 = (bf16[1024,512]{1,0:T(8,128)(2,1)S(1)}, bf16[1024,512]{1,0:T(8,128)(2,1)}, u32[]{:S(2)}, u32[]{:S(2)}) collective-permute-start(bf16[1024,512]{1,0:T(8,128)(2,1)S(1)} %collective-permute-done.1.refs_1_), channel_id=1, source_target_pairs={{8,0},{16,8},{24,16},{28,24},{20,28},{12,20},{4,12},{0,4},{9,1},{1... | collective-permute-start | bytes 3145736 | tf_op jit(solution)/shard_map/ppermute | solution.py:63
  35.3 27.7 %all-to-all-start = ((bf16[8,2,1312]{2,1,0:T(2,128)(2,1)}), bf16[8,2,1312]{2,1,0:T(2,128)(2,1)S(1)}, u32[]{:S(2)}, u32[]{:S(2)}) async-start(bf16[8,2,1312]{2,1,0:T(2,128)(2,1)} %reshape.370), calls=%async_computation | async-start | bytes 90112 | tf_op jit(solution)/shard_map/all_to_all | solution.py:540
  56.3 22.4 %collective-permute-start.4 = (bf16[1024,512]{1,0:T(8,128)(2,1)}, bf16[1024,512]{1,0:T(8,128)(2,1)S(1)}, u32[]{:S(2)}, u32[]{:S(2)}) collective-permute-start(bf16[1024,512]{1,0:T(8,128)(2,1)} %collective-permute-done.2.refs_7_.refs_6_), channel_id=1, source_target_pairs={{0,8},{8,16},{16,24},{24,28},{28,20},{20,12},{12,4},{4,0},{1,9},{9... | collective-permute-start | bytes 3145736 | tf_op jit(solution)/shard_map/ppermute | solution.py:63
  58.0 23.4 %collective-permute-start.5 = (bf16[1024,512]{1,0:T(8,128)(2,1)}, bf16[1024,512]{1,0:T(8,128)(2,1)S(1)}, u32[]{:S(2)}, u32[]{:S(2)}) collective-permute-start(bf16[1024,512]{1,0:T(8,128)(2,1)} %collective-permute-done.3.refs_2_), channel_id=1, source_target_pairs={{8,0},{16,8},{24,16},{28,24},{20,28},{12,20},{4,12},{0,4},{9,1},{1... | collective-permute-start | bytes 3145736 | tf_op jit(solution)/shard_map/ppermute | solution.py:63
  88.2 42.7 %collective-permute-start.10 = (bf16[512,512]{1,0:T(8,128)(2,1)}, bf16[512,512]{1,0:T(8,128)(2,1)S(1)}, u32[]{:S(2)}, u32[]{:S(2)}) collective-permute-start(bf16[512,512]{1,0:T(8,128)(2,1)} %get-tuple-element.284), channel_id=1, source_target_pairs={{0,16},{4,20},{8,24},{12,28},{16,0},{20,4},{24,8},{28,12},{1,17},{... | collective-permute-start | bytes 1572872 | tf_op jit(solution)/shard_map/ppermute | solution.py:492
  89.6 42.8 %collective-permute-start.11 = (bf16[512,512]{1,0:T(8,128)(2,1)S(1)}, bf16[512,512]{1,0:T(8,128)(2,1)S(1)}, u32[]{:S(2)}, u32[]{:S(2)}) collective-permute-start(bf16[512,512]{1,0:T(8,128)(2,1)S(1)} %get-tuple-element.283.refs_0_), channel_id=1, source_target_pairs={{0,4},{4,0},{8,12},{12,8},{16,20},{20,16},{24,28},{28,24},{1,5},{5... | collective-permute-start | bytes 1572872 | tf_op jit(solution)/shard_map/ppermute | solution.py:506
  89.6 42.8 %collective-permute-start.8 = (bf16[512,512]{1,0:T(8,128)(2,1)}, bf16[512,512]{1,0:T(8,128)(2,1)}, u32[]{:S(2)}, u32[]{:S(2)}) collective-permute-start(bf16[512,512]{1,0:T(8,128)(2,1)} %get-tuple-element.286), channel_id=1, source_target_pairs={{0,8},{4,12},{8,16},{12,20},{16,24},{20,28},{24,0},{28,4},{1,9},{5... | collective-permute-start | bytes 1572872 | tf_op jit(solution)/shard_map/ppermute | solution.py:492
  96.5 35.9 %collective-permute-start.9 = (bf16[512,512]{1,0:T(8,128)(2,1)}, bf16[512,512]{1,0:T(8,128)(2,1)}, u32[]{:S(2)}, u32[]{:S(2)}) collective-permute-start(bf16[512,512]{1,0:T(8,128)(2,1)} %get-tuple-element.285), channel_id=1, source_target_pairs={{0,24},{4,28},{8,0},{12,4},{16,8},{20,12},{24,16},{28,20},{1,25},{... | collective-permute-start | bytes 1572872 | tf_op jit(solution)/shard_map/ppermute | solution.py:492
  110.2 22.3 %collective-permute-start.12 = (f32[2,256]{0,1:T(8,128)S(1)}, f32[2,256]{0,1:T(8,128)S(1)}, u32[]{:S(2)}, u32[]{:S(2)}) collective-permute-start(f32[2,256]{0,1:T(8,128)S(1)} %slice_bitcast_fusion.26), channel_id=1, source_target_pairs={{0,1},{1,0},{2,3},{3,2},{4,5},{5,4},{6,7},{7,6},{8,9},{9,8},{10,11... | collective-permute-start | bytes 6152 | tf_op jit(solution)/shard_map/ppermute | solution.py:119
  149.3 18.4 %collective-permute-start.18 = (bf16[64,2048]{1,0:T(8,128)(2,1)S(1)}, bf16[64,2048]{1,0:T(8,128)(2,1)S(1)}, u32[]{:S(2)}, u32[]{:S(2)}) collective-permute-start(bf16[64,2048]{1,0:T(8,128)(2,1)S(1)} %fusion.30), channel_id=1, source_target_pairs={{0,16},{4,20},{8,24},{12,28},{16,0},{20,4},{24,8},{28,12},{1,17},{... | collective-permute-start | bytes 786440 | tf_op jit(solution)/shard_map/ppermute | solution.py:492
  156.6 71.8 %collective-permute-start.27 = (bf16[512,512]{1,0:T(8,128)(2,1)}, bf16[512,512]{1,0:T(8,128)(2,1)S(1)}, u32[]{:S(2)}, u32[]{:S(2)}) collective-permute-start(bf16[512,512]{1,0:T(8,128)(2,1)} %collective-permute-done.8.refs_1_), channel_id=1, source_target_pairs={{0,4},{4,0},{8,12},{12,8},{16,20},{20,16},{24,28},{28,24},{1,5},{5... | collective-permute-start | bytes 1572872 | tf_op jit(solution)/shard_map/ppermute | solution.py:506
  157.2 71.1 %collective-permute-start.28 = (bf16[512,512]{1,0:T(8,128)(2,1)}, bf16[512,512]{1,0:T(8,128)(2,1)S(1)}, u32[]{:S(2)}, u32[]{:S(2)}) collective-permute-start(bf16[512,512]{1,0:T(8,128)(2,1)} %collective-permute-done.9.refs_2_), channel_id=1, source_target_pairs={{0,4},{4,0},{8,12},{12,8},{16,20},{20,16},{24,28},{28,24},{1,5},{5... | collective-permute-start | bytes 1572872 | tf_op jit(solution)/shard_map/ppermute | solution.py:506
  178.1 18.5 %collective-permute-start.22 = (bf16[64,2048]{1,0:T(8,128)(2,1)S(1)}, bf16[64,2048]{1,0:T(8,128)(2,1)S(1)}, u32[]{:S(2)}, u32[]{:S(2)}) collective-permute-start(bf16[64,2048]{1,0:T(8,128)(2,1)S(1)} %add_convert_fusion.4), channel_id=1, source_target_pairs={{0,16},{4,20},{8,24},{12,28},{16,0},{20,4},{24,8},{28,12},{1,17},{... | collective-permute-start | bytes 786440 | tf_op jit(solution)/shard_map/ppermute | solution.py:492
  186.7 42.6 %collective-permute-start.30 = (bf16[256,2048]{1,0:T(8,128)(2,1)S(1)}, bf16[256,2048]{1,0:T(8,128)(2,1)S(1)}, u32[]{:S(2)}, u32[]{:S(2)}) collective-permute-start(bf16[256,2048]{1,0:T(8,128)(2,1)S(1)} %pad_maximum_fusion.2), channel_id=1, source_target_pairs={{0,2},{1,3},{2,0},{3,1},{4,6},{5,7},{6,4},{7,5},{8,10},{9,11},{10,... | collective-permute-start | bytes 3145736 | tf_op jit(solution)/shard_map/ppermute | solution.py:119
  196.6 20.9 %collective-permute-start.24 = (bf16[64,2048]{1,0:T(8,128)(2,1)S(1)}, bf16[64,2048]{1,0:T(8,128)(2,1)S(1)}, u32[]{:S(2)}, u32[]{:S(2)}) collective-permute-start(bf16[64,2048]{1,0:T(8,128)(2,1)S(1)} %collective-permute-done.20), channel_id=1, source_target_pairs={{0,2},{1,3},{2,0},{3,1},{4,6},{5,7},{6,4},{7,5},{8,10},{9,11},{10,... | collective-permute-start | bytes 786440 | tf_op jit(solution)/shard_map/ppermute | solution.py:119
  199.1 22.1 %collective-permute-start.25 = (bf16[64,2048]{1,0:T(8,128)(2,1)S(1)}, bf16[64,2048]{1,0:T(8,128)(2,1)S(1)}, u32[]{:S(2)}, u32[]{:S(2)}) collective-permute-start(bf16[64,2048]{1,0:T(8,128)(2,1)S(1)} %collective-permute-done.22), channel_id=1, source_target_pairs={{0,2},{1,3},{2,0},{3,1},{4,6},{5,7},{6,4},{7,5},{8,10},{9,11},{10,... | collective-permute-start | bytes 786440 | tf_op jit(solution)/shard_map/ppermute | solution.py:119
  276.8 17.1 %collective-permute-start.45 = (f32[3,256]{1,0:T(4,128)S(1)}, f32[3,256]{1,0:T(4,128)S(1)}, u32[]{:S(2)}, u32[]{:S(2)}) collective-permute-start(f32[3,256]{1,0:T(4,128)S(1)} %bitcast.268), channel_id=1, source_target_pairs={{0,4},{4,0},{8,12},{12,8},{16,20},{20,16},{24,28},{28,24},{1,5},{5... | collective-permute-start | bytes 9224 | tf_op jit(solution)/shard_map/ppermute | solution.py:506
  283.5 18.3 %collective-permute-start.48 = (bf16[64,2048]{1,0:T(8,128)(2,1)S(1)}, bf16[64,2048]{1,0:T(8,128)(2,1)S(1)}, u32[]{:S(2)}, u32[]{:S(2)}) collective-permute-start(bf16[64,2048]{1,0:T(8,128)(2,1)S(1)} %get-tuple-element.280), channel_id=1, source_target_pairs={{0,2},{1,3},{2,0},{3,1},{4,6},{5,7},{6,4},{7,5},{8,10},{9,11},{10,... | collective-permute-start | bytes 786440 | tf_op jit(solution)/shard_map/ppermute | solution.py:119
  295.3 24.1 %collective-permute-start.43 = (bf16[512,512]{1,0:T(8,128)(2,1)}, bf16[512,512]{1,0:T(8,128)(2,1)S(1)}, u32[]{:S(2)}, u32[]{:S(2)}) collective-permute-start(bf16[512,512]{1,0:T(8,128)(2,1)} %get-tuple-element.139), channel_id=1, source_target_pairs={{0,4},{4,0},{8,12},{12,8},{16,20},{20,16},{24,28},{28,24},{1,5},{5... | collective-permute-start | bytes 1572872 | tf_op jit(solution)/shard_map/ppermute | solution.py:506
  296.2 33.2 %collective-permute-start.44 = (bf16[512,512]{1,0:T(8,128)(2,1)}, bf16[512,512]{1,0:T(8,128)(2,1)S(1)}, u32[]{:S(2)}, u32[]{:S(2)}) collective-permute-start(bf16[512,512]{1,0:T(8,128)(2,1)} %get-tuple-element.140), channel_id=1, source_target_pairs={{0,4},{4,0},{8,12},{12,8},{16,20},{20,16},{24,28},{28,24},{1,5},{5... | collective-permute-start | bytes 1572872 | tf_op jit(solution)/shard_map/ppermute | solution.py:506
  303.4 26.0 %collective-permute-start.49 = (bf16[64,2048]{1,0:T(8,128)(2,1)S(1)}, bf16[64,2048]{1,0:T(8,128)(2,1)S(1)}, u32[]{:S(2)}, u32[]{:S(2)}) collective-permute-start(bf16[64,2048]{1,0:T(8,128)(2,1)S(1)} %get-tuple-element.145), channel_id=1, source_target_pairs={{0,24},{4,28},{8,0},{12,4},{16,8},{20,12},{24,16},{28,20},{1,25},{... | collective-permute-start | bytes 786440 | tf_op jit(solution)/shard_map/ppermute | solution.py:492
  307.0 22.4 %collective-permute-start.50 = (bf16[64,2048]{1,0:T(8,128)(2,1)S(1)}, bf16[64,2048]{1,0:T(8,128)(2,1)S(1)}, u32[]{:S(2)}, u32[]{:S(2)}) collective-permute-start(bf16[64,2048]{1,0:T(8,128)(2,1)S(1)} %get-tuple-element.146), channel_id=1, source_target_pairs={{0,8},{4,12},{8,16},{12,20},{16,24},{20,28},{24,0},{28,4},{1,9},{5... | collective-permute-start | bytes 786440 | tf_op jit(solution)/shard_map/ppermute | solution.py:492
  307.8 21.6 %collective-permute-start.46 = (bf16[64,2048]{1,0:T(8,128)(2,1)S(1)}, bf16[64,2048]{1,0:T(8,128)(2,1)S(1)}, u32[]{:S(2)}, u32[]{:S(2)}) collective-permute-start(bf16[64,2048]{1,0:T(8,128)(2,1)S(1)} %get-tuple-element.272), channel_id=1, source_target_pairs={{0,16},{4,20},{8,24},{12,28},{16,0},{20,4},{24,8},{28,12},{1,17},{... | collective-permute-start | bytes 786440 | tf_op jit(solution)/shard_map/ppermute | solution.py:492
  319.4 19.8 %collective-permute-start.54 = (bf16[512,512]{1,0:T(8,128)(2,1)S(1)}, bf16[512,512]{1,0:T(8,128)(2,1)S(1)}, u32[]{:S(2)}, u32[]{:S(2)}) collective-permute-start(bf16[512,512]{1,0:T(8,128)(2,1)S(1)} %copy-done.44), channel_id=1, source_target_pairs={{0,4},{4,0},{8,12},{12,8},{16,20},{20,16},{24,28},{28,24},{1,5},{5... | collective-permute-start | bytes 1572872 | tf_op jit(solution)/shard_map/ppermute | solution.py:506
  333.7 27.0 %collective-permute-start.55 = (bf16[512,512]{1,0:T(8,128)(2,1)}, bf16[512,512]{1,0:T(8,128)(2,1)S(1)}, u32[]{:S(2)}, u32[]{:S(2)}) collective-permute-start(bf16[512,512]{1,0:T(8,128)(2,1)} %add_convert_fusion.3), channel_id=1, source_target_pairs={{0,16},{4,20},{8,24},{12,28},{16,0},{20,4},{24,8},{28,12},{1,17},{... | collective-permute-start | bytes 1572872 | tf_op jit(solution)/shard_map/ppermute | solution.py:492
  334.6 68.3 %collective-permute-start.62 = (bf16[512,512]{1,0:T(8,128)(2,1)}, bf16[512,512]{1,0:T(8,128)(2,1)}, u32[]{:S(2)}, u32[]{:S(2)}) collective-permute-start(bf16[512,512]{1,0:T(8,128)(2,1)} %add_convert_fusion.1), channel_id=1, source_target_pairs={{0,24},{4,28},{8,0},{12,4},{16,8},{20,12},{24,16},{28,20},{1,25},{... | collective-permute-start | bytes 1572872 | tf_op jit(solution)/shard_map/ppermute | solution.py:492
  346.1 23.9 %collective-permute-start.56 = (f32[2,256]{0,1:T(8,128)S(1)}, f32[2,256]{0,1:T(8,128)S(1)}, u32[]{:S(2)}, u32[]{:S(2)}) collective-permute-start(f32[2,256]{0,1:T(8,128)S(1)} %slice_bitcast_fusion.25), channel_id=1, source_target_pairs={{0,1},{1,0},{2,3},{3,2},{4,5},{5,4},{6,7},{7,6},{8,9},{9,8},{10,11... | collective-permute-start | bytes 6152 | tf_op jit(solution)/shard_map/ppermute | solution.py:119
  346.2 23.9 %collective-permute-start.57 = (f32[2,256]{0,1:T(8,128)S(1)}, f32[2,256]{0,1:T(8,128)S(1)}, u32[]{:S(2)}, u32[]{:S(2)}) collective-permute-start(f32[2,256]{0,1:T(8,128)S(1)} %slice_bitcast_fusion.25), channel_id=1, source_target_pairs={{0,2},{1,3},{2,0},{3,1},{4,6},{5,7},{6,4},{7,5},{8,10},{9,11},{10,... | collective-permute-start | bytes 6152 | tf_op jit(solution)/shard_map/ppermute | solution.py:119
  347.6 22.4 %collective-permute-start.58 = (f32[2,256]{0,1:T(8,128)S(1)}, f32[2,256]{0,1:T(8,128)S(1)}, u32[]{:S(2)}, u32[]{:S(2)}) collective-permute-start(f32[2,256]{0,1:T(8,128)S(1)} %slice_bitcast_fusion.25), channel_id=1, source_target_pairs={{0,3},{1,2},{2,1},{3,0},{4,7},{5,6},{6,5},{7,4},{8,11},{9,10},{10,... | collective-permute-start | bytes 6152 | tf_op jit(solution)/shard_map/ppermute | solution.py:119
  360.7 42.2 %collective-permute-start.61 = (bf16[512,512]{1,0:T(8,128)(2,1)}, bf16[512,512]{1,0:T(8,128)(2,1)}, u32[]{:S(2)}, u32[]{:S(2)}) collective-permute-start(bf16[512,512]{1,0:T(8,128)(2,1)} %add_convert_fusion.2), channel_id=1, source_target_pairs={{0,8},{4,12},{8,16},{12,20},{16,24},{20,28},{24,0},{28,4},{1,9},{5... | collective-permute-start | bytes 1572872 | tf_op jit(solution)/shard_map/ppermute | solution.py:492
  382.3 20.6 %collective-permute-start.59 = (bf16[512,512]{1,0:T(8,128)(2,1)}, bf16[512,512]{1,0:T(8,128)(2,1)S(1)}, u32[]{:S(2)}, u32[]{:S(2)}) collective-permute-start(bf16[512,512]{1,0:T(8,128)(2,1)} %get-tuple-element.158), channel_id=1, source_target_pairs={{0,8},{8,16},{16,24},{24,28},{28,20},{20,12},{12,4},{4,0},{1,9},{9... | collective-permute-start | bytes 1572872 | tf_op jit(solution)/shard_map/ppermute | solution.py:63
  382.5 20.5 %collective-permute-start.60 = (bf16[512,512]{1,0:T(8,128)(2,1)}, bf16[512,512]{1,0:T(8,128)(2,1)S(1)}, u32[]{:S(2)}, u32[]{:S(2)}) collective-permute-start(bf16[512,512]{1,0:T(8,128)(2,1)} %get-tuple-element.159), channel_id=1, source_target_pairs={{8,0},{16,8},{24,16},{28,24},{20,28},{12,20},{4,12},{0,4},{9,1},{1... | collective-permute-start | bytes 1572872 | tf_op jit(solution)/shard_map/ppermute | solution.py:63
  406.7 26.0 %collective-permute-start.64 = (bf16[1024,512]{1,0:T(8,128)(2,1)}, bf16[1024,512]{1,0:T(8,128)(2,1)}, u32[]{:S(2)}, u32[]{:S(2)}) collective-permute-start(bf16[1024,512]{1,0:T(8,128)(2,1)} %pad_maximum_fusion.5), channel_id=1, source_target_pairs={{8,0},{16,8},{24,16},{28,24},{20,28},{12,20},{4,12},{0,4},{9,1},{1... | collective-permute-start | bytes 3145736 | tf_op jit(solution)/shard_map/ppermute | solution.py:63
  408.7 25.7 %collective-permute-start.63 = (bf16[1024,512]{1,0:T(8,128)(2,1)}, bf16[1024,512]{1,0:T(8,128)(2,1)}, u32[]{:S(2)}, u32[]{:S(2)}) collective-permute-start(bf16[1024,512]{1,0:T(8,128)(2,1)} %pad_maximum_fusion.4), channel_id=1, source_target_pairs={{0,8},{8,16},{16,24},{24,28},{28,20},{20,12},{12,4},{4,0},{1,9},{9... | collective-permute-start | bytes 3145736 | tf_op jit(solution)/shard_map/ppermute | solution.py:63
  439.8 36.1 %collective-permute-start.72 = (bf16[1024,512]{1,0:T(8,128)(2,1)}, bf16[1024,512]{1,0:T(8,128)(2,1)}, u32[]{:S(2)}, u32[]{:S(2)}) collective-permute-start(bf16[1024,512]{1,0:T(8,128)(2,1)} %get-tuple-element.267), channel_id=1, source_target_pairs={{0,8},{8,16},{16,24},{24,28},{28,20},{20,12},{12,4},{4,0},{1,9},{9... | collective-permute-start | bytes 3145736 | tf_op jit(solution)/shard_map/ppermute | solution.py:63
  442.5 31.2 %collective-permute-start.71 = (bf16[4,64,2048]{2,1,0:T(8,128)(2,1)}, bf16[4,64,2048]{2,1,0:T(8,128)(2,1)}, u32[]{:S(2)}, u32[]{:S(2)}) collective-permute-start(bf16[4,64,2048]{2,1,0:T(8,128)(2,1)} %fusion.10), channel_id=1, source_target_pairs={{0,2},{1,3},{2,0},{3,1},{4,6},{5,7},{6,4},{7,5},{8,10},{9,11},{10,... | collective-permute-start | bytes 3145736 | tf_op jit(solution)/shard_map/ppermute | solution.py:119
  443.9 32.1 %collective-permute-start.73 = (bf16[1024,512]{1,0:T(8,128)(2,1)}, bf16[1024,512]{1,0:T(8,128)(2,1)}, u32[]{:S(2)}, u32[]{:S(2)}) collective-permute-start(bf16[1024,512]{1,0:T(8,128)(2,1)} %get-tuple-element.266), channel_id=1, source_target_pairs={{8,0},{16,8},{24,16},{28,24},{20,28},{12,20},{4,12},{0,4},{9,1},{1... | collective-permute-start | bytes 3145736 | tf_op jit(solution)/shard_map/ppermute | solution.py:63
  450.5 23.1 %collective-permute-start.69 = (f32[6,2048]{1,0:T(8,128)S(1)}, f32[6,2048]{1,0:T(8,128)S(1)}, u32[]{:S(2)}, u32[]{:S(2)}) collective-permute-start(f32[6,2048]{1,0:T(8,128)S(1)} %stack.27), channel_id=1, source_target_pairs={{0,2},{1,3},{2,0},{3,1},{4,6},{5,7},{6,4},{7,5},{8,10},{9,11},{10,... | collective-permute-start | bytes 147464 | tf_op jit(solution)/shard_map/ppermute | solution.py:119
  451.8 21.9 %collective-permute-start.70 = (f32[6,2048]{1,0:T(8,128)S(1)}, f32[6,2048]{1,0:T(8,128)S(1)}, u32[]{:S(2)}, u32[]{:S(2)}) collective-permute-start(f32[6,2048]{1,0:T(8,128)S(1)} %stack.27), channel_id=1, source_target_pairs={{0,3},{1,2},{2,1},{3,0},{4,7},{5,6},{6,5},{7,4},{8,11},{9,10},{10,... | collective-permute-start | bytes 147464 | tf_op jit(solution)/shard_map/ppermute | solution.py:119
  480.8 56.8 %collective-permute-start.83 = (bf16[1024,512]{1,0:T(8,128)(2,1)}, bf16[1024,512]{1,0:T(8,128)(2,1)}, u32[]{:S(2)}, u32[]{:S(2)}) collective-permute-start(bf16[1024,512]{1,0:T(8,128)(2,1)} %get-tuple-element.265), channel_id=1, source_target_pairs={{0,8},{8,16},{16,24},{24,28},{28,20},{20,12},{12,4},{4,0},{1,9},{9... | collective-permute-start | bytes 3145736 | tf_op jit(solution)/shard_map/ppermute | solution.py:63
  482.3 34.3 %collective-permute-start.76 = (f32[64,2048]{1,0:T(8,128)}, f32[64,2048]{1,0:T(8,128)}, u32[]{:S(2)}, u32[]{:S(2)}) collective-permute-start(f32[64,2048]{1,0:T(8,128)} %fusion.23), channel_id=1, source_target_pairs={{0,1},{1,0},{2,3},{3,2},{4,5},{5,4},{6,7},{7,6},{8,9},{9,8},{10,11... | collective-permute-start | bytes 1572872 | tf_op jit(solution)/shard_map/ppermute | solution.py:119
  482.3 55.3 %collective-permute-start.84 = (bf16[1024,512]{1,0:T(8,128)(2,1)}, bf16[1024,512]{1,0:T(8,128)(2,1)}, u32[]{:S(2)}, u32[]{:S(2)}) collective-permute-start(bf16[1024,512]{1,0:T(8,128)(2,1)} %get-tuple-element.264), channel_id=1, source_target_pairs={{8,0},{16,8},{24,16},{28,24},{20,28},{12,20},{4,12},{0,4},{9,1},{1... | collective-permute-start | bytes 3145736 | tf_op jit(solution)/shard_map/ppermute | solution.py:63
  494.7 25.7 %collective-permute-start.75 = (f32[64,2048]{1,0:T(8,128)}, f32[64,2048]{1,0:T(8,128)S(1)}, u32[]{:S(2)}, u32[]{:S(2)}) collective-permute-start(f32[64,2048]{1,0:T(8,128)} %collective-permute-done.74), channel_id=1, source_target_pairs={{0,1},{1,0},{2,3},{3,2},{4,5},{5,4},{6,7},{7,6},{8,9},{9,8},{10,11... | collective-permute-start | bytes 1572872 | tf_op jit(solution)/shard_map/ppermute | solution.py:119
  495.4 21.2 %all-to-all-start.1 = ((f32[8,1,1856]{2,1,0:T(1,128)}), f32[8,1,1856]{2,1,0:T(1,128)S(1)}, u32[]{:S(2)}, u32[]{:S(2)}) async-start(f32[8,1,1856]{2,1,0:T(1,128)} %all_to_all.14), calls=%async_computation.1 | async-start | bytes 122880 | tf_op jit(solution)/shard_map/all_to_all | solution.py:1023
  501.9 21.8 %collective-permute-start.77 = (bf16[64,2048]{1,0:T(8,128)(2,1)S(1)}, bf16[64,2048]{1,0:T(8,128)(2,1)S(1)}, u32[]{:S(2)}, u32[]{:S(2)}) collective-permute-start(bf16[64,2048]{1,0:T(8,128)(2,1)S(1)} %get-tuple-element.292), channel_id=1, source_target_pairs={{0,16},{4,20},{8,24},{12,28},{16,0},{20,4},{24,8},{28,12},{1,17},{... | collective-permute-start | bytes 786440 | tf_op jit(solution)/shard_map/ppermute | solution.py:492
  (87 other events, 1102.9 us)

commit v3 on v2

--- a/solution.py
+++ b/solution.py
@@ -717,12 +717,12 @@
         compiler_params=big,
         cost_estimate=cost(2 * row_count * model_width * local_width, 5 << 20),
         name="output_product",
-    )(labels, rank_array, after(heads_out, *fc_received[1:], fc_theirs[0]), coefficients, head_vectors, *out_blocks)
-    branch = side_sum(core_sum(away, kept))
+    )(labels, rank_array, after(heads_out, *fc_received[1:3], fc_theirs[0]), coefficients, head_vectors, *out_blocks)
+    branch = side_sum(after(core_sum(away, kept), fc_received[3]))
     middle = my_rows(tokens).astype(f32) + branch + model_vectors[4]
     normed_mid, hat_mid, inverse_mid = norm_rows(middle, model_vectors[1], model_vectors[3])
 
-    cotangent_near = after(jnp.concatenate(cotangent_rows, axis=0), branch)
+    cotangent_near = after(jnp.concatenate(cotangent_rows, axis=0), fc_received[3])
     cotangent_near = jnp.concatenate([cotangent_near, tp_send(cotangent_near, 2)], axis=0)
     grad_out_all = (cotangent_near, tp_send(cotangent_near, 1))
     normed_mid_all = rows_gather(
@@ -896,7 +896,7 @@
         name="attention_backward",
     )(
         limits,
-        after(grad_post_attn, fc_spread[0]),
+        grad_post_attn,
         heads_out,
         coefficients,
         head_vectors,

time: 554 us -> 537 us (0.969)
  starting transfers between devices: 112 us -> 92.5 us
    ppermute x21, starting transfers between devices: 50 us -> 30.7 us  [group_send(): lax.ppermute(block, 'fsdp', [(g * others + o, (g + shift) % GROUPS * othe...]
    ppermute x21, waiting for transfers between devices: 65 us -> 51.6 us  [group_send(): lax.ppermute(block, 'fsdp', [(g * others + o, (g + shift) % GROUPS * othe...]
    ppermute x16, waiting for transfers between devices: 74 us -> 85 us  [send(): lax.ppermute(block, 'fsdp', self.forward if way > 0 else self.backward)]
    unnamed x119 -> x123, local copies, waits for them, and re-layouts: 13.7 us -> 14.6 us
  transfers between devices with their start and end apart: 87 -> 87, of which waited for: 38 -> 43; matrix products, arithmetic and copies ran while one was open for 14% -> 15% of each run, Pallas kernels for 15% -> 16%
where the time goes in v3:
time: 537 us; the launch traced here: 527 us
  waiting for transfers between devices  233 us (43%)
  Pallas kernels  99 us (18%)
  starting transfers between devices  92.5 us (17%)
  other arithmetic  54.6 us (10%)
  local copies, waits for them, and re-layouts  45.6 us (8%)
    ppermute x16, waiting for transfers between devices, send(): lax.ppermute(block, 'fsdp', self.forward if way > 0 else self.backward)  85 us
    ppermute x39, waiting for transfers between devices, tp_send(): return lax.ppermute(block, 'tp', [(i, i ^ mask) for i in range(4)])  75.4 us
    ppermute x21, waiting for transfers between devices, group_send(): lax.ppermute(block, 'fsdp', [(g * others + o, (g + shift) % GROUPS * othe...  51.6 us
    ppermute x21, starting transfers between devices, group_send(): lax.ppermute(block, 'fsdp', [(g * others + o, (g + shift) % GROUPS * othe...  30.7 us
    ppermute x39, starting transfers between devices, tp_send(): return lax.ppermute(block, 'tp', [(i, i ^ mask) for i in range(4)])  26 us
    ppermute x16, starting transfers between devices, send(): lax.ppermute(block, 'fsdp', self.forward if way > 0 else self.backward)  18.9 us
    pallas_call x2, Pallas kernels, fc_gradient(): pl.pallas_call(ffn_gradient, grid_spec=pltpu.PrefetchScalarGridSpec(num_s...  15.6 us
    unnamed x123, local copies, waits for them, and re-layouts  14.6 us
  transfers between devices with their start and end apart: 87, of which 43 were waited for; matrix products, arithmetic and copies ran while one was open for 15% of the time, Pallas kernels for 16%

profile of v3, /device:TPU:0, one launch (start us, length us, event | category | flops | bytes accessed | tf_op | source)
XLA Modules:
  0.0 526.9 jit_solution(12862743558196490780)
XLA Ops:
  3.1 3.1 collective-permute-start
  6.2 23.1 %collective-permute-done.refs_8_.refs_7_ = bf16[1024,512]{1,0:T(8,128)(2,1)S(1)} collective-permute-done((bf16[1024,512]{1,0:T(8,128)(2,1)S(1)}, bf16[1024,512]{1,0:T(8,128)(2,1)S(1)}, u32[]{:S(2)}, u32[]{:S(2)}) %collective-permute-start) | collective-permute-done | bytes 1048608 | tf_op jit(solution)/shard_map/ppermute | solution.py:63
  35.3 4.8 all-to-all-start
  46.4 8.4 %collective-permute-done.2.refs_7_.refs_6_ = bf16[1024,512]{1,0:T(8,128)(2,1)} collective-permute-done((bf16[1024,512]{1,0:T(8,128)(2,1)S(1)}, bf16[1024,512]{1,0:T(8,128)(2,1)}, u32[]{:S(2)}, u32[]{:S(2)}) %collective-permute-start.2) | collective-permute-done | bytes 1048608 | tf_op jit(solution)/shard_map/ppermute | solution.py:63
  63.2 15.4 %collective-permute-done.4.refs_6_.refs_5_ = bf16[1024,512]{1,0:T(8,128)(2,1)S(1)} collective-permute-done((bf16[1024,512]{1,0:T(8,128)(2,1)}, bf16[1024,512]{1,0:T(8,128)(2,1)S(1)}, u32[]{:S(2)}, u32[]{:S(2)}) %collective-permute-start.4) | collective-permute-done | bytes 1048608 | tf_op jit(solution)/shard_map/ppermute | solution.py:63
  92.9 12.5 %collective-permute-done.7.refs_5_.refs_4_ = bf16[512,512]{1,0:T(8,128)(2,1)S(1)} collective-permute-done((bf16[512,512]{1,0:T(8,128)(2,1)}, bf16[512,512]{1,0:T(8,128)(2,1)S(1)}, u32[]{:S(2)}, u32[]{:S(2)}) %collective-permute-start.7) | collective-permute-done | bytes 524320 | tf_op jit(solution)/shard_map/ppermute | solution.py:63
  106.2 11.0 %attention_forward.1 = (bf16[256,512]{1,0:T(8,128)(2,1)}, bf16[256,512]{1,0:T(8,128)(2,1)}, bf16[256,512]{1,0:T(8,128)(2,1)}, f32[256,512]{1,0:T(8,128)}, f32[256,128]{1,0:T(8,128)}) custom-call(s32[8]{0:T(128)} %get-tuple-element.325.labels, s32[2]{0:T(128)} %broadcast_add_fusion.limits, bf16[256,2048]{1,0:T(8,128)(2,1)} %fusion.3.x, ...), custom_call_target="tpu_custom_call" | custom-call | flops 1610612736 | bytes 12582912 | tf_op jit(solution)/shard_map/attention_forward/pallas_call | solution.py:676
  121.6 3.0 collective-permute-done.12
  128.5 4.4 output_product.1
  133.8 12.9 %collective-permute-done.15.refs_3_ = bf16[512,512]{1,0:T(8,128)(2,1)S(1)} collective-permute-done((bf16[512,512]{1,0:T(8,128)(2,1)}, bf16[512,512]{1,0:T(8,128)(2,1)S(1)}, u32[]{:S(2)}, u32[]{:S(2)}) %collective-permute-start.15) | collective-permute-done | bytes 524320 | tf_op jit(solution)/shard_map/ppermute | solution.py:492
  153.5 4.3 collective-permute-done.17
  157.9 9.8 %collective-permute-done.18 = bf16[64,2048]{1,0:T(8,128)(2,1)} collective-permute-done((bf16[64,2048]{1,0:T(8,128)(2,1)S(1)}, bf16[64,2048]{1,0:T(8,128)(2,1)}, u32[]{:S(2)}, u32[]{:S(2)}) %collective-permute-start.18) | collective-permute-done | bytes 262176 | tf_op jit(solution)/shard_map/ppermute | solution.py:492
  170.4 5.8 %collective-permute-start.20 = (bf16[64,2048]{1,0:T(8,128)(2,1)S(1)}, bf16[64,2048]{1,0:T(8,128)(2,1)S(1)}, u32[]{:S(2)}, u32[]{:S(2)}) collective-permute-start(bf16[64,2048]{1,0:T(8,128)(2,1)S(1)} %add_convert_fusion.4), channel_id=1, source_target_pairs={{0,8},{4,12},{8,16},{12,20},{16,24},{20,28},{24,0},{28,4},{1,9},{5... | collective-permute-start | bytes 786440 | tf_op jit(solution)/shard_map/ppermute | solution.py:492
  179.0 3.8 collective-permute-done.20
  186.3 6.0 %collective-permute-done.22 = bf16[64,2048]{1,0:T(8,128)(2,1)S(1)} collective-permute-done((bf16[64,2048]{1,0:T(8,128)(2,1)S(1)}, bf16[64,2048]{1,0:T(8,128)(2,1)S(1)}, u32[]{:S(2)}, u32[]{:S(2)}) %collective-permute-start.22) | collective-permute-done | bytes 262176 | tf_op jit(solution)/shard_map/ppermute | solution.py:492
  193.0 3.2 collective-permute-done.23
  199.1 8.8 %collective-permute-done.30 = bf16[256,2048]{1,0:T(8,128)(2,1)S(1)} collective-permute-done((bf16[256,2048]{1,0:T(8,128)(2,1)S(1)}, bf16[256,2048]{1,0:T(8,128)(2,1)S(1)}, u32[]{:S(2)}, u32[]{:S(2)}) %collective-permute-start.30) | collective-permute-done | bytes 1048608 | tf_op jit(solution)/shard_map/ppermute | solution.py:119
  209.5 4.0 collective-permute-done.24
  215.7 3.4 collective-permute-done.25
  219.8 3.2 collective-permute-done.26
  226.7 7.0 %ffn_forward.2 = (f32[512,512]{1,0:T(8,128)}, f32[512,512]{1,0:T(8,128)}, f32[512,512]{1,0:T(8,128)}, f32[8,512]{1,0:T(8,128)}) custom-call(s32[8]{0:T(128)} %fusion.41.labels, bf16[512,2048]{1,0:T(8,128)(2,1)} %constant_dynamic-update-slice_fusion.x.near_x, bf16[512,2048]{1,0:T(8,128)(2,1)} %copy-done.13, f32[3,512]{1,0:T(4,128)} %bitcast.229, ...), custom_call_target="tpu_custom_call" | custom-call | flops 2147483648 | bytes 10485760 | tf_op jit(solution)/shard_map/ffn_forward/pallas_call | solution.py:743
  234.4 7.0 %ffn_forward.3 = (f32[512,512]{1,0:T(8,128)}, f32[512,512]{1,0:T(8,128)}, f32[512,512]{1,0:T(8,128)}, f32[8,512]{1,0:T(8,128)}) custom-call(s32[8]{0:T(128)} %fusion.41.labels, bf16[512,2048]{1,0:T(8,128)(2,1)} %collective-permute-done.31.x.far_x, bf16[512,2048]{1,0:T(8,128)(2,1)} %collective-permute-done.32.g.far_g, f32[3,512]{1,0:T(4,128)} %bitcast.230, ...), custom_call_target="tpu_custom_call" | custom-call | flops 2147483648 | bytes 10485760 | tf_op jit(solution)/shard_map/ffn_forward/pallas_call | solution.py:743
  255.4 6.1 %ffn_backward.3 = (bf16[512,512]{1,0:T(8,128)(2,1)}, bf16[512,512]{1,0:T(8,128)(2,1)}, bf16[512,2048]{1,0:T(8,128)(2,1)}, f32[8,512]{1,0:T(8,128)}) custom-call(s32[8]{0:T(128)} %fusion.41.labels, f32[8,1024]{1,0:T(8,128)} %add_add_fusion.3.sums, f32[512,512]{1,0:T(8,128)} %get-tuple-element.126.active, f32[512,512]{1,0:T(8,128)} %get-tuple-element.127.slope, ...), custom_call_target="tpu_custom_call" | custom-call | flops 1073741824 | bytes 8388608 | tf_op jit(solution)/shard_map/ffn_backward/pallas_call | solution.py:760
  264.6 6.1 %ffn_backward.2 = (bf16[512,512]{1,0:T(8,128)(2,1)}, bf16[512,512]{1,0:T(8,128)(2,1)}, bf16[512,2048]{1,0:T(8,128)(2,1)}, f32[8,512]{1,0:T(8,128)}) custom-call(s32[8]{0:T(128)} %fusion.41.labels, f32[8,1024]{1,0:T(8,128)} %add_add_fusion.3.sums, f32[512,512]{1,0:T(8,128)} %get-tuple-element.122.active, f32[512,512]{1,0:T(8,128)} %get-tuple-element.123.slope, ...), custom_call_target="tpu_custom_call" | custom-call | flops 1073741824 | bytes 8388608 | tf_op jit(solution)/shard_map/ffn_backward/pallas_call | solution.py:760
  278.6 7.7 %ffn_gradient.3 = (bf16[512,512]{1,0:T(8,128)(2,1)}, bf16[512,512]{1,0:T(8,128)(2,1)}, bf16[512,512]{1,0:T(8,128)(2,1)}, bf16[512,512]{1,0:T(8,128)(2,1)}) custom-call(s32[4]{0:T(128)} %get-tuple-element.333.labels, bf16[512,2048]{1,0:T(8,128)(2,1)} %constant_dynamic-update-slice_fusion.x.near_x, bf16[512,2048]{1,0:T(8,128)(2,1)} %collective-permute-done.31.x.far_x, ...), custom_call_target="tpu_custom_call" | custom-call | flops 2147483648 | bytes 9437184 | tf_op jit(solution)/shard_map/ffn_gradient/pallas_call | solution.py:797
  292.8 3.6 collective-permute-done.48
  305.1 7.8 %ffn_gradient.2 = (bf16[512,512]{1,0:T(8,128)(2,1)}, bf16[512,512]{1,0:T(8,128)(2,1)}, bf16[512,512]{1,0:T(8,128)(2,1)}, bf16[512,512]{1,0:T(8,128)(2,1)}) custom-call(s32[4]{0:T(128)} %get-tuple-element.332.labels, bf16[512,2048]{1,0:T(8,128)(2,1)} %constant_dynamic-update-slice_fusion.x.near_x, bf16[512,2048]{1,0:T(8,128)(2,1)} %collective-permute-done.31.x.far_x, ...), custom_call_target="tpu_custom_call" | custom-call | flops 2147483648 | bytes 9437184 | tf_op jit(solution)/shard_map/ffn_gradient/pallas_call | solution.py:797
  314.8 9.1 %collective-permute-done.44 = bf16[512,512]{1,0:T(8,128)(2,1)S(1)} collective-permute-done((bf16[512,512]{1,0:T(8,128)(2,1)}, bf16[512,512]{1,0:T(8,128)(2,1)S(1)}, u32[]{:S(2)}, u32[]{:S(2)}) %collective-permute-start.44) | collective-permute-done | bytes 524320 | tf_op jit(solution)/shard_map/ppermute | solution.py:506
  334.2 3.6 output_back.1
  341.9 3.6 collective-permute-done.56
  348.6 5.4 %attention_backward.1 = (bf16[256,512]{1,0:T(8,128)(2,1)S(1)}, bf16[256,512]{1,0:T(8,128)(2,1)S(1)}, bf16[256,512]{1,0:T(8,128)(2,1)S(1)}, f32[8,512]{1,0:T(8,128)S(1)}) custom-call(s32[2]{0:T(128)S(1)} %copy-done.10, f32[256,512]{1,0:T(8,128)S(1)} %copy-done.5, f32[256,512]{1,0:T(8,128)S(1)} %copy-done, f32[256,4]{1,0:T(8,128)S(1)} %copy.57.coefficients, ...), custom_call_target="tpu_custom_call" | custom-call | flops 335544320 | bytes 4194304 | tf_op jit(solution)/shard_map/attention_backward/pallas_call | solution.py:875
  356.1 3.3 projection_gradient_far.1
  361.5 4.2 ffn_product.3
  365.6 4.2 ffn_product.2
  369.9 8.9 %projection_gradient.1 = bf16[7,1024,512]{2,1,0:T(8,128)(2,1)} custom-call(s32[7]{0:T(128)} %fusion.44.labels, bf16[256,2048]{1,0:T(8,128)(2,1)} %fusion.3.x, bf16[256,2048]{1,0:T(8,128)(2,1)} %pad_maximum_fusion.3.grad, bf16[256,512]{1,0:T(8,128)(2,1)} %copy-done.1, bf16[256,512]{1,0:T(8,128)(2,1)} %copy-done.2, bf16[256,512]{1,0:T(8,128)(2,1)} %copy-done.3, ...), custom_call_target="tpu_custom_call" | custom-call | flops 1879048192 | bytes 7340032 | tf_op jit(solution)/shard_map/projection_gradient/pallas_call | solution.py:909
  380.1 5.8 %collective-permute-done.59 = bf16[512,512]{1,0:T(8,128)(2,1)S(1)} collective-permute-done((bf16[512,512]{1,0:T(8,128)(2,1)}, bf16[512,512]{1,0:T(8,128)(2,1)S(1)}, u32[]{:S(2)}, u32[]{:S(2)}) %collective-permute-start.59) | collective-permute-done | bytes 524320 | tf_op jit(solution)/shard_map/ppermute | solution.py:63
  391.5 8.2 %projection_back.1 = (bf16[128,2048]{1,0:T(8,128)(2,1)}, f32[128,2048]{1,0:T(8,128)}) custom-call(s32[8]{0:T(128)} %get-tuple-element.325.labels, s32[1]{0:T(128)} %bitcast.1.rank, bf16[256,512]{1,0:T(8,128)(2,1)} %copy-done.1, bf16[256,512]{1,0:T(8,128)(2,1)} %copy-done.2, bf16[256,512]{1,0:T(8,128)(2,1)} %copy-done.3, bf16[1024,512]{1,0:T(8,128)(2,1)} %copy-done.11, ...), custom_call_target="tpu_custom_call" | custom-call | flops 1610612736 | bytes 10485760 | tf_op jit(solution)/shard_map/projection_back/pallas_call | solution.py:972
  402.2 13.3 %collective-permute-done.64 = bf16[1024,512]{1,0:T(8,128)(2,1)} collective-permute-done((bf16[1024,512]{1,0:T(8,128)(2,1)}, bf16[1024,512]{1,0:T(8,128)(2,1)}, u32[]{:S(2)}, u32[]{:S(2)}) %collective-permute-start.64) | collective-permute-done | bytes 1048608 | tf_op jit(solution)/shard_map/ppermute | solution.py:63
  417.2 4.2 fusion.7
  429.3 3.9 ffn_placed.1
  436.8 19.8 %collective-permute-done.69 = f32[6,2048]{1,0:T(8,128)S(1)} collective-permute-done((f32[6,2048]{1,0:T(8,128)S(1)}, f32[6,2048]{1,0:T(8,128)S(1)}, u32[]{:S(2)}, u32[]{:S(2)}) %collective-permute-start.69) | collective-permute-done | bytes 49184 | tf_op jit(solution)/shard_map/ppermute | solution.py:119
  458.8 4.1 fusion.5
  467.4 10.2 %collective-permute-done.74 = f32[64,2048]{1,0:T(8,128)} collective-permute-done((f32[64,2048]{1,0:T(8,128)}, f32[64,2048]{1,0:T(8,128)}, u32[]{:S(2)}, u32[]{:S(2)}) %collective-permute-start.74) | collective-permute-done | bytes 524320 | tf_op jit(solution)/shard_map/ppermute | solution.py:119
  478.2 5.7 %all-to-all-start.1 = ((f32[8,1,1856]{2,1,0:T(1,128)}), f32[8,1,1856]{2,1,0:T(1,128)S(1)}, u32[]{:S(2)}, u32[]{:S(2)}) async-start(f32[8,1,1856]{2,1,0:T(1,128)} %all_to_all.14), calls=%async_computation.1 | async-start | bytes 122880 | tf_op jit(solution)/shard_map/all_to_all | solution.py:1023
  488.0 11.7 %all-to-all-done.1 = f32[8,1,1856]{2,1,0:T(1,128)S(1)} async-done(((f32[8,1,1856]{2,1,0:T(1,128)}), f32[8,1,1856]{2,1,0:T(1,128)S(1)}, u32[]{:S(2)}, u32[]{:S(2)}) %all-to-all-start.1) | async-done | bytes 59424 | tf_op jit(solution)/shard_map/all_to_all | solution.py:1023
  499.9 3.8 collective-permute-start.78
  506.9 3.2 collective-permute-done.78
  510.1 3.9 collective-permute-done.79
  (401 shorter events, 188.1 us)
Async XLA Ops:
  3.1 26.2 %collective-permute-start = (bf16[1024,512]{1,0:T(8,128)(2,1)S(1)}, bf16[1024,512]{1,0:T(8,128)(2,1)S(1)}, u32[]{:S(2)}, u32[]{:S(2)}) collective-permute-start(bf16[1024,512]{1,0:T(8,128)(2,1)S(1)} %pad_maximum_fusion.1.refs_0_), channel_id=1, source_target_pairs={{0,8},{8,16},{16,24},{24,28},{28,20},{20,12},{12,4},{4,0},{1,9},{9... | collective-permute-start | bytes 3145736 | tf_op jit(solution)/shard_map/ppermute | solution.py:63
  6.2 24.6 %collective-permute-start.1 = (bf16[1024,512]{1,0:T(8,128)(2,1)S(1)}, bf16[1024,512]{1,0:T(8,128)(2,1)S(1)}, u32[]{:S(2)}, u32[]{:S(2)}) collective-permute-start(bf16[1024,512]{1,0:T(8,128)(2,1)S(1)} %pad_maximum_fusion.1.refs_0_), channel_id=1, source_target_pairs={{8,0},{16,8},{24,16},{28,24},{20,28},{12,20},{4,12},{0,4},{9,1},{1... | collective-permute-start | bytes 3145736 | tf_op jit(solution)/shard_map/ppermute | solution.py:63
  30.8 24.0 %collective-permute-start.2 = (bf16[1024,512]{1,0:T(8,128)(2,1)S(1)}, bf16[1024,512]{1,0:T(8,128)(2,1)}, u32[]{:S(2)}, u32[]{:S(2)}) collective-permute-start(bf16[1024,512]{1,0:T(8,128)(2,1)S(1)} %collective-permute-done.refs_8_.refs_7_), channel_id=1, source_target_pairs={{0,8},{8,16},{16,24},{24,28},{28,20},{20,12},{12,4},{4,0},{1,9},{9... | collective-permute-start | bytes 3145736 | tf_op jit(solution)/shard_map/ppermute | solution.py:63
  32.4 23.9 %collective-permute-start.3 = (bf16[1024,512]{1,0:T(8,128)(2,1)S(1)}, bf16[1024,512]{1,0:T(8,128)(2,1)}, u32[]{:S(2)}, u32[]{:S(2)}) collective-permute-start(bf16[1024,512]{1,0:T(8,128)(2,1)S(1)} %collective-permute-done.1.refs_1_), channel_id=1, source_target_pairs={{8,0},{16,8},{24,16},{28,24},{20,28},{12,20},{4,12},{0,4},{9,1},{1... | collective-permute-start | bytes 3145736 | tf_op jit(solution)/shard_map/ppermute | solution.py:63
  35.3 27.7 %all-to-all-start = ((bf16[8,2,1312]{2,1,0:T(2,128)(2,1)}), bf16[8,2,1312]{2,1,0:T(2,128)(2,1)S(1)}, u32[]{:S(2)}, u32[]{:S(2)}) async-start(bf16[8,2,1312]{2,1,0:T(2,128)(2,1)} %reshape.370), calls=%async_computation | async-start | bytes 90112 | tf_op jit(solution)/shard_map/all_to_all | solution.py:540
  56.3 22.4 %collective-permute-start.4 = (bf16[1024,512]{1,0:T(8,128)(2,1)}, bf16[1024,512]{1,0:T(8,128)(2,1)S(1)}, u32[]{:S(2)}, u32[]{:S(2)}) collective-permute-start(bf16[1024,512]{1,0:T(8,128)(2,1)} %collective-permute-done.2.refs_7_.refs_6_), channel_id=1, source_target_pairs={{0,8},{8,16},{16,24},{24,28},{28,20},{20,12},{12,4},{4,0},{1,9},{9... | collective-permute-start | bytes 3145736 | tf_op jit(solution)/shard_map/ppermute | solution.py:63
  58.0 22.4 %collective-permute-start.5 = (bf16[1024,512]{1,0:T(8,128)(2,1)}, bf16[1024,512]{1,0:T(8,128)(2,1)S(1)}, u32[]{:S(2)}, u32[]{:S(2)}) collective-permute-start(bf16[1024,512]{1,0:T(8,128)(2,1)} %collective-permute-done.3.refs_2_), channel_id=1, source_target_pairs={{8,0},{16,8},{24,16},{28,24},{20,28},{12,20},{4,12},{0,4},{9,1},{1... | collective-permute-start | bytes 3145736 | tf_op jit(solution)/shard_map/ppermute | solution.py:63
  81.3 24.1 %collective-permute-start.7 = (bf16[512,512]{1,0:T(8,128)(2,1)}, bf16[512,512]{1,0:T(8,128)(2,1)S(1)}, u32[]{:S(2)}, u32[]{:S(2)}) collective-permute-start(bf16[512,512]{1,0:T(8,128)(2,1)} %slice.297), channel_id=1, source_target_pairs={{8,0},{16,8},{24,16},{28,24},{20,28},{12,20},{4,12},{0,4},{9,1},{1... | collective-permute-start | bytes 1572872 | tf_op jit(solution)/shard_map/ppermute | solution.py:63
  82.4 23.0 %collective-permute-start.6 = (bf16[512,512]{1,0:T(8,128)(2,1)}, bf16[512,512]{1,0:T(8,128)(2,1)}, u32[]{:S(2)}, u32[]{:S(2)}) collective-permute-start(bf16[512,512]{1,0:T(8,128)(2,1)} %slice.296), channel_id=1, source_target_pairs={{0,8},{8,16},{16,24},{24,28},{28,20},{20,12},{12,4},{4,0},{1,9},{9... | collective-permute-start | bytes 1572872 | tf_op jit(solution)/shard_map/ppermute | solution.py:63
  88.0 31.8 %collective-permute-start.10 = (bf16[512,512]{1,0:T(8,128)(2,1)S(1)}, bf16[512,512]{1,0:T(8,128)(2,1)S(1)}, u32[]{:S(2)}, u32[]{:S(2)}) collective-permute-start(bf16[512,512]{1,0:T(8,128)(2,1)S(1)} %get-tuple-element.283.refs_0_), channel_id=1, source_target_pairs={{0,4},{4,0},{8,12},{12,8},{16,20},{20,16},{24,28},{28,24},{1,5},{5... | collective-permute-start | bytes 1572872 | tf_op jit(solution)/shard_map/ppermute | solution.py:506
  88.3 31.8 %collective-permute-start.8 = (bf16[512,512]{1,0:T(8,128)(2,1)}, bf16[512,512]{1,0:T(8,128)(2,1)}, u32[]{:S(2)}, u32[]{:S(2)}) collective-permute-start(bf16[512,512]{1,0:T(8,128)(2,1)} %get-tuple-element.285), channel_id=1, source_target_pairs={{0,8},{4,12},{8,16},{12,20},{16,24},{20,28},{24,0},{28,4},{1,9},{5... | collective-permute-start | bytes 1572872 | tf_op jit(solution)/shard_map/ppermute | solution.py:492
  89.4 32.2 %collective-permute-start.9 = (bf16[512,512]{1,0:T(8,128)(2,1)}, bf16[512,512]{1,0:T(8,128)(2,1)S(1)}, u32[]{:S(2)}, u32[]{:S(2)}) collective-permute-start(bf16[512,512]{1,0:T(8,128)(2,1)} %get-tuple-element.284), channel_id=1, source_target_pairs={{0,24},{4,28},{8,0},{12,4},{16,8},{20,12},{24,16},{28,20},{1,25},{... | collective-permute-start | bytes 1572872 | tf_op jit(solution)/shard_map/ppermute | solution.py:492
  120.1 26.5 %collective-permute-start.15 = (bf16[512,512]{1,0:T(8,128)(2,1)}, bf16[512,512]{1,0:T(8,128)(2,1)S(1)}, u32[]{:S(2)}, u32[]{:S(2)}) collective-permute-start(bf16[512,512]{1,0:T(8,128)(2,1)} %get-tuple-element.282), channel_id=1, source_target_pairs={{0,16},{4,20},{8,24},{12,28},{16,0},{20,4},{24,8},{28,12},{1,17},{... | collective-permute-start | bytes 1572872 | tf_op jit(solution)/shard_map/ppermute | solution.py:492
  132.9 17.5 %collective-permute-start.14 = (bf16[128,2048]{1,0:T(8,128)(2,1)}, bf16[128,2048]{1,0:T(8,128)(2,1)S(1)}, u32[]{:S(2)}, u32[]{:S(2)}) collective-permute-start(bf16[128,2048]{1,0:T(8,128)(2,1)} %get-tuple-element.113), channel_id=1, source_target_pairs={{0,1},{1,0},{2,3},{3,2},{4,5},{5,4},{6,7},{7,6},{8,9},{9,8},{10,11... | collective-permute-start | bytes 1572872 | tf_op jit(solution)/shard_map/ppermute | solution.py:119
  146.6 21.0 %collective-permute-start.18 = (bf16[64,2048]{1,0:T(8,128)(2,1)S(1)}, bf16[64,2048]{1,0:T(8,128)(2,1)}, u32[]{:S(2)}, u32[]{:S(2)}) collective-permute-start(bf16[64,2048]{1,0:T(8,128)(2,1)S(1)} %fusion.30), channel_id=1, source_target_pairs={{0,16},{4,20},{8,24},{12,28},{16,0},{20,4},{24,8},{28,12},{1,17},{... | collective-permute-start | bytes 786440 | tf_op jit(solution)/shard_map/ppermute | solution.py:492
  149.5 18.1 %collective-permute-start.19 = (bf16[64,2048]{1,0:T(8,128)(2,1)S(1)}, bf16[64,2048]{1,0:T(8,128)(2,1)}, u32[]{:S(2)}, u32[]{:S(2)}) collective-permute-start(bf16[64,2048]{1,0:T(8,128)(2,1)S(1)} %fusion.30), channel_id=1, source_target_pairs={{0,24},{4,28},{8,0},{12,4},{16,8},{20,12},{24,16},{28,20},{1,25},{... | collective-permute-start | bytes 786440 | tf_op jit(solution)/shard_map/ppermute | solution.py:492
  151.9 17.0 %collective-permute-start.16 = (bf16[64,2048]{1,0:T(8,128)(2,1)S(1)}, bf16[64,2048]{1,0:T(8,128)(2,1)S(1)}, u32[]{:S(2)}, u32[]{:S(2)}) collective-permute-start(bf16[64,2048]{1,0:T(8,128)(2,1)S(1)} %fusion.31), channel_id=1, source_target_pairs={{0,2},{1,3},{2,0},{3,1},{4,6},{5,7},{6,4},{7,5},{8,10},{9,11},{10,... | collective-permute-start | bytes 786440 | tf_op jit(solution)/shard_map/ppermute | solution.py:119
  153.5 70.3 %collective-permute-start.27 = (bf16[512,512]{1,0:T(8,128)(2,1)}, bf16[512,512]{1,0:T(8,128)(2,1)S(1)}, u32[]{:S(2)}, u32[]{:S(2)}) collective-permute-start(bf16[512,512]{1,0:T(8,128)(2,1)} %collective-permute-done.8.refs_1_), channel_id=1, source_target_pairs={{0,4},{4,0},{8,12},{12,8},{16,20},{20,16},{24,28},{28,24},{1,5},{5... | collective-permute-start | bytes 1572872 | tf_op jit(solution)/shard_map/ppermute | solution.py:506
  177.7 30.1 %collective-permute-start.30 = (bf16[256,2048]{1,0:T(8,128)(2,1)S(1)}, bf16[256,2048]{1,0:T(8,128)(2,1)S(1)}, u32[]{:S(2)}, u32[]{:S(2)}) collective-permute-start(bf16[256,2048]{1,0:T(8,128)(2,1)S(1)} %pad_maximum_fusion.2), channel_id=1, source_target_pairs={{0,2},{1,3},{2,0},{3,1},{4,6},{5,7},{6,4},{7,5},{8,10},{9,11},{10,... | collective-permute-start | bytes 3145736 | tf_op jit(solution)/shard_map/ppermute | solution.py:119
  182.9 40.9 %collective-permute-start.28 = (bf16[512,512]{1,0:T(8,128)(2,1)S(1)}, bf16[512,512]{1,0:T(8,128)(2,1)S(1)}, u32[]{:S(2)}, u32[]{:S(2)}) collective-permute-start(bf16[512,512]{1,0:T(8,128)(2,1)S(1)} %copy-done.19), channel_id=1, source_target_pairs={{0,4},{4,0},{8,12},{12,8},{16,20},{20,16},{24,28},{28,24},{1,5},{5... | collective-permute-start | bytes 1572872 | tf_op jit(solution)/shard_map/ppermute | solution.py:506
  192.3 31.5 %collective-permute-start.29 = (bf16[512,512]{1,0:T(8,128)(2,1)S(1)}, bf16[512,512]{1,0:T(8,128)(2,1)S(1)}, u32[]{:S(2)}, u32[]{:S(2)}) collective-permute-start(bf16[512,512]{1,0:T(8,128)(2,1)S(1)} %copy-done.21), channel_id=1, source_target_pairs={{0,4},{4,0},{8,12},{12,8},{16,20},{20,16},{24,28},{28,24},{1,5},{5... | collective-permute-start | bytes 1572872 | tf_op jit(solution)/shard_map/ppermute | solution.py:506
  196.2 17.2 %collective-permute-start.24 = (bf16[64,2048]{1,0:T(8,128)(2,1)S(1)}, bf16[64,2048]{1,0:T(8,128)(2,1)S(1)}, u32[]{:S(2)}, u32[]{:S(2)}) collective-permute-start(bf16[64,2048]{1,0:T(8,128)(2,1)S(1)} %collective-permute-done.20), channel_id=1, source_target_pairs={{0,2},{1,3},{2,0},{3,1},{4,6},{5,7},{6,4},{7,5},{8,10},{9,11},{10,... | collective-permute-start | bytes 786440 | tf_op jit(solution)/shard_map/ppermute | solution.py:119
  271.4 16.9 %collective-permute-start.45 = (f32[3,256]{1,0:T(4,128)S(1)}, f32[3,256]{1,0:T(4,128)S(1)}, u32[]{:S(2)}, u32[]{:S(2)}) collective-permute-start(f32[3,256]{1,0:T(4,128)S(1)} %bitcast.270), channel_id=1, source_target_pairs={{0,4},{4,0},{8,12},{12,8},{16,20},{20,16},{24,28},{28,24},{1,5},{5... | collective-permute-start | bytes 9224 | tf_op jit(solution)/shard_map/ppermute | solution.py:506
  278.1 18.3 %collective-permute-start.48 = (bf16[64,2048]{1,0:T(8,128)(2,1)S(1)}, bf16[64,2048]{1,0:T(8,128)(2,1)S(1)}, u32[]{:S(2)}, u32[]{:S(2)}) collective-permute-start(bf16[64,2048]{1,0:T(8,128)(2,1)S(1)} %get-tuple-element.279), channel_id=1, source_target_pairs={{0,2},{1,3},{2,0},{3,1},{4,6},{5,7},{6,4},{7,5},{8,10},{9,11},{10,... | collective-permute-start | bytes 786440 | tf_op jit(solution)/shard_map/ppermute | solution.py:119
  289.9 23.1 %collective-permute-start.43 = (bf16[512,512]{1,0:T(8,128)(2,1)}, bf16[512,512]{1,0:T(8,128)(2,1)S(1)}, u32[]{:S(2)}, u32[]{:S(2)}) collective-permute-start(bf16[512,512]{1,0:T(8,128)(2,1)} %get-tuple-element.140), channel_id=1, source_target_pairs={{0,4},{4,0},{8,12},{12,8},{16,20},{20,16},{24,28},{28,24},{1,5},{5... | collective-permute-start | bytes 1572872 | tf_op jit(solution)/shard_map/ppermute | solution.py:506
  290.8 33.1 %collective-permute-start.44 = (bf16[512,512]{1,0:T(8,128)(2,1)}, bf16[512,512]{1,0:T(8,128)(2,1)S(1)}, u32[]{:S(2)}, u32[]{:S(2)}) collective-permute-start(bf16[512,512]{1,0:T(8,128)(2,1)} %get-tuple-element.141), channel_id=1, source_target_pairs={{0,4},{4,0},{8,12},{12,8},{16,20},{20,16},{24,28},{28,24},{1,5},{5... | collective-permute-start | bytes 1572872 | tf_op jit(solution)/shard_map/ppermute | solution.py:506
  298.0 25.9 %collective-permute-start.49 = (bf16[64,2048]{1,0:T(8,128)(2,1)S(1)}, bf16[64,2048]{1,0:T(8,128)(2,1)S(1)}, u32[]{:S(2)}, u32[]{:S(2)}) collective-permute-start(bf16[64,2048]{1,0:T(8,128)(2,1)S(1)} %get-tuple-element.146), channel_id=1, source_target_pairs={{0,24},{4,28},{8,0},{12,4},{16,8},{20,12},{24,16},{28,20},{1,25},{... | collective-permute-start | bytes 786440 | tf_op jit(solution)/shard_map/ppermute | solution.py:492
  301.6 22.3 %collective-permute-start.50 = (bf16[64,2048]{1,0:T(8,128)(2,1)S(1)}, bf16[64,2048]{1,0:T(8,128)(2,1)S(1)}, u32[]{:S(2)}, u32[]{:S(2)}) collective-permute-start(bf16[64,2048]{1,0:T(8,128)(2,1)S(1)} %get-tuple-element.147), channel_id=1, source_target_pairs={{0,8},{4,12},{8,16},{12,20},{16,24},{20,28},{24,0},{28,4},{1,9},{5... | collective-permute-start | bytes 786440 | tf_op jit(solution)/shard_map/ppermute | solution.py:492
  302.5 21.4 %collective-permute-start.46 = (bf16[64,2048]{1,0:T(8,128)(2,1)S(1)}, bf16[64,2048]{1,0:T(8,128)(2,1)S(1)}, u32[]{:S(2)}, u32[]{:S(2)}) collective-permute-start(bf16[64,2048]{1,0:T(8,128)(2,1)S(1)} %get-tuple-element.271), channel_id=1, source_target_pairs={{0,16},{4,20},{8,24},{12,28},{16,0},{20,4},{24,8},{28,12},{1,17},{... | collective-permute-start | bytes 786440 | tf_op jit(solution)/shard_map/ppermute | solution.py:492
  313.0 21.3 %collective-permute-start.54 = (bf16[512,512]{1,0:T(8,128)(2,1)}, bf16[512,512]{1,0:T(8,128)(2,1)S(1)}, u32[]{:S(2)}, u32[]{:S(2)}) collective-permute-start(bf16[512,512]{1,0:T(8,128)(2,1)} %get-tuple-element.145), channel_id=1, source_target_pairs={{0,4},{4,0},{8,12},{12,8},{16,20},{20,16},{24,28},{28,24},{1,5},{5... | collective-permute-start | bytes 1572872 | tf_op jit(solution)/shard_map/ppermute | solution.py:506
  327.3 52.8 %collective-permute-start.62 = (bf16[512,512]{1,0:T(8,128)(2,1)}, bf16[512,512]{1,0:T(8,128)(2,1)}, u32[]{:S(2)}, u32[]{:S(2)}) collective-permute-start(bf16[512,512]{1,0:T(8,128)(2,1)} %add_convert_fusion.1), channel_id=1, source_target_pairs={{0,24},{4,28},{8,0},{12,4},{16,8},{20,12},{24,16},{28,20},{1,25},{... | collective-permute-start | bytes 1572872 | tf_op jit(solution)/shard_map/ppermute | solution.py:492
  330.1 50.0 %collective-permute-start.61 = (bf16[512,512]{1,0:T(8,128)(2,1)}, bf16[512,512]{1,0:T(8,128)(2,1)}, u32[]{:S(2)}, u32[]{:S(2)}) collective-permute-start(bf16[512,512]{1,0:T(8,128)(2,1)} %add_convert_fusion.2), channel_id=1, source_target_pairs={{0,8},{4,12},{8,16},{12,20},{16,24},{20,28},{24,0},{28,4},{1,9},{5... | collective-permute-start | bytes 1572872 | tf_op jit(solution)/shard_map/ppermute | solution.py:492
  341.9 38.2 %collective-permute-start.60 = (bf16[512,512]{1,0:T(8,128)(2,1)}, bf16[512,512]{1,0:T(8,128)(2,1)}, u32[]{:S(2)}, u32[]{:S(2)}) collective-permute-start(bf16[512,512]{1,0:T(8,128)(2,1)} %add_convert_fusion.3), channel_id=1, source_target_pairs={{0,16},{4,20},{8,24},{12,28},{16,0},{20,4},{24,8},{28,12},{1,17},{... | collective-permute-start | bytes 1572872 | tf_op jit(solution)/shard_map/ppermute | solution.py:492
  359.4 20.7 %collective-permute-start.58 = (bf16[512,512]{1,0:T(8,128)(2,1)}, bf16[512,512]{1,0:T(8,128)(2,1)S(1)}, u32[]{:S(2)}, u32[]{:S(2)}) collective-permute-start(bf16[512,512]{1,0:T(8,128)(2,1)} %get-tuple-element.158), channel_id=1, source_target_pairs={{0,8},{8,16},{16,24},{24,28},{28,20},{20,12},{12,4},{4,0},{1,9},{9... | collective-permute-start | bytes 1572872 | tf_op jit(solution)/shard_map/ppermute | solution.py:63
  360.1 25.8 %collective-permute-start.59 = (bf16[512,512]{1,0:T(8,128)(2,1)}, bf16[512,512]{1,0:T(8,128)(2,1)S(1)}, u32[]{:S(2)}, u32[]{:S(2)}) collective-permute-start(bf16[512,512]{1,0:T(8,128)(2,1)} %get-tuple-element.159), channel_id=1, source_target_pairs={{8,0},{16,8},{24,16},{28,24},{20,28},{12,20},{4,12},{0,4},{9,1},{1... | collective-permute-start | bytes 1572872 | tf_op jit(solution)/shard_map/ppermute | solution.py:63
  389.5 26.0 %collective-permute-start.64 = (bf16[1024,512]{1,0:T(8,128)(2,1)}, bf16[1024,512]{1,0:T(8,128)(2,1)}, u32[]{:S(2)}, u32[]{:S(2)}) collective-permute-start(bf16[1024,512]{1,0:T(8,128)(2,1)} %pad_maximum_fusion.5), channel_id=1, source_target_pairs={{8,0},{16,8},{24,16},{28,24},{20,28},{12,20},{4,12},{0,4},{9,1},{1... | collective-permute-start | bytes 3145736 | tf_op jit(solution)/shard_map/ppermute | solution.py:63
  390.7 26.5 %collective-permute-start.63 = (bf16[1024,512]{1,0:T(8,128)(2,1)}, bf16[1024,512]{1,0:T(8,128)(2,1)}, u32[]{:S(2)}, u32[]{:S(2)}) collective-permute-start(bf16[1024,512]{1,0:T(8,128)(2,1)} %pad_maximum_fusion.4), channel_id=1, source_target_pairs={{0,8},{8,16},{16,24},{24,28},{28,20},{20,12},{12,4},{4,0},{1,9},{9... | collective-permute-start | bytes 3145736 | tf_op jit(solution)/shard_map/ppermute | solution.py:63
  422.6 36.2 %collective-permute-start.72 = (bf16[1024,512]{1,0:T(8,128)(2,1)}, bf16[1024,512]{1,0:T(8,128)(2,1)}, u32[]{:S(2)}, u32[]{:S(2)}) collective-permute-start(bf16[1024,512]{1,0:T(8,128)(2,1)} %get-tuple-element.266), channel_id=1, source_target_pairs={{0,8},{8,16},{16,24},{24,28},{28,20},{20,12},{12,4},{4,0},{1,9},{9... | collective-permute-start | bytes 3145736 | tf_op jit(solution)/shard_map/ppermute | solution.py:63
  425.3 31.2 %collective-permute-start.71 = (bf16[4,64,2048]{2,1,0:T(8,128)(2,1)}, bf16[4,64,2048]{2,1,0:T(8,128)(2,1)}, u32[]{:S(2)}, u32[]{:S(2)}) collective-permute-start(bf16[4,64,2048]{2,1,0:T(8,128)(2,1)} %fusion.10), channel_id=1, source_target_pairs={{0,2},{1,3},{2,0},{3,1},{4,6},{5,7},{6,4},{7,5},{8,10},{9,11},{10,... | collective-permute-start | bytes 3145736 | tf_op jit(solution)/shard_map/ppermute | solution.py:119
  426.7 32.1 %collective-permute-start.73 = (bf16[1024,512]{1,0:T(8,128)(2,1)}, bf16[1024,512]{1,0:T(8,128)(2,1)}, u32[]{:S(2)}, u32[]{:S(2)}) collective-permute-start(bf16[1024,512]{1,0:T(8,128)(2,1)} %get-tuple-element.265), channel_id=1, source_target_pairs={{8,0},{16,8},{24,16},{28,24},{20,28},{12,20},{4,12},{0,4},{9,1},{1... | collective-permute-start | bytes 3145736 | tf_op jit(solution)/shard_map/ppermute | solution.py:63
  433.7 22.8 %collective-permute-start.69 = (f32[6,2048]{1,0:T(8,128)S(1)}, f32[6,2048]{1,0:T(8,128)S(1)}, u32[]{:S(2)}, u32[]{:S(2)}) collective-permute-start(f32[6,2048]{1,0:T(8,128)S(1)} %stack.27), channel_id=1, source_target_pairs={{0,2},{1,3},{2,0},{3,1},{4,6},{5,7},{6,4},{7,5},{8,10},{9,11},{10,... | collective-permute-start | bytes 147464 | tf_op jit(solution)/shard_map/ppermute | solution.py:119
  435.0 21.5 %collective-permute-start.70 = (f32[6,2048]{1,0:T(8,128)S(1)}, f32[6,2048]{1,0:T(8,128)S(1)}, u32[]{:S(2)}, u32[]{:S(2)}) collective-permute-start(f32[6,2048]{1,0:T(8,128)S(1)} %stack.27), channel_id=1, source_target_pairs={{0,3},{1,2},{2,1},{3,0},{4,7},{5,6},{6,5},{7,4},{8,11},{9,10},{10,... | collective-permute-start | bytes 147464 | tf_op jit(solution)/shard_map/ppermute | solution.py:119
  463.8 56.9 %collective-permute-start.83 = (bf16[1024,512]{1,0:T(8,128)(2,1)}, bf16[1024,512]{1,0:T(8,128)(2,1)}, u32[]{:S(2)}, u32[]{:S(2)}) collective-permute-start(bf16[1024,512]{1,0:T(8,128)(2,1)} %get-tuple-element.264), channel_id=1, source_target_pairs={{0,8},{8,16},{16,24},{24,28},{28,20},{20,12},{12,4},{4,0},{1,9},{9... | collective-permute-start | bytes 3145736 | tf_op jit(solution)/shard_map/ppermute | solution.py:63
  465.5 34.3 %collective-permute-start.76 = (f32[64,2048]{1,0:T(8,128)}, f32[64,2048]{1,0:T(8,128)}, u32[]{:S(2)}, u32[]{:S(2)}) collective-permute-start(f32[64,2048]{1,0:T(8,128)} %fusion.23), channel_id=1, source_target_pairs={{0,1},{1,0},{2,3},{3,2},{4,5},{5,4},{6,7},{7,6},{8,9},{9,8},{10,11... | collective-permute-start | bytes 1572872 | tf_op jit(solution)/shard_map/ppermute | solution.py:119
  465.5 55.2 %collective-permute-start.84 = (bf16[1024,512]{1,0:T(8,128)(2,1)}, bf16[1024,512]{1,0:T(8,128)(2,1)}, u32[]{:S(2)}, u32[]{:S(2)}) collective-permute-start(bf16[1024,512]{1,0:T(8,128)(2,1)} %get-tuple-element.263), channel_id=1, source_target_pairs={{8,0},{16,8},{24,16},{28,24},{20,28},{12,20},{4,12},{0,4},{9,1},{1... | collective-permute-start | bytes 3145736 | tf_op jit(solution)/shard_map/ppermute | solution.py:63
  477.6 26.1 %collective-permute-start.75 = (f32[64,2048]{1,0:T(8,128)}, f32[64,2048]{1,0:T(8,128)S(1)}, u32[]{:S(2)}, u32[]{:S(2)}) collective-permute-start(f32[64,2048]{1,0:T(8,128)} %collective-permute-done.74), channel_id=1, source_target_pairs={{0,1},{1,0},{2,3},{3,2},{4,5},{5,4},{6,7},{7,6},{8,9},{9,8},{10,11... | collective-permute-start | bytes 1572872 | tf_op jit(solution)/shard_map/ppermute | solution.py:119
  478.2 21.6 %all-to-all-start.1 = ((f32[8,1,1856]{2,1,0:T(1,128)}), f32[8,1,1856]{2,1,0:T(1,128)S(1)}, u32[]{:S(2)}, u32[]{:S(2)}) async-start(f32[8,1,1856]{2,1,0:T(1,128)} %all_to_all.14), calls=%async_computation.1 | async-start | bytes 122880 | tf_op jit(solution)/shard_map/all_to_all | solution.py:1023
  485.1 21.9 %collective-permute-start.77 = (bf16[64,2048]{1,0:T(8,128)(2,1)S(1)}, bf16[64,2048]{1,0:T(8,128)(2,1)S(1)}, u32[]{:S(2)}, u32[]{:S(2)}) collective-permute-start(bf16[64,2048]{1,0:T(8,128)(2,1)S(1)} %get-tuple-element.291), channel_id=1, source_target_pairs={{0,16},{4,20},{8,24},{12,28},{16,0},{20,4},{24,8},{28,12},{1,17},{... | collective-permute-start | bytes 786440 | tf_op jit(solution)/shard_map/ppermute | solution.py:492
  (89 other events, 953.4 us)

commit v4 on v3

--- a/solution.py
+++ b/solution.py
@@ -69,7 +69,6 @@
         for step in range(1, half):
             onward = self.send(onward, 1)
             backward = self.send(backward, -1)
-            onward, backward = lax.optimization_barrier((onward, backward))
             parts += [(-step, onward), (step, backward)]
         cut = block.shape[0] // 2
         return parts, [self.send(onward[:cut], 1), self.send(backward[cut:], -1)]
@@ -578,7 +577,7 @@
         return {k: total[0, k] + tp_send(total[1, k].astype(bf16), 2).astype(f32) for k in (2, 1, 3, 0)}
 
     def group_total(shares):
-        sent = [group_send(shares[k].astype(bf16), -k).astype(f32) for k in (2, 1, 3)]
+        sent = [group_send(shares[k].astype(bf16), -k).astype(f32) for k in (1, 3, 2)]
         return shares[0], sent
 
     def group_sum(values):
@@ -985,6 +984,9 @@
         results["core"] = group_core(*after(tuple(results["parts"]), token))
         return back_away, back_kept, results["core"]
 
+    def by_block(vectors_in, blocks_in):
+        return vectors_in.reshape(vectors_in.shape[0], blocks_in, -1).transpose(1, 0, 2)
+
     def while_second(token):
         grad_in_normed = side_sum(core_sum(*after(results["back"], token)))
         _, hat_in, inverse_in = norm_rows(
@@ -993,7 +995,7 @@
         grad_token_rows = grad_middle + norm_back_rows(
             grad_in_normed * model_vectors[0], hat_in, inverse_in
         )
-        results["model"] = tp_sum(
+        model_grads = (
             jnp.stack(
                 [
                     jnp.sum(grad_in_normed * hat_in, axis=0),
@@ -1007,25 +1009,22 @@
         )
         results["shares"] = group_shares(after(results["core"], token))
         results["tokens"] = grad_token_rows
-        results["placed"] = place_ffn(token)
-        return [results["model"], results["tokens"], results["shares"]] + list(results["placed"])
-
-    def by_block(vectors_in, blocks_in):
-        return vectors_in.reshape(vectors_in.shape[0], blocks_in, -1).transpose(1, 0, 2)
-
-    def while_third(token):
-        model_grads, token_rows, shares = after(
-            (results["model"], results["tokens"], results["shares"]), token
-        )
         model_blocks = by_block(model_grads, fsdp_size).reshape(fsdp_size, -1)
         head_blocks = by_block(head_sums_back[:5], fsdp_size).reshape(fsdp_size, -1)
         joined = jnp.concatenate([model_blocks, head_blocks], axis=1)
-        joined_s = jnp.sum(lax.all_to_all(joined, "fsdp", 0, 0), axis=0)
-        results["model_s"] = joined_s[: model_blocks.shape[1]].reshape(6, -1)
-        results["head_s"] = joined_s[model_blocks.shape[1] :].reshape(5, -1)
+        results["joined"] = jnp.sum(lax.all_to_all(joined, "fsdp", 0, 0), axis=0)
+        results["placed"] = place_ffn(token)
+        return [results["joined"], results["tokens"], results["shares"]] + list(results["placed"])
+
+    def while_third(token):
+        joined_s, token_rows, shares = after(
+            (results["joined"], results["tokens"], results["shares"]), token
+        )
+        model_size = 6 * model_width // fsdp_size
+        results["model_s"] = tp_sum(joined_s[None, :model_size]).reshape(6, -1)
+        results["head_s"] = joined_s[model_size:].reshape(5, -1)
         results["grad_tokens"] = tp_rows_gather(token_rows, core, side)
         own, sent = group_total(shares)
-        own = after(own, joined_s, results["grad_tokens"])
         second = own + sent[0] + sent[1] + sent[2]
         out_rows = ((middle + second + model_vectors[5]) * my_keep).astype(bf16)
         results["layer_out"] = tp_rows_gather(out_rows, core, side)

time: 537 us -> 533 us (level)
  waiting for transfers between devices: 233 us -> 224 us
  starting transfers between devices: 92.5 us -> 98.4 us
    ppermute x39, waiting for transfers between devices: 75.4 us -> 52.5 us  [tp_send(): return lax.ppermute(block, 'tp', [(i, i ^ mask) for i in range(4)])]
    ppermute x9, starting transfers between devices: 6.38 us -> 15.8 us  [pair_send(): return lax.ppermute(block, 'fsdp', [(f, f ^ 1) for f in range(fsdp_size)])]
    ppermute x21, waiting for transfers between devices: 51.6 us -> 58.8 us  [group_send(): lax.ppermute(block, 'fsdp', [(g * others + o, (g + shift) % GROUPS * othe...]
  transfers between devices with their start and end apart: 87 -> 87, of which waited for: 43 -> 39; matrix products, arithmetic and copies ran while one was open for 15% -> 15% of each run, Pallas kernels for 16% -> 16%
where the time goes in v4:
time: 533 us; the launch traced here: 525 us
  waiting for transfers between devices  224 us (42%)
  Pallas kernels  99.1 us (19%)
  starting transfers between devices  98.4 us (18%)
  other arithmetic  55.1 us (10%)
  local copies, waits for them, and re-layouts  46.2 us (9%)
    ppermute x16, waiting for transfers between devices, send(): lax.ppermute(block, 'fsdp', self.forward if way > 0 else self.backward)  84.9 us
    ppermute x21, waiting for transfers between devices, group_send(): lax.ppermute(block, 'fsdp', [(g * others + o, (g + shift) % GROUPS * othe...  58.8 us
    ppermute x39, waiting for transfers between devices, tp_send(): return lax.ppermute(block, 'tp', [(i, i ^ mask) for i in range(4)])  52.5 us
    ppermute x39, starting transfers between devices, tp_send(): return lax.ppermute(block, 'tp', [(i, i ^ mask) for i in range(4)])  27.4 us
    ppermute x21, starting transfers between devices, group_send(): lax.ppermute(block, 'fsdp', [(g * others + o, (g + shift) % GROUPS * othe...  25.5 us
    ppermute x16, starting transfers between devices, send(): lax.ppermute(block, 'fsdp', self.forward if way > 0 else self.backward)  18.1 us
    all_to_all x1, waiting for transfers between devices, while_second(): results['joined'] = jnp.sum(lax.all_to_all(joined, 'fsdp', 0, 0), axis=0)  16.6 us
    ppermute x9, starting transfers between devices, pair_send(): return lax.ppermute(block, 'fsdp', [(f, f ^ 1) for f in range(fsdp_size)])  15.8 us
  transfers between devices with their start and end apart: 87, of which 39 were waited for; matrix products, arithmetic and copies ran while one was open for 15% of the time, Pallas kernels for 16%

profile of v4, /device:TPU:0, one launch (start us, length us, event | category | flops | bytes accessed | tf_op | source)
XLA Modules:
  0.0 524.8 jit_solution(3230039443950533449)
XLA Ops:
  3.1 3.0 collective-permute-start
  6.2 23.1 %collective-permute-done.refs_1_ = bf16[1024,512]{1,0:T(8,128)(2,1)S(1)} collective-permute-done((bf16[1024,512]{1,0:T(8,128)(2,1)S(1)}, bf16[1024,512]{1,0:T(8,128)(2,1)S(1)}, u32[]{:S(2)}, u32[]{:S(2)}) %collective-permute-start) | collective-permute-done | bytes 1048608 | tf_op jit(solution)/shard_map/ppermute | solution.py:63
  33.8 6.0 %all-to-all-start = ((bf16[8,2,1312]{2,1,0:T(2,128)(2,1)}), bf16[8,2,1312]{2,1,0:T(2,128)(2,1)S(1)}, u32[]{:S(2)}, u32[]{:S(2)}) async-start(bf16[8,2,1312]{2,1,0:T(2,128)(2,1)} %reshape.387), calls=%async_computation | async-start | bytes 90112 | tf_op jit(solution)/shard_map/all_to_all | solution.py:539
  46.1 8.0 %collective-permute-done.1.refs_2_ = bf16[1024,512]{1,0:T(8,128)(2,1)} collective-permute-done((bf16[1024,512]{1,0:T(8,128)(2,1)S(1)}, bf16[1024,512]{1,0:T(8,128)(2,1)}, u32[]{:S(2)}, u32[]{:S(2)}) %collective-permute-start.1) | collective-permute-done | bytes 1048608 | tf_op jit(solution)/shard_map/ppermute | solution.py:63
  61.1 16.5 %collective-permute-done.2.refs_3_ = bf16[1024,512]{1,0:T(8,128)(2,1)S(1)} collective-permute-done((bf16[1024,512]{1,0:T(8,128)(2,1)}, bf16[1024,512]{1,0:T(8,128)(2,1)S(1)}, u32[]{:S(2)}, u32[]{:S(2)}) %collective-permute-start.2) | collective-permute-done | bytes 1048608 | tf_op jit(solution)/shard_map/ppermute | solution.py:63
  90.8 12.7 %collective-permute-done.7.refs_5_.refs_4_ = bf16[512,512]{1,0:T(8,128)(2,1)S(1)} collective-permute-done((bf16[512,512]{1,0:T(8,128)(2,1)}, bf16[512,512]{1,0:T(8,128)(2,1)S(1)}, u32[]{:S(2)}, u32[]{:S(2)}) %collective-permute-start.7) | collective-permute-done | bytes 524320 | tf_op jit(solution)/shard_map/ppermute | solution.py:63
  104.3 11.0 %attention_forward.1 = (bf16[256,512]{1,0:T(8,128)(2,1)}, bf16[256,512]{1,0:T(8,128)(2,1)}, bf16[256,512]{1,0:T(8,128)(2,1)}, f32[256,512]{1,0:T(8,128)}, f32[256,128]{1,0:T(8,128)}) custom-call(s32[8]{0:T(128)} %get-tuple-element.311.labels, s32[2]{0:T(128)} %broadcast_add_fusion.limits, bf16[256,2048]{1,0:T(8,128)(2,1)} %fusion.3.x, ...), custom_call_target="tpu_custom_call" | custom-call | flops 1610612736 | bytes 12582912 | tf_op jit(solution)/shard_map/attention_forward/pallas_call | solution.py:675
  118.3 4.5 collective-permute-done.12
  126.6 4.4 output_product.1
  131.9 11.5 %collective-permute-done.15.refs_3_ = bf16[512,512]{1,0:T(8,128)(2,1)S(1)} collective-permute-done((bf16[512,512]{1,0:T(8,128)(2,1)}, bf16[512,512]{1,0:T(8,128)(2,1)S(1)}, u32[]{:S(2)}, u32[]{:S(2)}) %collective-permute-start.15) | collective-permute-done | bytes 524320 | tf_op jit(solution)/shard_map/ppermute | solution.py:491
  150.1 3.3 collective-permute-start.27
  154.6 10.2 %collective-permute-done.18 = bf16[64,2048]{1,0:T(8,128)(2,1)} collective-permute-done((bf16[64,2048]{1,0:T(8,128)(2,1)S(1)}, bf16[64,2048]{1,0:T(8,128)(2,1)}, u32[]{:S(2)}, u32[]{:S(2)}) %collective-permute-start.18) | collective-permute-done | bytes 262176 | tf_op jit(solution)/shard_map/ppermute | solution.py:491
  167.5 5.3 %collective-permute-start.20 = (bf16[64,2048]{1,0:T(8,128)(2,1)S(1)}, bf16[64,2048]{1,0:T(8,128)(2,1)S(1)}, u32[]{:S(2)}, u32[]{:S(2)}) collective-permute-start(bf16[64,2048]{1,0:T(8,128)(2,1)S(1)} %add_convert_fusion.4), channel_id=1, source_target_pairs={{0,8},{4,12},{8,16},{12,20},{16,24},{20,28},{24,0},{28,4},{1,9},{5... | collective-permute-start | bytes 786440 | tf_op jit(solution)/shard_map/ppermute | solution.py:491
  175.7 3.9 collective-permute-done.20
  179.6 3.0 collective-permute-start.28
  183.5 5.4 %collective-permute-done.22 = bf16[64,2048]{1,0:T(8,128)(2,1)S(1)} collective-permute-done((bf16[64,2048]{1,0:T(8,128)(2,1)S(1)}, bf16[64,2048]{1,0:T(8,128)(2,1)S(1)}, u32[]{:S(2)}, u32[]{:S(2)}) %collective-permute-start.22) | collective-permute-done | bytes 262176 | tf_op jit(solution)/shard_map/ppermute | solution.py:491
  196.9 7.6 %collective-permute-done.30 = bf16[256,2048]{1,0:T(8,128)(2,1)S(1)} collective-permute-done((bf16[256,2048]{1,0:T(8,128)(2,1)S(1)}, bf16[256,2048]{1,0:T(8,128)(2,1)S(1)}, u32[]{:S(2)}, u32[]{:S(2)}) %collective-permute-start.30) | collective-permute-done | bytes 1048608 | tf_op jit(solution)/shard_map/ppermute | solution.py:118
  206.1 4.1 collective-permute-done.24
  212.3 3.5 collective-permute-done.25
  223.0 7.0 %ffn_forward.2 = (f32[512,512]{1,0:T(8,128)}, f32[512,512]{1,0:T(8,128)}, f32[512,512]{1,0:T(8,128)}, f32[8,512]{1,0:T(8,128)}) custom-call(s32[8]{0:T(128)} %fusion.47.labels, bf16[512,2048]{1,0:T(8,128)(2,1)} %constant_dynamic-update-slice_fusion.x.near_x, bf16[512,2048]{1,0:T(8,128)(2,1)} %copy-done.13, f32[3,512]{1,0:T(4,128)} %bitcast.231, ...), custom_call_target="tpu_custom_call" | custom-call | flops 2147483648 | bytes 10485760 | tf_op jit(solution)/shard_map/ffn_forward/pallas_call | solution.py:742
  230.7 7.0 %ffn_forward.3 = (f32[512,512]{1,0:T(8,128)}, f32[512,512]{1,0:T(8,128)}, f32[512,512]{1,0:T(8,128)}, f32[8,512]{1,0:T(8,128)}) custom-call(s32[8]{0:T(128)} %fusion.47.labels, bf16[512,2048]{1,0:T(8,128)(2,1)} %collective-permute-done.31.x.far_x, bf16[512,2048]{1,0:T(8,128)(2,1)} %collective-permute-done.32.g.far_g, f32[3,512]{1,0:T(4,128)} %bitcast.232, ...), custom_call_target="tpu_custom_call" | custom-call | flops 2147483648 | bytes 10485760 | tf_op jit(solution)/shard_map/ffn_forward/pallas_call | solution.py:742
  251.6 6.1 %ffn_backward.3 = (bf16[512,512]{1,0:T(8,128)(2,1)}, bf16[512,512]{1,0:T(8,128)(2,1)}, bf16[512,2048]{1,0:T(8,128)(2,1)}, f32[8,512]{1,0:T(8,128)}) custom-call(s32[8]{0:T(128)} %fusion.47.labels, f32[8,1024]{1,0:T(8,128)} %add_add_fusion.2.sums, f32[512,512]{1,0:T(8,128)} %get-tuple-element.113.active, f32[512,512]{1,0:T(8,128)} %get-tuple-element.114.slope, ...), custom_call_target="tpu_custom_call" | custom-call | flops 1073741824 | bytes 8388608 | tf_op jit(solution)/shard_map/ffn_backward/pallas_call | solution.py:759
  260.8 6.1 %ffn_backward.2 = (bf16[512,512]{1,0:T(8,128)(2,1)}, bf16[512,512]{1,0:T(8,128)(2,1)}, bf16[512,2048]{1,0:T(8,128)(2,1)}, f32[8,512]{1,0:T(8,128)}) custom-call(s32[8]{0:T(128)} %fusion.47.labels, f32[8,1024]{1,0:T(8,128)} %add_add_fusion.2.sums, f32[512,512]{1,0:T(8,128)} %get-tuple-element.109.active, f32[512,512]{1,0:T(8,128)} %get-tuple-element.110.slope, ...), custom_call_target="tpu_custom_call" | custom-call | flops 1073741824 | bytes 8388608 | tf_op jit(solution)/shard_map/ffn_backward/pallas_call | solution.py:759
  267.7 3.4 collective-permute-start.45
  278.2 7.7 %ffn_gradient.3 = (bf16[512,512]{1,0:T(8,128)(2,1)}, bf16[512,512]{1,0:T(8,128)(2,1)}, bf16[512,512]{1,0:T(8,128)(2,1)}, bf16[512,512]{1,0:T(8,128)(2,1)}) custom-call(s32[4]{0:T(128)} %get-tuple-element.319.labels, bf16[512,2048]{1,0:T(8,128)(2,1)} %constant_dynamic-update-slice_fusion.x.near_x, bf16[512,2048]{1,0:T(8,128)(2,1)} %collective-permute-done.31.x.far_x, ...), custom_call_target="tpu_custom_call" | custom-call | flops 2147483648 | bytes 9437184 | tf_op jit(solution)/shard_map/ffn_gradient/pallas_call | solution.py:796
  290.4 5.6 %collective-permute-done.47 = bf16[64,2048]{1,0:T(8,128)(2,1)S(1)} collective-permute-done((bf16[64,2048]{1,0:T(8,128)(2,1)S(1)}, bf16[64,2048]{1,0:T(8,128)(2,1)S(1)}, u32[]{:S(2)}, u32[]{:S(2)}) %collective-permute-start.47) | collective-permute-done | bytes 262176 | tf_op jit(solution)/shard_map/ppermute | solution.py:118
  304.4 7.9 %ffn_gradient.2 = (bf16[512,512]{1,0:T(8,128)(2,1)}, bf16[512,512]{1,0:T(8,128)(2,1)}, bf16[512,512]{1,0:T(8,128)(2,1)}, bf16[512,512]{1,0:T(8,128)(2,1)}) custom-call(s32[4]{0:T(128)} %get-tuple-element.318.labels, bf16[512,2048]{1,0:T(8,128)(2,1)} %constant_dynamic-update-slice_fusion.x.near_x, bf16[512,2048]{1,0:T(8,128)(2,1)} %collective-permute-done.31.x.far_x, ...), custom_call_target="tpu_custom_call" | custom-call | flops 2147483648 | bytes 9437184 | tf_op jit(solution)/shard_map/ffn_gradient/pallas_call | solution.py:796
  312.7 10.8 %collective-permute-done.44 = bf16[512,512]{1,0:T(8,128)(2,1)S(1)} collective-permute-done((bf16[512,512]{1,0:T(8,128)(2,1)}, bf16[512,512]{1,0:T(8,128)(2,1)S(1)}, u32[]{:S(2)}, u32[]{:S(2)}) %collective-permute-start.44) | collective-permute-done | bytes 524320 | tf_op jit(solution)/shard_map/ppermute | solution.py:505
  333.5 3.6 output_back.1
  341.5 3.3 collective-permute-done.56
  347.9 5.4 %attention_backward.1 = (bf16[256,512]{1,0:T(8,128)(2,1)S(1)}, bf16[256,512]{1,0:T(8,128)(2,1)S(1)}, bf16[256,512]{1,0:T(8,128)(2,1)S(1)}, f32[8,512]{1,0:T(8,128)S(1)}) custom-call(s32[2]{0:T(128)S(1)} %copy-done.10, f32[256,512]{1,0:T(8,128)S(1)} %copy-done.5, f32[256,512]{1,0:T(8,128)S(1)} %copy-done, f32[256,4]{1,0:T(8,128)S(1)} %copy.57.coefficients, ...), custom_call_target="tpu_custom_call" | custom-call | flops 335544320 | bytes 4194304 | tf_op jit(solution)/shard_map/attention_backward/pallas_call | solution.py:874
  355.4 3.3 projection_gradient_far.1
  360.8 4.2 ffn_product.3
  364.9 4.2 ffn_product.2
  369.1 9.0 %projection_gradient.1 = bf16[7,1024,512]{2,1,0:T(8,128)(2,1)} custom-call(s32[7]{0:T(128)} %fusion.50.labels, bf16[256,2048]{1,0:T(8,128)(2,1)} %fusion.3.x, bf16[256,2048]{1,0:T(8,128)(2,1)} %pad_maximum_fusion.3.grad, bf16[256,512]{1,0:T(8,128)(2,1)} %copy-done.1, bf16[256,512]{1,0:T(8,128)(2,1)} %copy-done.2, bf16[256,512]{1,0:T(8,128)(2,1)} %copy-done.3, ...), custom_call_target="tpu_custom_call" | custom-call | flops 1879048192 | bytes 7340032 | tf_op jit(solution)/shard_map/projection_gradient/pallas_call | solution.py:908
  379.4 6.0 %collective-permute-done.59 = bf16[512,512]{1,0:T(8,128)(2,1)S(1)} collective-permute-done((bf16[512,512]{1,0:T(8,128)(2,1)}, bf16[512,512]{1,0:T(8,128)(2,1)S(1)}, u32[]{:S(2)}, u32[]{:S(2)}) %collective-permute-start.59) | collective-permute-done | bytes 524320 | tf_op jit(solution)/shard_map/ppermute | solution.py:63
  391.1 8.2 %projection_back.1 = (bf16[128,2048]{1,0:T(8,128)(2,1)}, f32[128,2048]{1,0:T(8,128)}) custom-call(s32[8]{0:T(128)} %get-tuple-element.311.labels, s32[1]{0:T(128)} %bitcast.1.rank, bf16[256,512]{1,0:T(8,128)(2,1)} %copy-done.1, bf16[256,512]{1,0:T(8,128)(2,1)} %copy-done.2, bf16[256,512]{1,0:T(8,128)(2,1)} %copy-done.3, bf16[1024,512]{1,0:T(8,128)(2,1)} %copy-done.11, ...), custom_call_target="tpu_custom_call" | custom-call | flops 1610612736 | bytes 10485760 | tf_op jit(solution)/shard_map/projection_back/pallas_call | solution.py:971
  399.3 4.4 convert_add_fusion
  403.7 11.3 %collective-permute-done.64 = bf16[1024,512]{1,0:T(8,128)(2,1)} collective-permute-done((bf16[1024,512]{1,0:T(8,128)(2,1)}, bf16[1024,512]{1,0:T(8,128)(2,1)}, u32[]{:S(2)}, u32[]{:S(2)}) %collective-permute-start.64) | collective-permute-done | bytes 1048608 | tf_op jit(solution)/shard_map/ppermute | solution.py:63
  415.1 4.2 fusion.7
  428.4 3.9 ffn_placed.1
  433.5 5.6 %all-to-all-start.1 = ((f32[8,1,1856]{2,1,0:T(1,128)}), f32[8,1,1856]{2,1,0:T(1,128)S(1)}, u32[]{:S(2)}, u32[]{:S(2)}) async-start(f32[8,1,1856]{2,1,0:T(1,128)} %all_to_all.14), calls=%async_computation.1 | async-start | bytes 122880 | tf_op jit(solution)/shard_map/all_to_all | solution.py:1015
  439.5 16.6 %all-to-all-done.1 = f32[8,1,1856]{2,1,0:T(1,128)S(1)} async-done(((f32[8,1,1856]{2,1,0:T(1,128)}), f32[8,1,1856]{2,1,0:T(1,128)S(1)}, u32[]{:S(2)}, u32[]{:S(2)}) %all-to-all-start.1) | async-done | bytes 59424 | tf_op jit(solution)/shard_map/all_to_all | solution.py:1015
  458.4 4.1 fusion.5
  465.8 9.4 %collective-permute-done.71 = bf16[64,2048]{1,0:T(8,128)(2,1)S(1)} collective-permute-done((bf16[64,2048]{1,0:T(8,128)(2,1)S(1)}, bf16[64,2048]{1,0:T(8,128)(2,1)S(1)}, u32[]{:S(2)}, u32[]{:S(2)}) %collective-permute-start.71) | collective-permute-done | bytes 262176 | tf_op jit(solution)/shard_map/ppermute | solution.py:491
  478.2 8.4 %collective-permute-done.73 = bf16[64,2048]{1,0:T(8,128)(2,1)S(1)} collective-permute-done((bf16[64,2048]{1,0:T(8,128)(2,1)S(1)}, bf16[64,2048]{1,0:T(8,128)(2,1)S(1)}, u32[]{:S(2)}, u32[]{:S(2)}) %collective-permute-start.73) | collective-permute-done | bytes 262176 | tf_op jit(solution)/shard_map/ppermute | solution.py:491
  496.9 10.5 %collective-permute-done.77 = f32[64,2048]{1,0:T(8,128)S(1)} collective-permute-done((f32[64,2048]{1,0:T(8,128)S(1)}, f32[64,2048]{1,0:T(8,128)S(1)}, u32[]{:S(2)}, u32[]{:S(2)}) %collective-permute-start.77) | collective-permute-done | bytes 524320 | tf_op jit(solution)/shard_map/ppermute | solution.py:118
  510.2 6.0 %collective-permute-done.80 = bf16[1024,512]{1,0:T(8,128)(2,1)S(1)} collective-permute-done((bf16[1024,512]{1,0:T(8,128)(2,1)}, bf16[1024,512]{1,0:T(8,128)(2,1)S(1)}, u32[]{:S(2)}, u32[]{:S(2)}) %collective-permute-start.80) | collective-permute-done | bytes 1048608 | tf_op jit(solution)/shard_map/ppermute | solution.py:63
  (407 shorter events, 182.1 us)
Async XLA Ops:
  3.1 26.2 %collective-permute-start = (bf16[1024,512]{1,0:T(8,128)(2,1)S(1)}, bf16[1024,512]{1,0:T(8,128)(2,1)S(1)}, u32[]{:S(2)}, u32[]{:S(2)}) collective-permute-start(bf16[1024,512]{1,0:T(8,128)(2,1)S(1)} %pad_maximum_fusion.1.refs_0_), channel_id=1, source_target_pairs={{8,0},{16,8},{24,16},{28,24},{20,28},{12,20},{4,12},{0,4},{9,1},{1... | collective-permute-start | bytes 3145736 | tf_op jit(solution)/shard_map/ppermute | solution.py:63
  6.1 24.9 %collective-permute-start.3 = (bf16[1024,512]{1,0:T(8,128)(2,1)S(1)}, bf16[1024,512]{1,0:T(8,128)(2,1)S(1)}, u32[]{:S(2)}, u32[]{:S(2)}) collective-permute-start(bf16[1024,512]{1,0:T(8,128)(2,1)S(1)} %pad_maximum_fusion.1.refs_0_), channel_id=1, source_target_pairs={{0,8},{8,16},{16,24},{24,28},{28,20},{20,12},{12,4},{4,0},{1,9},{9... | collective-permute-start | bytes 3145736 | tf_op jit(solution)/shard_map/ppermute | solution.py:63
  29.3 24.8 %collective-permute-start.1 = (bf16[1024,512]{1,0:T(8,128)(2,1)S(1)}, bf16[1024,512]{1,0:T(8,128)(2,1)}, u32[]{:S(2)}, u32[]{:S(2)}) collective-permute-start(bf16[1024,512]{1,0:T(8,128)(2,1)S(1)} %collective-permute-done.refs_1_), channel_id=1, source_target_pairs={{8,0},{16,8},{24,16},{28,24},{20,28},{12,20},{4,12},{0,4},{9,1},{1... | collective-permute-start | bytes 3145736 | tf_op jit(solution)/shard_map/ppermute | solution.py:63
  31.0 24.4 %collective-permute-start.4 = (bf16[1024,512]{1,0:T(8,128)(2,1)S(1)}, bf16[1024,512]{1,0:T(8,128)(2,1)}, u32[]{:S(2)}, u32[]{:S(2)}) collective-permute-start(bf16[1024,512]{1,0:T(8,128)(2,1)S(1)} %collective-permute-done.3.refs_8_.refs_7_), channel_id=1, source_target_pairs={{0,8},{8,16},{16,24},{24,28},{28,20},{20,12},{12,4},{4,0},{1,9},{9... | collective-permute-start | bytes 3145736 | tf_op jit(solution)/shard_map/ppermute | solution.py:63
  33.8 27.1 %all-to-all-start = ((bf16[8,2,1312]{2,1,0:T(2,128)(2,1)}), bf16[8,2,1312]{2,1,0:T(2,128)(2,1)S(1)}, u32[]{:S(2)}, u32[]{:S(2)}) async-start(bf16[8,2,1312]{2,1,0:T(2,128)(2,1)} %reshape.387), calls=%async_computation | async-start | bytes 90112 | tf_op jit(solution)/shard_map/all_to_all | solution.py:539
  54.1 23.5 %collective-permute-start.2 = (bf16[1024,512]{1,0:T(8,128)(2,1)}, bf16[1024,512]{1,0:T(8,128)(2,1)S(1)}, u32[]{:S(2)}, u32[]{:S(2)}) collective-permute-start(bf16[1024,512]{1,0:T(8,128)(2,1)} %collective-permute-done.1.refs_2_), channel_id=1, source_target_pairs={{8,0},{16,8},{24,16},{28,24},{20,28},{12,20},{4,12},{0,4},{9,1},{1... | collective-permute-start | bytes 3145736 | tf_op jit(solution)/shard_map/ppermute | solution.py:63
  55.4 24.1 %collective-permute-start.5 = (bf16[1024,512]{1,0:T(8,128)(2,1)}, bf16[1024,512]{1,0:T(8,128)(2,1)S(1)}, u32[]{:S(2)}, u32[]{:S(2)}) collective-permute-start(bf16[1024,512]{1,0:T(8,128)(2,1)} %collective-permute-done.4.refs_7_.refs_6_), channel_id=1, source_target_pairs={{0,8},{8,16},{16,24},{24,28},{28,20},{20,12},{12,4},{4,0},{1,9},{9... | collective-permute-start | bytes 3145736 | tf_op jit(solution)/shard_map/ppermute | solution.py:63
  78.5 25.0 %collective-permute-start.7 = (bf16[512,512]{1,0:T(8,128)(2,1)}, bf16[512,512]{1,0:T(8,128)(2,1)S(1)}, u32[]{:S(2)}, u32[]{:S(2)}) collective-permute-start(bf16[512,512]{1,0:T(8,128)(2,1)} %slice.374), channel_id=1, source_target_pairs={{8,0},{16,8},{24,16},{28,24},{20,28},{12,20},{4,12},{0,4},{9,1},{1... | collective-permute-start | bytes 1572872 | tf_op jit(solution)/shard_map/ppermute | solution.py:63
  80.4 23.2 %collective-permute-start.6 = (bf16[512,512]{1,0:T(8,128)(2,1)}, bf16[512,512]{1,0:T(8,128)(2,1)}, u32[]{:S(2)}, u32[]{:S(2)}) collective-permute-start(bf16[512,512]{1,0:T(8,128)(2,1)} %slice.373), channel_id=1, source_target_pairs={{0,8},{8,16},{16,24},{24,28},{28,20},{20,12},{12,4},{4,0},{1,9},{9... | collective-permute-start | bytes 1572872 | tf_op jit(solution)/shard_map/ppermute | solution.py:63
  85.3 31.1 %collective-permute-start.10 = (bf16[512,512]{1,0:T(8,128)(2,1)S(1)}, bf16[512,512]{1,0:T(8,128)(2,1)S(1)}, u32[]{:S(2)}, u32[]{:S(2)}) collective-permute-start(bf16[512,512]{1,0:T(8,128)(2,1)S(1)} %get-tuple-element.269.refs_0_), channel_id=1, source_target_pairs={{0,4},{4,0},{8,12},{12,8},{16,20},{20,16},{24,28},{28,24},{1,5},{5... | collective-permute-start | bytes 1572872 | tf_op jit(solution)/shard_map/ppermute | solution.py:505
  86.2 32.0 %collective-permute-start.8 = (bf16[512,512]{1,0:T(8,128)(2,1)}, bf16[512,512]{1,0:T(8,128)(2,1)}, u32[]{:S(2)}, u32[]{:S(2)}) collective-permute-start(bf16[512,512]{1,0:T(8,128)(2,1)} %get-tuple-element.271), channel_id=1, source_target_pairs={{0,8},{4,12},{8,16},{12,20},{16,24},{20,28},{24,0},{28,4},{1,9},{5... | collective-permute-start | bytes 1572872 | tf_op jit(solution)/shard_map/ppermute | solution.py:491
  87.7 30.5 %collective-permute-start.9 = (bf16[512,512]{1,0:T(8,128)(2,1)}, bf16[512,512]{1,0:T(8,128)(2,1)S(1)}, u32[]{:S(2)}, u32[]{:S(2)}) collective-permute-start(bf16[512,512]{1,0:T(8,128)(2,1)} %get-tuple-element.270), channel_id=1, source_target_pairs={{0,24},{4,28},{8,0},{12,4},{16,8},{20,12},{24,16},{28,20},{1,25},{... | collective-permute-start | bytes 1572872 | tf_op jit(solution)/shard_map/ppermute | solution.py:491
  118.2 25.1 %collective-permute-start.15 = (bf16[512,512]{1,0:T(8,128)(2,1)}, bf16[512,512]{1,0:T(8,128)(2,1)S(1)}, u32[]{:S(2)}, u32[]{:S(2)}) collective-permute-start(bf16[512,512]{1,0:T(8,128)(2,1)} %get-tuple-element.268), channel_id=1, source_target_pairs={{0,16},{4,20},{8,24},{12,28},{16,0},{20,4},{24,8},{28,12},{1,17},{... | collective-permute-start | bytes 1572872 | tf_op jit(solution)/shard_map/ppermute | solution.py:491
  131.1 16.1 %collective-permute-start.14 = (bf16[128,2048]{1,0:T(8,128)(2,1)}, bf16[128,2048]{1,0:T(8,128)(2,1)S(1)}, u32[]{:S(2)}, u32[]{:S(2)}) collective-permute-start(bf16[128,2048]{1,0:T(8,128)(2,1)} %get-tuple-element.100), channel_id=1, source_target_pairs={{0,1},{1,0},{2,3},{3,2},{4,5},{5,4},{6,7},{7,6},{8,9},{9,8},{10,11... | collective-permute-start | bytes 1572872 | tf_op jit(solution)/shard_map/ppermute | solution.py:118
  143.4 21.4 %collective-permute-start.18 = (bf16[64,2048]{1,0:T(8,128)(2,1)S(1)}, bf16[64,2048]{1,0:T(8,128)(2,1)}, u32[]{:S(2)}, u32[]{:S(2)}) collective-permute-start(bf16[64,2048]{1,0:T(8,128)(2,1)S(1)} %fusion.36), channel_id=1, source_target_pairs={{0,16},{4,20},{8,24},{12,28},{16,0},{20,4},{24,8},{28,12},{1,17},{... | collective-permute-start | bytes 786440 | tf_op jit(solution)/shard_map/ppermute | solution.py:491
  144.2 20.6 %collective-permute-start.19 = (bf16[64,2048]{1,0:T(8,128)(2,1)S(1)}, bf16[64,2048]{1,0:T(8,128)(2,1)}, u32[]{:S(2)}, u32[]{:S(2)}) collective-permute-start(bf16[64,2048]{1,0:T(8,128)(2,1)S(1)} %fusion.36), channel_id=1, source_target_pairs={{0,24},{4,28},{8,0},{12,4},{16,8},{20,12},{24,16},{28,20},{1,25},{... | collective-permute-start | bytes 786440 | tf_op jit(solution)/shard_map/ppermute | solution.py:491
  148.6 17.4 %collective-permute-start.16 = (bf16[64,2048]{1,0:T(8,128)(2,1)S(1)}, bf16[64,2048]{1,0:T(8,128)(2,1)S(1)}, u32[]{:S(2)}, u32[]{:S(2)}) collective-permute-start(bf16[64,2048]{1,0:T(8,128)(2,1)S(1)} %fusion.37), channel_id=1, source_target_pairs={{0,2},{1,3},{2,0},{3,1},{4,6},{5,7},{6,4},{7,5},{8,10},{9,11},{10,... | collective-permute-start | bytes 786440 | tf_op jit(solution)/shard_map/ppermute | solution.py:118
  150.1 69.9 %collective-permute-start.27 = (bf16[512,512]{1,0:T(8,128)(2,1)}, bf16[512,512]{1,0:T(8,128)(2,1)S(1)}, u32[]{:S(2)}, u32[]{:S(2)}) collective-permute-start(bf16[512,512]{1,0:T(8,128)(2,1)} %collective-permute-done.8.refs_1_), channel_id=1, source_target_pairs={{0,4},{4,0},{8,12},{12,8},{16,20},{20,16},{24,28},{28,24},{1,5},{5... | collective-permute-start | bytes 1572872 | tf_op jit(solution)/shard_map/ppermute | solution.py:505
  174.4 30.2 %collective-permute-start.30 = (bf16[256,2048]{1,0:T(8,128)(2,1)S(1)}, bf16[256,2048]{1,0:T(8,128)(2,1)S(1)}, u32[]{:S(2)}, u32[]{:S(2)}) collective-permute-start(bf16[256,2048]{1,0:T(8,128)(2,1)S(1)} %pad_maximum_fusion.2), channel_id=1, source_target_pairs={{0,2},{1,3},{2,0},{3,1},{4,6},{5,7},{6,4},{7,5},{8,10},{9,11},{10,... | collective-permute-start | bytes 3145736 | tf_op jit(solution)/shard_map/ppermute | solution.py:118
  179.6 40.4 %collective-permute-start.28 = (bf16[512,512]{1,0:T(8,128)(2,1)S(1)}, bf16[512,512]{1,0:T(8,128)(2,1)S(1)}, u32[]{:S(2)}, u32[]{:S(2)}) collective-permute-start(bf16[512,512]{1,0:T(8,128)(2,1)S(1)} %copy-done.19), channel_id=1, source_target_pairs={{0,4},{4,0},{8,12},{12,8},{16,20},{20,16},{24,28},{28,24},{1,5},{5... | collective-permute-start | bytes 1572872 | tf_op jit(solution)/shard_map/ppermute | solution.py:505
  189.0 31.1 %collective-permute-start.29 = (bf16[512,512]{1,0:T(8,128)(2,1)S(1)}, bf16[512,512]{1,0:T(8,128)(2,1)S(1)}, u32[]{:S(2)}, u32[]{:S(2)}) collective-permute-start(bf16[512,512]{1,0:T(8,128)(2,1)S(1)} %copy-done.21), channel_id=1, source_target_pairs={{0,4},{4,0},{8,12},{12,8},{16,20},{20,16},{24,28},{28,24},{1,5},{5... | collective-permute-start | bytes 1572872 | tf_op jit(solution)/shard_map/ppermute | solution.py:505
  194.0 16.2 %collective-permute-start.24 = (bf16[64,2048]{1,0:T(8,128)(2,1)S(1)}, bf16[64,2048]{1,0:T(8,128)(2,1)S(1)}, u32[]{:S(2)}, u32[]{:S(2)}) collective-permute-start(bf16[64,2048]{1,0:T(8,128)(2,1)S(1)} %collective-permute-done.20), channel_id=1, source_target_pairs={{0,2},{1,3},{2,0},{3,1},{4,6},{5,7},{6,4},{7,5},{8,10},{9,11},{10,... | collective-permute-start | bytes 786440 | tf_op jit(solution)/shard_map/ppermute | solution.py:118
  215.8 14.9 %collective-permute-start.32 = (bf16[512,2048]{1,0:T(8,128)(2,1)S(1)}, bf16[512,2048]{1,0:T(8,128)(2,1)}, u32[]{:S(2)}, u32[]{:S(2)}) collective-permute-start(bf16[512,2048]{1,0:T(8,128)(2,1)S(1)} %constant_dynamic-update-slice_fusion.8.g.near_g), channel_id=1, source_target_pairs={{0,1},{1,0},{2,3},{3,2},{4,5},{5,4},{6,7},{7,6},{8,9},{9,8},{10,11... | collective-permute-start | bytes 6291464 | tf_op jit(solution)/shard_map/ppermute | solution.py:118
  267.7 18.2 %collective-permute-start.45 = (f32[3,256]{1,0:T(4,128)S(1)}, f32[3,256]{1,0:T(4,128)S(1)}, u32[]{:S(2)}, u32[]{:S(2)}) collective-permute-start(f32[3,256]{1,0:T(4,128)S(1)} %bitcast.268), channel_id=1, source_target_pairs={{0,4},{4,0},{8,12},{12,8},{16,20},{20,16},{24,28},{28,24},{1,5},{5... | collective-permute-start | bytes 9224 | tf_op jit(solution)/shard_map/ppermute | solution.py:505
  277.7 18.4 %collective-permute-start.47 = (bf16[64,2048]{1,0:T(8,128)(2,1)S(1)}, bf16[64,2048]{1,0:T(8,128)(2,1)S(1)}, u32[]{:S(2)}, u32[]{:S(2)}) collective-permute-start(bf16[64,2048]{1,0:T(8,128)(2,1)S(1)} %get-tuple-element.265), channel_id=1, source_target_pairs={{0,2},{1,3},{2,0},{3,1},{4,6},{5,7},{6,4},{7,5},{8,10},{9,11},{10,... | collective-permute-start | bytes 786440 | tf_op jit(solution)/shard_map/ppermute | solution.py:118
  285.9 15.9 %collective-permute-start.42 = (bf16[512,512]{1,0:T(8,128)(2,1)}, bf16[512,512]{1,0:T(8,128)(2,1)S(1)}, u32[]{:S(2)}, u32[]{:S(2)}) collective-permute-start(bf16[512,512]{1,0:T(8,128)(2,1)} %get-tuple-element.126), channel_id=1, source_target_pairs={{0,4},{4,0},{8,12},{12,8},{16,20},{20,16},{24,28},{28,24},{1,5},{5... | collective-permute-start | bytes 1572872 | tf_op jit(solution)/shard_map/ppermute | solution.py:505
  286.0 14.9 %collective-permute-start.40 = (bf16[64,2048]{1,0:T(8,128)(2,1)S(1)}, bf16[64,2048]{1,0:T(8,128)(2,1)S(1)}, u32[]{:S(2)}, u32[]{:S(2)}) collective-permute-start(bf16[64,2048]{1,0:T(8,128)(2,1)S(1)} %get-tuple-element.264), channel_id=1, source_target_pairs={{0,2},{1,3},{2,0},{3,1},{4,6},{5,7},{6,4},{7,5},{8,10},{9,11},{10,... | collective-permute-start | bytes 786440 | tf_op jit(solution)/shard_map/ppermute | solution.py:118
  287.5 24.8 %collective-permute-start.43 = (bf16[512,512]{1,0:T(8,128)(2,1)}, bf16[512,512]{1,0:T(8,128)(2,1)S(1)}, u32[]{:S(2)}, u32[]{:S(2)}) collective-permute-start(bf16[512,512]{1,0:T(8,128)(2,1)} %get-tuple-element.127), channel_id=1, source_target_pairs={{0,4},{4,0},{8,12},{12,8},{16,20},{20,16},{24,28},{28,24},{1,5},{5... | collective-permute-start | bytes 1572872 | tf_op jit(solution)/shard_map/ppermute | solution.py:505
  290.4 33.1 %collective-permute-start.44 = (bf16[512,512]{1,0:T(8,128)(2,1)}, bf16[512,512]{1,0:T(8,128)(2,1)S(1)}, u32[]{:S(2)}, u32[]{:S(2)}) collective-permute-start(bf16[512,512]{1,0:T(8,128)(2,1)} %get-tuple-element.128), channel_id=1, source_target_pairs={{0,4},{4,0},{8,12},{12,8},{16,20},{20,16},{24,28},{28,24},{1,5},{5... | collective-permute-start | bytes 1572872 | tf_op jit(solution)/shard_map/ppermute | solution.py:505
  297.6 25.9 %collective-permute-start.48 = (bf16[64,2048]{1,0:T(8,128)(2,1)S(1)}, bf16[64,2048]{1,0:T(8,128)(2,1)S(1)}, u32[]{:S(2)}, u32[]{:S(2)}) collective-permute-start(bf16[64,2048]{1,0:T(8,128)(2,1)S(1)} %get-tuple-element.133), channel_id=1, source_target_pairs={{0,24},{4,28},{8,0},{12,4},{16,8},{20,12},{24,16},{28,20},{1,25},{... | collective-permute-start | bytes 786440 | tf_op jit(solution)/shard_map/ppermute | solution.py:491
  300.9 22.6 %collective-permute-start.49 = (bf16[64,2048]{1,0:T(8,128)(2,1)S(1)}, bf16[64,2048]{1,0:T(8,128)(2,1)S(1)}, u32[]{:S(2)}, u32[]{:S(2)}) collective-permute-start(bf16[64,2048]{1,0:T(8,128)(2,1)S(1)} %get-tuple-element.134), channel_id=1, source_target_pairs={{0,8},{4,12},{8,16},{12,20},{16,24},{20,28},{24,0},{28,4},{1,9},{5... | collective-permute-start | bytes 786440 | tf_op jit(solution)/shard_map/ppermute | solution.py:491
  301.8 21.7 %collective-permute-start.50 = (bf16[64,2048]{1,0:T(8,128)(2,1)S(1)}, bf16[64,2048]{1,0:T(8,128)(2,1)S(1)}, u32[]{:S(2)}, u32[]{:S(2)}) collective-permute-start(bf16[64,2048]{1,0:T(8,128)(2,1)S(1)} %get-tuple-element.259), channel_id=1, source_target_pairs={{0,16},{4,20},{8,24},{12,28},{16,0},{20,4},{24,8},{28,12},{1,17},{... | collective-permute-start | bytes 786440 | tf_op jit(solution)/shard_map/ppermute | solution.py:491
  312.3 21.2 %collective-permute-start.54 = (bf16[512,512]{1,0:T(8,128)(2,1)}, bf16[512,512]{1,0:T(8,128)(2,1)S(1)}, u32[]{:S(2)}, u32[]{:S(2)}) collective-permute-start(bf16[512,512]{1,0:T(8,128)(2,1)} %get-tuple-element.132), channel_id=1, source_target_pairs={{0,4},{4,0},{8,12},{12,8},{16,20},{20,16},{24,28},{28,24},{1,5},{5... | collective-permute-start | bytes 1572872 | tf_op jit(solution)/shard_map/ppermute | solution.py:505
  326.8 52.6 %collective-permute-start.62 = (bf16[512,512]{1,0:T(8,128)(2,1)}, bf16[512,512]{1,0:T(8,128)(2,1)}, u32[]{:S(2)}, u32[]{:S(2)}) collective-permute-start(bf16[512,512]{1,0:T(8,128)(2,1)} %add_convert_fusion.1), channel_id=1, source_target_pairs={{0,24},{4,28},{8,0},{12,4},{16,8},{20,12},{24,16},{28,20},{1,25},{... | collective-permute-start | bytes 1572872 | tf_op jit(solution)/shard_map/ppermute | solution.py:491
  329.7 49.7 %collective-permute-start.61 = (bf16[512,512]{1,0:T(8,128)(2,1)}, bf16[512,512]{1,0:T(8,128)(2,1)}, u32[]{:S(2)}, u32[]{:S(2)}) collective-permute-start(bf16[512,512]{1,0:T(8,128)(2,1)} %add_convert_fusion.2), channel_id=1, source_target_pairs={{0,8},{4,12},{8,16},{12,20},{16,24},{20,28},{24,0},{28,4},{1,9},{5... | collective-permute-start | bytes 1572872 | tf_op jit(solution)/shard_map/ppermute | solution.py:491
  341.2 38.3 %collective-permute-start.60 = (bf16[512,512]{1,0:T(8,128)(2,1)}, bf16[512,512]{1,0:T(8,128)(2,1)}, u32[]{:S(2)}, u32[]{:S(2)}) collective-permute-start(bf16[512,512]{1,0:T(8,128)(2,1)} %add_convert_fusion.3), channel_id=1, source_target_pairs={{0,16},{4,20},{8,24},{12,28},{16,0},{20,4},{24,8},{28,12},{1,17},{... | collective-permute-start | bytes 1572872 | tf_op jit(solution)/shard_map/ppermute | solution.py:491
  358.7 20.7 %collective-permute-start.58 = (bf16[512,512]{1,0:T(8,128)(2,1)}, bf16[512,512]{1,0:T(8,128)(2,1)S(1)}, u32[]{:S(2)}, u32[]{:S(2)}) collective-permute-start(bf16[512,512]{1,0:T(8,128)(2,1)} %get-tuple-element.145), channel_id=1, source_target_pairs={{0,8},{8,16},{16,24},{24,28},{28,20},{20,12},{12,4},{4,0},{1,9},{9... | collective-permute-start | bytes 1572872 | tf_op jit(solution)/shard_map/ppermute | solution.py:63
  359.7 25.8 %collective-permute-start.59 = (bf16[512,512]{1,0:T(8,128)(2,1)}, bf16[512,512]{1,0:T(8,128)(2,1)S(1)}, u32[]{:S(2)}, u32[]{:S(2)}) collective-permute-start(bf16[512,512]{1,0:T(8,128)(2,1)} %get-tuple-element.146), channel_id=1, source_target_pairs={{8,0},{16,8},{24,16},{28,24},{20,28},{12,20},{4,12},{0,4},{9,1},{1... | collective-permute-start | bytes 1572872 | tf_op jit(solution)/shard_map/ppermute | solution.py:63
  389.0 26.0 %collective-permute-start.64 = (bf16[1024,512]{1,0:T(8,128)(2,1)}, bf16[1024,512]{1,0:T(8,128)(2,1)}, u32[]{:S(2)}, u32[]{:S(2)}) collective-permute-start(bf16[1024,512]{1,0:T(8,128)(2,1)} %pad_maximum_fusion.5), channel_id=1, source_target_pairs={{8,0},{16,8},{24,16},{28,24},{20,28},{12,20},{4,12},{0,4},{9,1},{1... | collective-permute-start | bytes 3145736 | tf_op jit(solution)/shard_map/ppermute | solution.py:63
  389.0 26.0 %collective-permute-start.63 = (bf16[1024,512]{1,0:T(8,128)(2,1)}, bf16[1024,512]{1,0:T(8,128)(2,1)}, u32[]{:S(2)}, u32[]{:S(2)}) collective-permute-start(bf16[1024,512]{1,0:T(8,128)(2,1)} %pad_maximum_fusion.4), channel_id=1, source_target_pairs={{0,8},{8,16},{16,24},{24,28},{28,20},{20,12},{12,4},{4,0},{1,9},{9... | collective-permute-start | bytes 3145736 | tf_op jit(solution)/shard_map/ppermute | solution.py:63
  420.6 37.8 %collective-permute-start.69 = (bf16[1024,512]{1,0:T(8,128)(2,1)}, bf16[1024,512]{1,0:T(8,128)(2,1)}, u32[]{:S(2)}, u32[]{:S(2)}) collective-permute-start(bf16[1024,512]{1,0:T(8,128)(2,1)} %get-tuple-element.252), channel_id=1, source_target_pairs={{0,8},{8,16},{16,24},{24,28},{28,20},{20,12},{12,4},{4,0},{1,9},{9... | collective-permute-start | bytes 3145736 | tf_op jit(solution)/shard_map/ppermute | solution.py:63
  426.7 29.5 %collective-permute-start.68 = (bf16[4,64,2048]{2,1,0:T(8,128)(2,1)}, bf16[4,64,2048]{2,1,0:T(8,128)(2,1)}, u32[]{:S(2)}, u32[]{:S(2)}) collective-permute-start(bf16[4,64,2048]{2,1,0:T(8,128)(2,1)} %fusion.10), channel_id=1, source_target_pairs={{0,2},{1,3},{2,0},{3,1},{4,6},{5,7},{6,4},{7,5},{8,10},{9,11},{10,... | collective-permute-start | bytes 3145736 | tf_op jit(solution)/shard_map/ppermute | solution.py:118
  428.0 30.4 %collective-permute-start.70 = (bf16[1024,512]{1,0:T(8,128)(2,1)}, bf16[1024,512]{1,0:T(8,128)(2,1)}, u32[]{:S(2)}, u32[]{:S(2)}) collective-permute-start(bf16[1024,512]{1,0:T(8,128)(2,1)} %get-tuple-element.251), channel_id=1, source_target_pairs={{8,0},{16,8},{24,16},{28,24},{20,28},{12,20},{4,12},{0,4},{9,1},{1... | collective-permute-start | bytes 3145736 | tf_op jit(solution)/shard_map/ppermute | solution.py:63
  433.5 22.6 %all-to-all-start.1 = ((f32[8,1,1856]{2,1,0:T(1,128)}), f32[8,1,1856]{2,1,0:T(1,128)S(1)}, u32[]{:S(2)}, u32[]{:S(2)}) async-start(f32[8,1,1856]{2,1,0:T(1,128)} %all_to_all.14), calls=%async_computation.1 | async-start | bytes 122880 | tf_op jit(solution)/shard_map/all_to_all | solution.py:1015
  463.9 14.3 %collective-permute-start.72 = (bf16[64,2048]{1,0:T(8,128)(2,1)S(1)}, bf16[64,2048]{1,0:T(8,128)(2,1)S(1)}, u32[]{:S(2)}, u32[]{:S(2)}) collective-permute-start(bf16[64,2048]{1,0:T(8,128)(2,1)S(1)} %get-tuple-element.279), channel_id=1, source_target_pairs={{0,8},{4,12},{8,16},{12,20},{16,24},{20,28},{24,0},{28,4},{1,9},{5... | collective-permute-start | bytes 786440 | tf_op jit(solution)/shard_map/ppermute | solution.py:491
  464.8 21.8 %collective-permute-start.73 = (bf16[64,2048]{1,0:T(8,128)(2,1)S(1)}, bf16[64,2048]{1,0:T(8,128)(2,1)S(1)}, u32[]{:S(2)}, u32[]{:S(2)}) collective-permute-start(bf16[64,2048]{1,0:T(8,128)(2,1)S(1)} %get-tuple-element.278), channel_id=1, source_target_pairs={{0,16},{4,20},{8,24},{12,28},{16,0},{20,4},{24,8},{28,12},{1,17},{... | collective-permute-start | bytes 786440 | tf_op jit(solution)/shard_map/ppermute | solution.py:491
  490.6 25.6 %collective-permute-start.80 = (bf16[1024,512]{1,0:T(8,128)(2,1)}, bf16[1024,512]{1,0:T(8,128)(2,1)S(1)}, u32[]{:S(2)}, u32[]{:S(2)}) collective-permute-start(bf16[1024,512]{1,0:T(8,128)(2,1)} %get-tuple-element.250), channel_id=1, source_target_pairs={{0,8},{8,16},{16,24},{24,28},{28,20},{20,12},{12,4},{4,0},{1,9},{9... | collective-permute-start | bytes 3145736 | tf_op jit(solution)/shard_map/ppermute | solution.py:63
  491.8 25.6 %collective-permute-start.81 = (bf16[1024,512]{1,0:T(8,128)(2,1)}, bf16[1024,512]{1,0:T(8,128)(2,1)S(1)}, u32[]{:S(2)}, u32[]{:S(2)}) collective-permute-start(bf16[1024,512]{1,0:T(8,128)(2,1)} %get-tuple-element.249), channel_id=1, source_target_pairs={{8,0},{16,8},{24,16},{28,24},{20,28},{12,20},{4,12},{0,4},{9,1},{1... | collective-permute-start | bytes 3145736 | tf_op jit(solution)/shard_map/ppermute | solution.py:63
  (87 other events, 925.4 us)

commit v5 on v4

--- a/solution.py
+++ b/solution.py
@@ -132,7 +132,7 @@
 
 def rotation_tables(count, row_width):
     position = np.arange(count, dtype=np.float32)[:, None]
-    lane = np.arange(2 * row_width)[None, :]
+    lane = np.arange(row_width)[None, :]
     channel = (lane % row_width // 2).astype(np.float32)
     frequency = np.exp(-(2.0 * channel / row_width) * np.log(np.float32(10000.0)))
     angle = (position * frequency).astype(np.float32)
@@ -141,7 +141,8 @@
     cosine = np.cos(angle)
     sine = np.sin(angle) * np.where(lane % 2 == 0, -1.0, 1.0)
     tables = [cosine * growth, sine * growth, cosine / growth, sine / growth]
-    return jnp.asarray(np.stack(tables).astype(np.float32))
+    one_head = lax.optimization_barrier(jnp.asarray(np.stack(tables).astype(np.float32)))
+    return jnp.concatenate([one_head, one_head], axis=2)
 
 
 def swapped(values):

time: 533 us -> 534 us (level)
    unnamed x123 -> x127, local copies, waits for them, and re-layouts: 14.6 us -> 14.6 us
  transfers between devices with their start and end apart: 87 -> 87, of which waited for: 39 -> 40; matrix products, arithmetic and copies ran while one was open for 15% -> 15% of each run, Pallas kernels for 16% -> 16%
where the time goes in v5:
time: 534 us; the launch traced here: 525 us
  waiting for transfers between devices  225 us (42%)
  Pallas kernels  99 us (19%)
  starting transfers between devices  97.6 us (18%)
  other arithmetic  54.9 us (10%)
  local copies, waits for them, and re-layouts  46.3 us (9%)
    ppermute x16, waiting for transfers between devices, send(): lax.ppermute(block, 'fsdp', self.forward if way > 0 else self.backward)  84.8 us
    ppermute x21, waiting for transfers between devices, group_send(): lax.ppermute(block, 'fsdp', [(g * others + o, (g + shift) % GROUPS * othe...  58.7 us
    ppermute x39, waiting for transfers between devices, tp_send(): return lax.ppermute(block, 'tp', [(i, i ^ mask) for i in range(4)])  53.2 us
    ppermute x39, starting transfers between devices, tp_send(): return lax.ppermute(block, 'tp', [(i, i ^ mask) for i in range(4)])  27.2 us
    ppermute x21, starting transfers between devices, group_send(): lax.ppermute(block, 'fsdp', [(g * others + o, (g + shift) % GROUPS * othe...  25.1 us
    ppermute x16, starting transfers between devices, send(): lax.ppermute(block, 'fsdp', self.forward if way > 0 else self.backward)  18.1 us
    all_to_all x1, waiting for transfers between devices, while_second(): results['joined'] = jnp.sum(lax.all_to_all(joined, 'fsdp', 0, 0), axis=0)  16.6 us
    pallas_call x2, Pallas kernels, fc_gradient(): pl.pallas_call(ffn_gradient, grid_spec=pltpu.PrefetchScalarGridSpec(num_s...  15.6 us
  transfers between devices with their start and end apart: 87, of which 40 were waited for; matrix products, arithmetic and copies ran while one was open for 15% of the time, Pallas kernels for 16%

profile of v5, /device:TPU:0, one launch (start us, length us, event | category | flops | bytes accessed | tf_op | source)
XLA Modules:
  0.0 524.9 jit_solution(17694798284885594587)
XLA Ops:
  6.2 23.1 %collective-permute-done.refs_1_ = bf16[1024,512]{1,0:T(8,128)(2,1)S(1)} collective-permute-done((bf16[1024,512]{1,0:T(8,128)(2,1)S(1)}, bf16[1024,512]{1,0:T(8,128)(2,1)S(1)}, u32[]{:S(2)}, u32[]{:S(2)}) %collective-permute-start) | collective-permute-done | bytes 1048608 | tf_op jit(solution)/shard_map/ppermute | solution.py:63
  33.8 6.0 %all-to-all-start = ((bf16[8,2,1312]{2,1,0:T(2,128)(2,1)}), bf16[8,2,1312]{2,1,0:T(2,128)(2,1)S(1)}, u32[]{:S(2)}, u32[]{:S(2)}) async-start(bf16[8,2,1312]{2,1,0:T(2,128)(2,1)} %reshape.387), calls=%async_computation | async-start | bytes 90112 | tf_op jit(solution)/shard_map/all_to_all | solution.py:540
  44.5 3.1 maximum_bitcast_fusion
  48.0 6.1 %collective-permute-done.1.refs_2_ = bf16[1024,512]{1,0:T(8,128)(2,1)} collective-permute-done((bf16[1024,512]{1,0:T(8,128)(2,1)S(1)}, bf16[1024,512]{1,0:T(8,128)(2,1)}, u32[]{:S(2)}, u32[]{:S(2)}) %collective-permute-start.1) | collective-permute-done | bytes 1048608 | tf_op jit(solution)/shard_map/ppermute | solution.py:63
  59.0 18.7 %collective-permute-done.2.refs_3_ = bf16[1024,512]{1,0:T(8,128)(2,1)S(1)} collective-permute-done((bf16[1024,512]{1,0:T(8,128)(2,1)}, bf16[1024,512]{1,0:T(8,128)(2,1)S(1)}, u32[]{:S(2)}, u32[]{:S(2)}) %collective-permute-start.2) | collective-permute-done | bytes 1048608 | tf_op jit(solution)/shard_map/ppermute | solution.py:63
  90.9 12.7 %collective-permute-done.7.refs_5_.refs_4_ = bf16[512,512]{1,0:T(8,128)(2,1)S(1)} collective-permute-done((bf16[512,512]{1,0:T(8,128)(2,1)}, bf16[512,512]{1,0:T(8,128)(2,1)S(1)}, u32[]{:S(2)}, u32[]{:S(2)}) %collective-permute-start.7) | collective-permute-done | bytes 524320 | tf_op jit(solution)/shard_map/ppermute | solution.py:63
  104.3 11.0 %attention_forward.1 = (bf16[256,512]{1,0:T(8,128)(2,1)}, bf16[256,512]{1,0:T(8,128)(2,1)}, bf16[256,512]{1,0:T(8,128)(2,1)}, f32[256,512]{1,0:T(8,128)}, f32[256,128]{1,0:T(8,128)}) custom-call(s32[8]{0:T(128)} %get-tuple-element.311.labels, s32[2]{0:T(128)} %broadcast_add_fusion.limits, bf16[256,2048]{1,0:T(8,128)(2,1)} %fusion.3.x, ...), custom_call_target="tpu_custom_call" | custom-call | flops 1610612736 | bytes 12582912 | tf_op jit(solution)/shard_map/attention_forward/pallas_call | solution.py:676
  118.2 4.5 collective-permute-done.12
  126.6 4.4 output_product.1
  131.9 11.5 %collective-permute-done.15.refs_3_ = bf16[512,512]{1,0:T(8,128)(2,1)S(1)} collective-permute-done((bf16[512,512]{1,0:T(8,128)(2,1)}, bf16[512,512]{1,0:T(8,128)(2,1)S(1)}, u32[]{:S(2)}, u32[]{:S(2)}) %collective-permute-start.15) | collective-permute-done | bytes 524320 | tf_op jit(solution)/shard_map/ppermute | solution.py:492
  150.2 3.2 collective-permute-start.27
  154.5 10.2 %collective-permute-done.18 = bf16[64,2048]{1,0:T(8,128)(2,1)} collective-permute-done((bf16[64,2048]{1,0:T(8,128)(2,1)S(1)}, bf16[64,2048]{1,0:T(8,128)(2,1)}, u32[]{:S(2)}, u32[]{:S(2)}) %collective-permute-start.18) | collective-permute-done | bytes 262176 | tf_op jit(solution)/shard_map/ppermute | solution.py:492
  167.5 5.3 %collective-permute-start.20 = (bf16[64,2048]{1,0:T(8,128)(2,1)S(1)}, bf16[64,2048]{1,0:T(8,128)(2,1)S(1)}, u32[]{:S(2)}, u32[]{:S(2)}) collective-permute-start(bf16[64,2048]{1,0:T(8,128)(2,1)S(1)} %add_convert_fusion.4), channel_id=1, source_target_pairs={{0,8},{4,12},{8,16},{12,20},{16,24},{20,28},{24,0},{28,4},{1,9},{5... | collective-permute-start | bytes 786440 | tf_op jit(solution)/shard_map/ppermute | solution.py:492
  175.7 3.9 collective-permute-done.20
  179.6 3.1 collective-permute-start.28
  183.5 5.4 %collective-permute-done.22 = bf16[64,2048]{1,0:T(8,128)(2,1)S(1)} collective-permute-done((bf16[64,2048]{1,0:T(8,128)(2,1)S(1)}, bf16[64,2048]{1,0:T(8,128)(2,1)S(1)}, u32[]{:S(2)}, u32[]{:S(2)}) %collective-permute-start.22) | collective-permute-done | bytes 262176 | tf_op jit(solution)/shard_map/ppermute | solution.py:492
  196.9 7.6 %collective-permute-done.30 = bf16[256,2048]{1,0:T(8,128)(2,1)S(1)} collective-permute-done((bf16[256,2048]{1,0:T(8,128)(2,1)S(1)}, bf16[256,2048]{1,0:T(8,128)(2,1)S(1)}, u32[]{:S(2)}, u32[]{:S(2)}) %collective-permute-start.30) | collective-permute-done | bytes 1048608 | tf_op jit(solution)/shard_map/ppermute | solution.py:118
  206.2 4.0 collective-permute-done.24
  212.4 3.4 collective-permute-done.25
  222.9 7.0 %ffn_forward.2 = (f32[512,512]{1,0:T(8,128)}, f32[512,512]{1,0:T(8,128)}, f32[512,512]{1,0:T(8,128)}, f32[8,512]{1,0:T(8,128)}) custom-call(s32[8]{0:T(128)} %fusion.47.labels, bf16[512,2048]{1,0:T(8,128)(2,1)} %constant_dynamic-update-slice_fusion.x.near_x, bf16[512,2048]{1,0:T(8,128)(2,1)} %copy-done.13, f32[3,512]{1,0:T(4,128)} %bitcast.231, ...), custom_call_target="tpu_custom_call" | custom-call | flops 2147483648 | bytes 10485760 | tf_op jit(solution)/shard_map/ffn_forward/pallas_call | solution.py:743
  230.7 7.0 %ffn_forward.3 = (f32[512,512]{1,0:T(8,128)}, f32[512,512]{1,0:T(8,128)}, f32[512,512]{1,0:T(8,128)}, f32[8,512]{1,0:T(8,128)}) custom-call(s32[8]{0:T(128)} %fusion.47.labels, bf16[512,2048]{1,0:T(8,128)(2,1)} %collective-permute-done.31.x.far_x, bf16[512,2048]{1,0:T(8,128)(2,1)} %collective-permute-done.32.g.far_g, f32[3,512]{1,0:T(4,128)} %bitcast.232, ...), custom_call_target="tpu_custom_call" | custom-call | flops 2147483648 | bytes 10485760 | tf_op jit(solution)/shard_map/ffn_forward/pallas_call | solution.py:743
  251.7 6.1 %ffn_backward.3 = (bf16[512,512]{1,0:T(8,128)(2,1)}, bf16[512,512]{1,0:T(8,128)(2,1)}, bf16[512,2048]{1,0:T(8,128)(2,1)}, f32[8,512]{1,0:T(8,128)}) custom-call(s32[8]{0:T(128)} %fusion.47.labels, f32[8,1024]{1,0:T(8,128)} %add_add_fusion.2.sums, f32[512,512]{1,0:T(8,128)} %get-tuple-element.113.active, f32[512,512]{1,0:T(8,128)} %get-tuple-element.114.slope, ...), custom_call_target="tpu_custom_call" | custom-call | flops 1073741824 | bytes 8388608 | tf_op jit(solution)/shard_map/ffn_backward/pallas_call | solution.py:760
  260.9 6.1 %ffn_backward.2 = (bf16[512,512]{1,0:T(8,128)(2,1)}, bf16[512,512]{1,0:T(8,128)(2,1)}, bf16[512,2048]{1,0:T(8,128)(2,1)}, f32[8,512]{1,0:T(8,128)}) custom-call(s32[8]{0:T(128)} %fusion.47.labels, f32[8,1024]{1,0:T(8,128)} %add_add_fusion.2.sums, f32[512,512]{1,0:T(8,128)} %get-tuple-element.109.active, f32[512,512]{1,0:T(8,128)} %get-tuple-element.110.slope, ...), custom_call_target="tpu_custom_call" | custom-call | flops 1073741824 | bytes 8388608 | tf_op jit(solution)/shard_map/ffn_backward/pallas_call | solution.py:760
  267.8 3.4 collective-permute-start.45
  278.6 7.7 %ffn_gradient.3 = (bf16[512,512]{1,0:T(8,128)(2,1)}, bf16[512,512]{1,0:T(8,128)(2,1)}, bf16[512,512]{1,0:T(8,128)(2,1)}, bf16[512,512]{1,0:T(8,128)(2,1)}) custom-call(s32[4]{0:T(128)} %get-tuple-element.319.labels, bf16[512,2048]{1,0:T(8,128)(2,1)} %constant_dynamic-update-slice_fusion.x.near_x, bf16[512,2048]{1,0:T(8,128)(2,1)} %collective-permute-done.31.x.far_x, ...), custom_call_target="tpu_custom_call" | custom-call | flops 2147483648 | bytes 9437184 | tf_op jit(solution)/shard_map/ffn_gradient/pallas_call | solution.py:797
  290.5 5.6 %collective-permute-done.47 = bf16[64,2048]{1,0:T(8,128)(2,1)S(1)} collective-permute-done((bf16[64,2048]{1,0:T(8,128)(2,1)S(1)}, bf16[64,2048]{1,0:T(8,128)(2,1)S(1)}, u32[]{:S(2)}, u32[]{:S(2)}) %collective-permute-start.47) | collective-permute-done | bytes 262176 | tf_op jit(solution)/shard_map/ppermute | solution.py:118
  304.5 7.9 %ffn_gradient.2 = (bf16[512,512]{1,0:T(8,128)(2,1)}, bf16[512,512]{1,0:T(8,128)(2,1)}, bf16[512,512]{1,0:T(8,128)(2,1)}, bf16[512,512]{1,0:T(8,128)(2,1)}) custom-call(s32[4]{0:T(128)} %get-tuple-element.318.labels, bf16[512,2048]{1,0:T(8,128)(2,1)} %constant_dynamic-update-slice_fusion.x.near_x, bf16[512,2048]{1,0:T(8,128)(2,1)} %collective-permute-done.31.x.far_x, ...), custom_call_target="tpu_custom_call" | custom-call | flops 2147483648 | bytes 9437184 | tf_op jit(solution)/shard_map/ffn_gradient/pallas_call | solution.py:797
  312.7 11.2 %collective-permute-done.44 = bf16[512,512]{1,0:T(8,128)(2,1)S(1)} collective-permute-done((bf16[512,512]{1,0:T(8,128)(2,1)}, bf16[512,512]{1,0:T(8,128)(2,1)S(1)}, u32[]{:S(2)}, u32[]{:S(2)}) %collective-permute-start.44) | collective-permute-done | bytes 524320 | tf_op jit(solution)/shard_map/ppermute | solution.py:506
  333.9 3.6 output_back.1
  341.6 3.6 collective-permute-done.56
  348.3 5.4 %attention_backward.1 = (bf16[256,512]{1,0:T(8,128)(2,1)S(1)}, bf16[256,512]{1,0:T(8,128)(2,1)S(1)}, bf16[256,512]{1,0:T(8,128)(2,1)S(1)}, f32[8,512]{1,0:T(8,128)S(1)}) custom-call(s32[2]{0:T(128)S(1)} %copy-done.10, f32[256,512]{1,0:T(8,128)S(1)} %copy-done.5, f32[256,512]{1,0:T(8,128)S(1)} %copy-done, f32[256,4]{1,0:T(8,128)S(1)} %copy.57.coefficients, ...), custom_call_target="tpu_custom_call" | custom-call | flops 335544320 | bytes 4194304 | tf_op jit(solution)/shard_map/attention_backward/pallas_call | solution.py:875
  355.8 3.3 projection_gradient_far.1
  361.2 4.2 ffn_product.3
  365.3 4.2 ffn_product.2
  369.6 8.9 %projection_gradient.1 = bf16[7,1024,512]{2,1,0:T(8,128)(2,1)} custom-call(s32[7]{0:T(128)} %fusion.50.labels, bf16[256,2048]{1,0:T(8,128)(2,1)} %fusion.3.x, bf16[256,2048]{1,0:T(8,128)(2,1)} %pad_maximum_fusion.3.grad, bf16[256,512]{1,0:T(8,128)(2,1)} %copy-done.2, bf16[256,512]{1,0:T(8,128)(2,1)} %copy-done.3, bf16[256,512]{1,0:T(8,128)(2,1)} %copy-done.4, ...), custom_call_target="tpu_custom_call" | custom-call | flops 1879048192 | bytes 7340032 | tf_op jit(solution)/shard_map/projection_gradient/pallas_call | solution.py:909
  379.8 5.6 %collective-permute-done.59 = bf16[512,512]{1,0:T(8,128)(2,1)S(1)} collective-permute-done((bf16[512,512]{1,0:T(8,128)(2,1)}, bf16[512,512]{1,0:T(8,128)(2,1)S(1)}, u32[]{:S(2)}, u32[]{:S(2)}) %collective-permute-start.59) | collective-permute-done | bytes 524320 | tf_op jit(solution)/shard_map/ppermute | solution.py:63
  391.0 8.2 %projection_back.1 = (bf16[128,2048]{1,0:T(8,128)(2,1)}, f32[128,2048]{1,0:T(8,128)}) custom-call(s32[8]{0:T(128)} %get-tuple-element.311.labels, s32[1]{0:T(128)} %bitcast.1.rank, bf16[256,512]{1,0:T(8,128)(2,1)} %copy-done.2, bf16[256,512]{1,0:T(8,128)(2,1)} %copy-done.3, bf16[256,512]{1,0:T(8,128)(2,1)} %copy-done.4, bf16[1024,512]{1,0:T(8,128)(2,1)} %copy-done.11, ...), custom_call_target="tpu_custom_call" | custom-call | flops 1610612736 | bytes 10485760 | tf_op jit(solution)/shard_map/projection_back/pallas_call | solution.py:972
  399.3 4.5 convert_add_fusion
  403.7 11.4 %collective-permute-done.64 = bf16[1024,512]{1,0:T(8,128)(2,1)} collective-permute-done((bf16[1024,512]{1,0:T(8,128)(2,1)}, bf16[1024,512]{1,0:T(8,128)(2,1)}, u32[]{:S(2)}, u32[]{:S(2)}) %collective-permute-start.64) | collective-permute-done | bytes 1048608 | tf_op jit(solution)/shard_map/ppermute | solution.py:63
  415.1 4.2 fusion.7
  428.5 3.9 ffn_placed.1
  433.6 5.6 %all-to-all-start.1 = ((f32[8,1,1856]{2,1,0:T(1,128)}), f32[8,1,1856]{2,1,0:T(1,128)S(1)}, u32[]{:S(2)}, u32[]{:S(2)}) async-start(f32[8,1,1856]{2,1,0:T(1,128)} %all_to_all.14), calls=%async_computation.1 | async-start | bytes 122880 | tf_op jit(solution)/shard_map/all_to_all | solution.py:1016
  439.6 16.6 %all-to-all-done.1 = f32[8,1,1856]{2,1,0:T(1,128)S(1)} async-done(((f32[8,1,1856]{2,1,0:T(1,128)}), f32[8,1,1856]{2,1,0:T(1,128)S(1)}, u32[]{:S(2)}, u32[]{:S(2)}) %all-to-all-start.1) | async-done | bytes 59424 | tf_op jit(solution)/shard_map/all_to_all | solution.py:1016
  458.5 4.1 fusion.5
  465.9 9.4 %collective-permute-done.71 = bf16[64,2048]{1,0:T(8,128)(2,1)S(1)} collective-permute-done((bf16[64,2048]{1,0:T(8,128)(2,1)S(1)}, bf16[64,2048]{1,0:T(8,128)(2,1)S(1)}, u32[]{:S(2)}, u32[]{:S(2)}) %collective-permute-start.71) | collective-permute-done | bytes 262176 | tf_op jit(solution)/shard_map/ppermute | solution.py:492
  478.3 8.4 %collective-permute-done.73 = bf16[64,2048]{1,0:T(8,128)(2,1)S(1)} collective-permute-done((bf16[64,2048]{1,0:T(8,128)(2,1)S(1)}, bf16[64,2048]{1,0:T(8,128)(2,1)S(1)}, u32[]{:S(2)}, u32[]{:S(2)}) %collective-permute-start.73) | collective-permute-done | bytes 262176 | tf_op jit(solution)/shard_map/ppermute | solution.py:492
  497.0 10.5 %collective-permute-done.77 = f32[64,2048]{1,0:T(8,128)S(1)} collective-permute-done((f32[64,2048]{1,0:T(8,128)S(1)}, f32[64,2048]{1,0:T(8,128)S(1)}, u32[]{:S(2)}, u32[]{:S(2)}) %collective-permute-start.77) | collective-permute-done | bytes 524320 | tf_op jit(solution)/shard_map/ppermute | solution.py:118
  510.3 6.0 %collective-permute-done.80 = bf16[1024,512]{1,0:T(8,128)(2,1)S(1)} collective-permute-done((bf16[1024,512]{1,0:T(8,128)(2,1)}, bf16[1024,512]{1,0:T(8,128)(2,1)S(1)}, u32[]{:S(2)}, u32[]{:S(2)}) %collective-permute-start.80) | collective-permute-done | bytes 1048608 | tf_op jit(solution)/shard_map/ppermute | solution.py:63
  (412 shorter events, 181.8 us)
Async XLA Ops:
  3.1 26.2 %collective-permute-start = (bf16[1024,512]{1,0:T(8,128)(2,1)S(1)}, bf16[1024,512]{1,0:T(8,128)(2,1)S(1)}, u32[]{:S(2)}, u32[]{:S(2)}) collective-permute-start(bf16[1024,512]{1,0:T(8,128)(2,1)S(1)} %pad_maximum_fusion.1.refs_0_), channel_id=1, source_target_pairs={{8,0},{16,8},{24,16},{28,24},{20,28},{12,20},{4,12},{0,4},{9,1},{1... | collective-permute-start | bytes 3145736 | tf_op jit(solution)/shard_map/ppermute | solution.py:63
  6.1 24.9 %collective-permute-start.3 = (bf16[1024,512]{1,0:T(8,128)(2,1)S(1)}, bf16[1024,512]{1,0:T(8,128)(2,1)S(1)}, u32[]{:S(2)}, u32[]{:S(2)}) collective-permute-start(bf16[1024,512]{1,0:T(8,128)(2,1)S(1)} %pad_maximum_fusion.1.refs_0_), channel_id=1, source_target_pairs={{0,8},{8,16},{16,24},{24,28},{28,20},{20,12},{12,4},{4,0},{1,9},{9... | collective-permute-start | bytes 3145736 | tf_op jit(solution)/shard_map/ppermute | solution.py:63
  29.3 24.8 %collective-permute-start.1 = (bf16[1024,512]{1,0:T(8,128)(2,1)S(1)}, bf16[1024,512]{1,0:T(8,128)(2,1)}, u32[]{:S(2)}, u32[]{:S(2)}) collective-permute-start(bf16[1024,512]{1,0:T(8,128)(2,1)S(1)} %collective-permute-done.refs_1_), channel_id=1, source_target_pairs={{8,0},{16,8},{24,16},{28,24},{20,28},{12,20},{4,12},{0,4},{9,1},{1... | collective-permute-start | bytes 3145736 | tf_op jit(solution)/shard_map/ppermute | solution.py:63
  31.0 24.4 %collective-permute-start.4 = (bf16[1024,512]{1,0:T(8,128)(2,1)S(1)}, bf16[1024,512]{1,0:T(8,128)(2,1)}, u32[]{:S(2)}, u32[]{:S(2)}) collective-permute-start(bf16[1024,512]{1,0:T(8,128)(2,1)S(1)} %collective-permute-done.3.refs_8_.refs_7_), channel_id=1, source_target_pairs={{0,8},{8,16},{16,24},{24,28},{28,20},{20,12},{12,4},{4,0},{1,9},{9... | collective-permute-start | bytes 3145736 | tf_op jit(solution)/shard_map/ppermute | solution.py:63
  33.8 24.9 %all-to-all-start = ((bf16[8,2,1312]{2,1,0:T(2,128)(2,1)}), bf16[8,2,1312]{2,1,0:T(2,128)(2,1)S(1)}, u32[]{:S(2)}, u32[]{:S(2)}) async-start(bf16[8,2,1312]{2,1,0:T(2,128)(2,1)} %reshape.387), calls=%async_computation | async-start | bytes 90112 | tf_op jit(solution)/shard_map/all_to_all | solution.py:540
  54.1 23.5 %collective-permute-start.2 = (bf16[1024,512]{1,0:T(8,128)(2,1)}, bf16[1024,512]{1,0:T(8,128)(2,1)S(1)}, u32[]{:S(2)}, u32[]{:S(2)}) collective-permute-start(bf16[1024,512]{1,0:T(8,128)(2,1)} %collective-permute-done.1.refs_2_), channel_id=1, source_target_pairs={{8,0},{16,8},{24,16},{28,24},{20,28},{12,20},{4,12},{0,4},{9,1},{1... | collective-permute-start | bytes 3145736 | tf_op jit(solution)/shard_map/ppermute | solution.py:63
  55.4 24.1 %collective-permute-start.5 = (bf16[1024,512]{1,0:T(8,128)(2,1)}, bf16[1024,512]{1,0:T(8,128)(2,1)S(1)}, u32[]{:S(2)}, u32[]{:S(2)}) collective-permute-start(bf16[1024,512]{1,0:T(8,128)(2,1)} %collective-permute-done.4.refs_7_.refs_6_), channel_id=1, source_target_pairs={{0,8},{8,16},{16,24},{24,28},{28,20},{20,12},{12,4},{4,0},{1,9},{9... | collective-permute-start | bytes 3145736 | tf_op jit(solution)/shard_map/ppermute | solution.py:63
  78.6 24.9 %collective-permute-start.7 = (bf16[512,512]{1,0:T(8,128)(2,1)}, bf16[512,512]{1,0:T(8,128)(2,1)S(1)}, u32[]{:S(2)}, u32[]{:S(2)}) collective-permute-start(bf16[512,512]{1,0:T(8,128)(2,1)} %slice.374), channel_id=1, source_target_pairs={{8,0},{16,8},{24,16},{28,24},{20,28},{12,20},{4,12},{0,4},{9,1},{1... | collective-permute-start | bytes 1572872 | tf_op jit(solution)/shard_map/ppermute | solution.py:63
  80.4 23.1 %collective-permute-start.6 = (bf16[512,512]{1,0:T(8,128)(2,1)}, bf16[512,512]{1,0:T(8,128)(2,1)}, u32[]{:S(2)}, u32[]{:S(2)}) collective-permute-start(bf16[512,512]{1,0:T(8,128)(2,1)} %slice.373), channel_id=1, source_target_pairs={{0,8},{8,16},{16,24},{24,28},{28,20},{20,12},{12,4},{4,0},{1,9},{9... | collective-permute-start | bytes 1572872 | tf_op jit(solution)/shard_map/ppermute | solution.py:63
  85.3 31.1 %collective-permute-start.10 = (bf16[512,512]{1,0:T(8,128)(2,1)S(1)}, bf16[512,512]{1,0:T(8,128)(2,1)S(1)}, u32[]{:S(2)}, u32[]{:S(2)}) collective-permute-start(bf16[512,512]{1,0:T(8,128)(2,1)S(1)} %get-tuple-element.269.refs_0_), channel_id=1, source_target_pairs={{0,4},{4,0},{8,12},{12,8},{16,20},{20,16},{24,28},{28,24},{1,5},{5... | collective-permute-start | bytes 1572872 | tf_op jit(solution)/shard_map/ppermute | solution.py:506
  86.3 32.0 %collective-permute-start.8 = (bf16[512,512]{1,0:T(8,128)(2,1)}, bf16[512,512]{1,0:T(8,128)(2,1)}, u32[]{:S(2)}, u32[]{:S(2)}) collective-permute-start(bf16[512,512]{1,0:T(8,128)(2,1)} %get-tuple-element.271), channel_id=1, source_target_pairs={{0,8},{4,12},{8,16},{12,20},{16,24},{20,28},{24,0},{28,4},{1,9},{5... | collective-permute-start | bytes 1572872 | tf_op jit(solution)/shard_map/ppermute | solution.py:492
  87.7 30.5 %collective-permute-start.9 = (bf16[512,512]{1,0:T(8,128)(2,1)}, bf16[512,512]{1,0:T(8,128)(2,1)S(1)}, u32[]{:S(2)}, u32[]{:S(2)}) collective-permute-start(bf16[512,512]{1,0:T(8,128)(2,1)} %get-tuple-element.270), channel_id=1, source_target_pairs={{0,24},{4,28},{8,0},{12,4},{16,8},{20,12},{24,16},{28,20},{1,25},{... | collective-permute-start | bytes 1572872 | tf_op jit(solution)/shard_map/ppermute | solution.py:492
  118.2 25.1 %collective-permute-start.15 = (bf16[512,512]{1,0:T(8,128)(2,1)}, bf16[512,512]{1,0:T(8,128)(2,1)S(1)}, u32[]{:S(2)}, u32[]{:S(2)}) collective-permute-start(bf16[512,512]{1,0:T(8,128)(2,1)} %get-tuple-element.268), channel_id=1, source_target_pairs={{0,16},{4,20},{8,24},{12,28},{16,0},{20,4},{24,8},{28,12},{1,17},{... | collective-permute-start | bytes 1572872 | tf_op jit(solution)/shard_map/ppermute | solution.py:492
  131.0 16.1 %collective-permute-start.14 = (bf16[128,2048]{1,0:T(8,128)(2,1)}, bf16[128,2048]{1,0:T(8,128)(2,1)S(1)}, u32[]{:S(2)}, u32[]{:S(2)}) collective-permute-start(bf16[128,2048]{1,0:T(8,128)(2,1)} %get-tuple-element.100), channel_id=1, source_target_pairs={{0,1},{1,0},{2,3},{3,2},{4,5},{5,4},{6,7},{7,6},{8,9},{9,8},{10,11... | collective-permute-start | bytes 1572872 | tf_op jit(solution)/shard_map/ppermute | solution.py:118
  143.3 21.4 %collective-permute-start.18 = (bf16[64,2048]{1,0:T(8,128)(2,1)S(1)}, bf16[64,2048]{1,0:T(8,128)(2,1)}, u32[]{:S(2)}, u32[]{:S(2)}) collective-permute-start(bf16[64,2048]{1,0:T(8,128)(2,1)S(1)} %fusion.36), channel_id=1, source_target_pairs={{0,16},{4,20},{8,24},{12,28},{16,0},{20,4},{24,8},{28,12},{1,17},{... | collective-permute-start | bytes 786440 | tf_op jit(solution)/shard_map/ppermute | solution.py:492
  144.2 20.6 %collective-permute-start.19 = (bf16[64,2048]{1,0:T(8,128)(2,1)S(1)}, bf16[64,2048]{1,0:T(8,128)(2,1)}, u32[]{:S(2)}, u32[]{:S(2)}) collective-permute-start(bf16[64,2048]{1,0:T(8,128)(2,1)S(1)} %fusion.36), channel_id=1, source_target_pairs={{0,24},{4,28},{8,0},{12,4},{16,8},{20,12},{24,16},{28,20},{1,25},{... | collective-permute-start | bytes 786440 | tf_op jit(solution)/shard_map/ppermute | solution.py:492
  148.6 17.4 %collective-permute-start.16 = (bf16[64,2048]{1,0:T(8,128)(2,1)S(1)}, bf16[64,2048]{1,0:T(8,128)(2,1)S(1)}, u32[]{:S(2)}, u32[]{:S(2)}) collective-permute-start(bf16[64,2048]{1,0:T(8,128)(2,1)S(1)} %fusion.37), channel_id=1, source_target_pairs={{0,2},{1,3},{2,0},{3,1},{4,6},{5,7},{6,4},{7,5},{8,10},{9,11},{10,... | collective-permute-start | bytes 786440 | tf_op jit(solution)/shard_map/ppermute | solution.py:118
  150.2 69.8 %collective-permute-start.27 = (bf16[512,512]{1,0:T(8,128)(2,1)}, bf16[512,512]{1,0:T(8,128)(2,1)S(1)}, u32[]{:S(2)}, u32[]{:S(2)}) collective-permute-start(bf16[512,512]{1,0:T(8,128)(2,1)} %collective-permute-done.8.refs_1_), channel_id=1, source_target_pairs={{0,4},{4,0},{8,12},{12,8},{16,20},{20,16},{24,28},{28,24},{1,5},{5... | collective-permute-start | bytes 1572872 | tf_op jit(solution)/shard_map/ppermute | solution.py:506
  174.4 30.1 %collective-permute-start.30 = (bf16[256,2048]{1,0:T(8,128)(2,1)S(1)}, bf16[256,2048]{1,0:T(8,128)(2,1)S(1)}, u32[]{:S(2)}, u32[]{:S(2)}) collective-permute-start(bf16[256,2048]{1,0:T(8,128)(2,1)S(1)} %pad_maximum_fusion.2), channel_id=1, source_target_pairs={{0,2},{1,3},{2,0},{3,1},{4,6},{5,7},{6,4},{7,5},{8,10},{9,11},{10,... | collective-permute-start | bytes 3145736 | tf_op jit(solution)/shard_map/ppermute | solution.py:118
  179.6 40.4 %collective-permute-start.28 = (bf16[512,512]{1,0:T(8,128)(2,1)S(1)}, bf16[512,512]{1,0:T(8,128)(2,1)S(1)}, u32[]{:S(2)}, u32[]{:S(2)}) collective-permute-start(bf16[512,512]{1,0:T(8,128)(2,1)S(1)} %copy-done.19), channel_id=1, source_target_pairs={{0,4},{4,0},{8,12},{12,8},{16,20},{20,16},{24,28},{28,24},{1,5},{5... | collective-permute-start | bytes 1572872 | tf_op jit(solution)/shard_map/ppermute | solution.py:506
  188.9 31.1 %collective-permute-start.29 = (bf16[512,512]{1,0:T(8,128)(2,1)S(1)}, bf16[512,512]{1,0:T(8,128)(2,1)S(1)}, u32[]{:S(2)}, u32[]{:S(2)}) collective-permute-start(bf16[512,512]{1,0:T(8,128)(2,1)S(1)} %copy-done.21), channel_id=1, source_target_pairs={{0,4},{4,0},{8,12},{12,8},{16,20},{20,16},{24,28},{28,24},{1,5},{5... | collective-permute-start | bytes 1572872 | tf_op jit(solution)/shard_map/ppermute | solution.py:506
  194.0 16.1 %collective-permute-start.24 = (bf16[64,2048]{1,0:T(8,128)(2,1)S(1)}, bf16[64,2048]{1,0:T(8,128)(2,1)S(1)}, u32[]{:S(2)}, u32[]{:S(2)}) collective-permute-start(bf16[64,2048]{1,0:T(8,128)(2,1)S(1)} %collective-permute-done.20), channel_id=1, source_target_pairs={{0,2},{1,3},{2,0},{3,1},{4,6},{5,7},{6,4},{7,5},{8,10},{9,11},{10,... | collective-permute-start | bytes 786440 | tf_op jit(solution)/shard_map/ppermute | solution.py:118
  215.8 14.9 %collective-permute-start.32 = (bf16[512,2048]{1,0:T(8,128)(2,1)S(1)}, bf16[512,2048]{1,0:T(8,128)(2,1)}, u32[]{:S(2)}, u32[]{:S(2)}) collective-permute-start(bf16[512,2048]{1,0:T(8,128)(2,1)S(1)} %constant_dynamic-update-slice_fusion.8.g.near_g), channel_id=1, source_target_pairs={{0,1},{1,0},{2,3},{3,2},{4,5},{5,4},{6,7},{7,6},{8,9},{9,8},{10,11... | collective-permute-start | bytes 6291464 | tf_op jit(solution)/shard_map/ppermute | solution.py:118
  267.8 18.6 %collective-permute-start.45 = (f32[3,256]{1,0:T(4,128)S(1)}, f32[3,256]{1,0:T(4,128)S(1)}, u32[]{:S(2)}, u32[]{:S(2)}) collective-permute-start(f32[3,256]{1,0:T(4,128)S(1)} %bitcast.268), channel_id=1, source_target_pairs={{0,4},{4,0},{8,12},{12,8},{16,20},{20,16},{24,28},{28,24},{1,5},{5... | collective-permute-start | bytes 9224 | tf_op jit(solution)/shard_map/ppermute | solution.py:506
  277.7 18.4 %collective-permute-start.47 = (bf16[64,2048]{1,0:T(8,128)(2,1)S(1)}, bf16[64,2048]{1,0:T(8,128)(2,1)S(1)}, u32[]{:S(2)}, u32[]{:S(2)}) collective-permute-start(bf16[64,2048]{1,0:T(8,128)(2,1)S(1)} %get-tuple-element.265), channel_id=1, source_target_pairs={{0,2},{1,3},{2,0},{3,1},{4,6},{5,7},{6,4},{7,5},{8,10},{9,11},{10,... | collective-permute-start | bytes 786440 | tf_op jit(solution)/shard_map/ppermute | solution.py:118
  286.4 15.5 %collective-permute-start.42 = (bf16[512,512]{1,0:T(8,128)(2,1)}, bf16[512,512]{1,0:T(8,128)(2,1)S(1)}, u32[]{:S(2)}, u32[]{:S(2)}) collective-permute-start(bf16[512,512]{1,0:T(8,128)(2,1)} %get-tuple-element.126), channel_id=1, source_target_pairs={{0,4},{4,0},{8,12},{12,8},{16,20},{20,16},{24,28},{28,24},{1,5},{5... | collective-permute-start | bytes 1572872 | tf_op jit(solution)/shard_map/ppermute | solution.py:506
  286.4 14.6 %collective-permute-start.40 = (bf16[64,2048]{1,0:T(8,128)(2,1)S(1)}, bf16[64,2048]{1,0:T(8,128)(2,1)S(1)}, u32[]{:S(2)}, u32[]{:S(2)}) collective-permute-start(bf16[64,2048]{1,0:T(8,128)(2,1)S(1)} %get-tuple-element.264), channel_id=1, source_target_pairs={{0,2},{1,3},{2,0},{3,1},{4,6},{5,7},{6,4},{7,5},{8,10},{9,11},{10,... | collective-permute-start | bytes 786440 | tf_op jit(solution)/shard_map/ppermute | solution.py:118
  287.6 25.1 %collective-permute-start.43 = (bf16[512,512]{1,0:T(8,128)(2,1)}, bf16[512,512]{1,0:T(8,128)(2,1)S(1)}, u32[]{:S(2)}, u32[]{:S(2)}) collective-permute-start(bf16[512,512]{1,0:T(8,128)(2,1)} %get-tuple-element.127), channel_id=1, source_target_pairs={{0,4},{4,0},{8,12},{12,8},{16,20},{20,16},{24,28},{28,24},{1,5},{5... | collective-permute-start | bytes 1572872 | tf_op jit(solution)/shard_map/ppermute | solution.py:506
  290.5 33.4 %collective-permute-start.44 = (bf16[512,512]{1,0:T(8,128)(2,1)}, bf16[512,512]{1,0:T(8,128)(2,1)S(1)}, u32[]{:S(2)}, u32[]{:S(2)}) collective-permute-start(bf16[512,512]{1,0:T(8,128)(2,1)} %get-tuple-element.128), channel_id=1, source_target_pairs={{0,4},{4,0},{8,12},{12,8},{16,20},{20,16},{24,28},{28,24},{1,5},{5... | collective-permute-start | bytes 1572872 | tf_op jit(solution)/shard_map/ppermute | solution.py:506
  297.6 26.3 %collective-permute-start.48 = (bf16[64,2048]{1,0:T(8,128)(2,1)S(1)}, bf16[64,2048]{1,0:T(8,128)(2,1)S(1)}, u32[]{:S(2)}, u32[]{:S(2)}) collective-permute-start(bf16[64,2048]{1,0:T(8,128)(2,1)S(1)} %get-tuple-element.133), channel_id=1, source_target_pairs={{0,24},{4,28},{8,0},{12,4},{16,8},{20,12},{24,16},{28,20},{1,25},{... | collective-permute-start | bytes 786440 | tf_op jit(solution)/shard_map/ppermute | solution.py:492
  301.0 23.0 %collective-permute-start.49 = (bf16[64,2048]{1,0:T(8,128)(2,1)S(1)}, bf16[64,2048]{1,0:T(8,128)(2,1)S(1)}, u32[]{:S(2)}, u32[]{:S(2)}) collective-permute-start(bf16[64,2048]{1,0:T(8,128)(2,1)S(1)} %get-tuple-element.134), channel_id=1, source_target_pairs={{0,8},{4,12},{8,16},{12,20},{16,24},{20,28},{24,0},{28,4},{1,9},{5... | collective-permute-start | bytes 786440 | tf_op jit(solution)/shard_map/ppermute | solution.py:492
  301.9 22.0 %collective-permute-start.50 = (bf16[64,2048]{1,0:T(8,128)(2,1)S(1)}, bf16[64,2048]{1,0:T(8,128)(2,1)S(1)}, u32[]{:S(2)}, u32[]{:S(2)}) collective-permute-start(bf16[64,2048]{1,0:T(8,128)(2,1)S(1)} %get-tuple-element.259), channel_id=1, source_target_pairs={{0,16},{4,20},{8,24},{12,28},{16,0},{20,4},{24,8},{28,12},{1,17},{... | collective-permute-start | bytes 786440 | tf_op jit(solution)/shard_map/ppermute | solution.py:492
  312.7 21.2 %collective-permute-start.54 = (bf16[512,512]{1,0:T(8,128)(2,1)}, bf16[512,512]{1,0:T(8,128)(2,1)S(1)}, u32[]{:S(2)}, u32[]{:S(2)}) collective-permute-start(bf16[512,512]{1,0:T(8,128)(2,1)} %get-tuple-element.132), channel_id=1, source_target_pairs={{0,4},{4,0},{8,12},{12,8},{16,20},{20,16},{24,28},{28,24},{1,5},{5... | collective-permute-start | bytes 1572872 | tf_op jit(solution)/shard_map/ppermute | solution.py:506
  326.9 52.9 %collective-permute-start.62 = (bf16[512,512]{1,0:T(8,128)(2,1)}, bf16[512,512]{1,0:T(8,128)(2,1)}, u32[]{:S(2)}, u32[]{:S(2)}) collective-permute-start(bf16[512,512]{1,0:T(8,128)(2,1)} %add_convert_fusion.1), channel_id=1, source_target_pairs={{0,24},{4,28},{8,0},{12,4},{16,8},{20,12},{24,16},{28,20},{1,25},{... | collective-permute-start | bytes 1572872 | tf_op jit(solution)/shard_map/ppermute | solution.py:492
  329.7 50.1 %collective-permute-start.61 = (bf16[512,512]{1,0:T(8,128)(2,1)}, bf16[512,512]{1,0:T(8,128)(2,1)}, u32[]{:S(2)}, u32[]{:S(2)}) collective-permute-start(bf16[512,512]{1,0:T(8,128)(2,1)} %add_convert_fusion.2), channel_id=1, source_target_pairs={{0,8},{4,12},{8,16},{12,20},{16,24},{20,28},{24,0},{28,4},{1,9},{5... | collective-permute-start | bytes 1572872 | tf_op jit(solution)/shard_map/ppermute | solution.py:492
  341.6 38.2 %collective-permute-start.60 = (bf16[512,512]{1,0:T(8,128)(2,1)}, bf16[512,512]{1,0:T(8,128)(2,1)}, u32[]{:S(2)}, u32[]{:S(2)}) collective-permute-start(bf16[512,512]{1,0:T(8,128)(2,1)} %add_convert_fusion.3), channel_id=1, source_target_pairs={{0,16},{4,20},{8,24},{12,28},{16,0},{20,4},{24,8},{28,12},{1,17},{... | collective-permute-start | bytes 1572872 | tf_op jit(solution)/shard_map/ppermute | solution.py:492
  359.1 20.7 %collective-permute-start.58 = (bf16[512,512]{1,0:T(8,128)(2,1)}, bf16[512,512]{1,0:T(8,128)(2,1)S(1)}, u32[]{:S(2)}, u32[]{:S(2)}) collective-permute-start(bf16[512,512]{1,0:T(8,128)(2,1)} %get-tuple-element.145), channel_id=1, source_target_pairs={{0,8},{8,16},{16,24},{24,28},{28,20},{20,12},{12,4},{4,0},{1,9},{9... | collective-permute-start | bytes 1572872 | tf_op jit(solution)/shard_map/ppermute | solution.py:63
  359.7 25.8 %collective-permute-start.59 = (bf16[512,512]{1,0:T(8,128)(2,1)}, bf16[512,512]{1,0:T(8,128)(2,1)S(1)}, u32[]{:S(2)}, u32[]{:S(2)}) collective-permute-start(bf16[512,512]{1,0:T(8,128)(2,1)} %get-tuple-element.146), channel_id=1, source_target_pairs={{8,0},{16,8},{24,16},{28,24},{20,28},{12,20},{4,12},{0,4},{9,1},{1... | collective-permute-start | bytes 1572872 | tf_op jit(solution)/shard_map/ppermute | solution.py:63
  389.0 26.1 %collective-permute-start.64 = (bf16[1024,512]{1,0:T(8,128)(2,1)}, bf16[1024,512]{1,0:T(8,128)(2,1)}, u32[]{:S(2)}, u32[]{:S(2)}) collective-permute-start(bf16[1024,512]{1,0:T(8,128)(2,1)} %pad_maximum_fusion.5), channel_id=1, source_target_pairs={{8,0},{16,8},{24,16},{28,24},{20,28},{12,20},{4,12},{0,4},{9,1},{1... | collective-permute-start | bytes 3145736 | tf_op jit(solution)/shard_map/ppermute | solution.py:63
  389.0 26.1 %collective-permute-start.63 = (bf16[1024,512]{1,0:T(8,128)(2,1)}, bf16[1024,512]{1,0:T(8,128)(2,1)}, u32[]{:S(2)}, u32[]{:S(2)}) collective-permute-start(bf16[1024,512]{1,0:T(8,128)(2,1)} %pad_maximum_fusion.4), channel_id=1, source_target_pairs={{0,8},{8,16},{16,24},{24,28},{28,20},{20,12},{12,4},{4,0},{1,9},{9... | collective-permute-start | bytes 3145736 | tf_op jit(solution)/shard_map/ppermute | solution.py:63
  420.7 37.8 %collective-permute-start.69 = (bf16[1024,512]{1,0:T(8,128)(2,1)}, bf16[1024,512]{1,0:T(8,128)(2,1)}, u32[]{:S(2)}, u32[]{:S(2)}) collective-permute-start(bf16[1024,512]{1,0:T(8,128)(2,1)} %get-tuple-element.252), channel_id=1, source_target_pairs={{0,8},{8,16},{16,24},{24,28},{28,20},{20,12},{12,4},{4,0},{1,9},{9... | collective-permute-start | bytes 3145736 | tf_op jit(solution)/shard_map/ppermute | solution.py:63
  426.7 29.6 %collective-permute-start.68 = (bf16[4,64,2048]{2,1,0:T(8,128)(2,1)}, bf16[4,64,2048]{2,1,0:T(8,128)(2,1)}, u32[]{:S(2)}, u32[]{:S(2)}) collective-permute-start(bf16[4,64,2048]{2,1,0:T(8,128)(2,1)} %fusion.10), channel_id=1, source_target_pairs={{0,2},{1,3},{2,0},{3,1},{4,6},{5,7},{6,4},{7,5},{8,10},{9,11},{10,... | collective-permute-start | bytes 3145736 | tf_op jit(solution)/shard_map/ppermute | solution.py:118
  428.1 30.4 %collective-permute-start.70 = (bf16[1024,512]{1,0:T(8,128)(2,1)}, bf16[1024,512]{1,0:T(8,128)(2,1)}, u32[]{:S(2)}, u32[]{:S(2)}) collective-permute-start(bf16[1024,512]{1,0:T(8,128)(2,1)} %get-tuple-element.251), channel_id=1, source_target_pairs={{8,0},{16,8},{24,16},{28,24},{20,28},{12,20},{4,12},{0,4},{9,1},{1... | collective-permute-start | bytes 3145736 | tf_op jit(solution)/shard_map/ppermute | solution.py:63
  433.6 22.6 %all-to-all-start.1 = ((f32[8,1,1856]{2,1,0:T(1,128)}), f32[8,1,1856]{2,1,0:T(1,128)S(1)}, u32[]{:S(2)}, u32[]{:S(2)}) async-start(f32[8,1,1856]{2,1,0:T(1,128)} %all_to_all.14), calls=%async_computation.1 | async-start | bytes 122880 | tf_op jit(solution)/shard_map/all_to_all | solution.py:1016
  464.0 14.3 %collective-permute-start.72 = (bf16[64,2048]{1,0:T(8,128)(2,1)S(1)}, bf16[64,2048]{1,0:T(8,128)(2,1)S(1)}, u32[]{:S(2)}, u32[]{:S(2)}) collective-permute-start(bf16[64,2048]{1,0:T(8,128)(2,1)S(1)} %get-tuple-element.279), channel_id=1, source_target_pairs={{0,8},{4,12},{8,16},{12,20},{16,24},{20,28},{24,0},{28,4},{1,9},{5... | collective-permute-start | bytes 786440 | tf_op jit(solution)/shard_map/ppermute | solution.py:492
  464.9 21.8 %collective-permute-start.73 = (bf16[64,2048]{1,0:T(8,128)(2,1)S(1)}, bf16[64,2048]{1,0:T(8,128)(2,1)S(1)}, u32[]{:S(2)}, u32[]{:S(2)}) collective-permute-start(bf16[64,2048]{1,0:T(8,128)(2,1)S(1)} %get-tuple-element.278), channel_id=1, source_target_pairs={{0,16},{4,20},{8,24},{12,28},{16,0},{20,4},{24,8},{28,12},{1,17},{... | collective-permute-start | bytes 786440 | tf_op jit(solution)/shard_map/ppermute | solution.py:492
  490.7 25.6 %collective-permute-start.80 = (bf16[1024,512]{1,0:T(8,128)(2,1)}, bf16[1024,512]{1,0:T(8,128)(2,1)S(1)}, u32[]{:S(2)}, u32[]{:S(2)}) collective-permute-start(bf16[1024,512]{1,0:T(8,128)(2,1)} %get-tuple-element.250), channel_id=1, source_target_pairs={{0,8},{8,16},{16,24},{24,28},{28,20},{20,12},{12,4},{4,0},{1,9},{9... | collective-permute-start | bytes 3145736 | tf_op jit(solution)/shard_map/ppermute | solution.py:63
  491.8 25.6 %collective-permute-start.81 = (bf16[1024,512]{1,0:T(8,128)(2,1)}, bf16[1024,512]{1,0:T(8,128)(2,1)S(1)}, u32[]{:S(2)}, u32[]{:S(2)}) collective-permute-start(bf16[1024,512]{1,0:T(8,128)(2,1)} %get-tuple-element.249), channel_id=1, source_target_pairs={{8,0},{16,8},{24,16},{28,24},{20,28},{12,20},{4,12},{0,4},{9,1},{1... | collective-permute-start | bytes 3145736 | tf_op jit(solution)/shard_map/ppermute | solution.py:63
  (89 other events, 951.6 us)
